TPU v7x, 32 devices: a whole 2x2x4 slice. The times are simulated.
32 devices in a mesh: dp: 4 (over y, x), seq: 8 (over z, core).
Axes of the slice: x: 2, y: 2, z: 4, core: 2. Of those that a mesh axis runs over, the one named last changes fastest.
Arguments:
- residual_in: bfloat16 [4, 1024, 2048], P('dp', 'seq'), may hold values from -6 to 6
- attn_gain: bfloat16 [2048], P(('dp', 'seq')), may hold values from 0.099609375 to 1.8984375
- attn_shift: bfloat16 [2048], P(('dp', 'seq')), may hold values from -3 to 3
- qkv_weight: bfloat16 [2048, 6144], P(('dp', 'seq')), may hold values from -0.125 to 0.125
- qkv_bias: bfloat16 [6144], P(('dp', 'seq')), may hold values from -3 to 3
- out_weight: bfloat16 [2048, 2048], P(('dp', 'seq')), may hold values from -1 to 1
- ffn_gain: bfloat16 [2048], P(('dp', 'seq')), may hold values from 0.099609375 to 1.8984375
- ffn_shift: bfloat16 [2048], P(('dp', 'seq')), may hold values from -3 to 3
- gate_weight: bfloat16 [2048, 5632], P(('dp', 'seq')), may hold values from -0.125 to 0.125
- up_weight: bfloat16 [2048, 5632], P(('dp', 'seq')), may hold values from -0.125 to 0.125
- down_weight: bfloat16 [2048, 5632], P(('dp', 'seq')), may hold values from -0.078125 to 0.078125
- positions: int32 [4, 1024], P('dp', 'seq'), may hold values from 0 to 511, as said below
- cotangent: bfloat16 [4, 1024, 2048], P('dp', 'seq'), may hold values from -6 to 6
Outputs:
- residual_out: bfloat16 [4, 1024, 2048], P('dp', 'seq')
- grad_residual_in: float32 [4, 1024, 2048], P('dp', 'seq')
- grad_attn_gain: float32 [2048], P(('dp', 'seq'))
- grad_attn_shift: float32 [2048], P(('dp', 'seq'))
- grad_qkv_weight: float32 [2048, 6144], P(('dp', 'seq'))
- grad_qkv_bias: float32 [6144], P(('dp', 'seq'))
- grad_out_weight: float32 [2048, 2048], P(('dp', 'seq'))
- grad_ffn_gain: float32 [2048], P(('dp', 'seq'))
- grad_ffn_shift: float32 [2048], P(('dp', 'seq'))
- grad_gate_weight: float32 [2048, 5632], P(('dp', 'seq'))
- grad_up_weight: float32 [2048, 5632], P(('dp', 'seq'))
- grad_down_weight: float32 [2048, 5632], P(('dp', 'seq'))
Inputs may be any that keep to these rules, and one draw needn't show every extreme that they name: `positions`: positions count from the start of each token's document and restart at 0 where a document begins; the first token of a sequence has position 0; a sequence holds at most four documents, one of exactly 512 tokens.
All inputs are finite; a program needn't handle non-finite values.
Results may differ from a plain program's by a relative error of at most 0.015.
Values may be sent and summed in bfloat16 or wider, within the bound.
No kernel may reach another device: no remote copies, remote signals or barrier semaphores. Data moves between devices by JAX's collectives and lax.ppermute only.
A program may use at most 192 MiB of HBM per device.

v0:
```python
import functools

import jax
import jax.numpy as jnp
from jax import lax
from jax.experimental import pallas as pl
from jax.experimental.pallas import tpu as pltpu
from jax.sharding import PartitionSpec as P


HEADS = 32
HD = 64
ROT = 16
LANES = 128
EPSILON = 1e-05
ROPE_BASE = 10000.0
MASKED = -1e30
BF = jnp.bfloat16
F32 = jnp.float32


def rotary_rows(position):
    lane = jnp.arange(LANES, dtype=jnp.int32) % HD
    half = ROT // 2
    power = ROPE_BASE ** (-(lane % half).astype(F32) * (2.0 / ROT))
    freq = jnp.where(lane < ROT, power, 0.0)
    angle = position.astype(F32)[:, None] * freq[None, :]
    cosine = jnp.cos(angle); sine = jnp.sin(angle)
    first = jnp.where(lane < half, -sine, 0.0)
    second = jnp.where((lane >= half) & (lane < ROT), sine, 0.0)
    return cosine, first, second


def turn(x, cosine, first, second):
    return x * cosine + pltpu.roll(x, LANES - ROT // 2, 1) * first + pltpu.roll(x, ROT // 2, 1) * second


def head_mask(x, h):
    lane = lax.broadcasted_iota(jnp.int32, x.shape, 1)
    return jnp.where((lane >= h * HD) & (lane < (h + 1) * HD), x, jnp.zeros_like(x))


def nt(a, b):
    return lax.dot_general(a, b, (((1,), (1,)), ((), ())), preferred_element_type=F32)


def nn(a, b):
    return lax.dot_general(a, b, (((1,), (0,)), ((), ())), preferred_element_type=F32)


def block_bias(i, j, bq, low_row):
    key = j * bq + lax.broadcasted_iota(jnp.int32, (bq, bq), 0)
    query = i * bq + lax.broadcasted_iota(jnp.int32, (bq, bq), 1)
    return jnp.where((key <= query) & (key >= low_row), 0.0, MASKED)


def fwd_kernel(heads, bq, first_ref, low_ref, cos_ref, s1_ref, s2_ref, proj_ref,
               qkv_ref, ctx_ref, lse_ref, k_s, vt_s, st_s):
    i = pl.program_id(0)
    hc = heads * HD
    c, s1, s2 = cos_ref[...], s1_ref[...], s2_ref[...]
    parts = []
    for base in (0, hc):
        for t in range(hc // LANES):
            x = proj_ref[:, base + t * LANES: base + (t + 1) * LANES]
            parts.append(turn(x, c, s1, s2).astype(BF))
    n = hc // LANES
    q = jnp.concatenate(parts[:n], axis=1) if n > 1 else parts[0]
    k = jnp.concatenate(parts[n:], axis=1) if n > 1 else parts[n]
    v32 = proj_ref[:, 2 * hc:]
    v = v32.astype(BF)
    qkv_ref[:, :hc] = q
    qkv_ref[:, hc:2 * hc] = k
    qkv_ref[:, 2 * hc:] = v
    rows = pl.ds(pl.multiple_of(i * bq, bq), bq)
    k_s[rows, :] = k
    vt_s[:, rows] = v32.T.astype(BF)
    low = low_ref[0:1, :]
    qm = [head_mask(q, h) for h in range(heads)]
    first = first_ref[i]

    def score_step(j, tops):
        kj = k_s[pl.ds(pl.multiple_of(j * bq, bq), bq), :]
        bias = block_bias(i, j, bq, low)
        out = []
        for h in range(heads):
            s = nt(kj, qm[h]) * 0.125 + bias
            st_s[h, pl.ds(pl.multiple_of(j * bq, bq), bq), :] = s
            out.append(jnp.maximum(tops[h], jnp.max(s.reshape(bq // 8, 8, bq), axis=0)))
        return tuple(out)

    tops = lax.fori_loop(first, i + 1, score_step,
                         tuple(jnp.full((8, bq), MASKED, F32) for _ in range(heads)))
    tops = [jnp.max(t, axis=0, keepdims=True) for t in tops]

    def value_step(j, state):
        new = []
        vt = vt_s[:, pl.ds(pl.multiple_of(j * bq, bq), bq)]
        for h in range(heads):
            tot, acc = state[h]
            p = jnp.exp(st_s[h, pl.ds(pl.multiple_of(j * bq, bq), bq), :] - tops[h])
            tot = tot + jnp.sum(p.reshape(bq // 8, 8, bq), axis=0)
            acc = acc + nn(vt[h * HD:(h + 1) * HD, :], p.astype(BF))
            new.append((tot, acc))
        return tuple(new)

    state = lax.fori_loop(first, i + 1, value_step,
                          tuple((jnp.zeros((8, bq), F32), jnp.zeros((HD, bq), F32)) for _ in range(heads)))
    outs = []
    lses = []
    for h in range(heads):
        tot, acc = state[h]
        tot = jnp.sum(tot, axis=0, keepdims=True)
        outs.append(acc / tot)
        lses.append(tops[h] + jnp.log(tot))
    ctx_ref[...] = jnp.concatenate(outs, axis=0).T.astype(BF)
    pad = [jnp.zeros((8 - heads, bq), F32)] if heads < 8 else []
    lse_ref[...] = jnp.concatenate(lses + pad, axis=0)


def attend_fwd(proj, tables, low8, first, heads, bq):
    T = proj.shape[0]; hc = heads * HD
    row = lambda w: pl.BlockSpec((bq, w), lambda i, f: (i, 0))
    return pl.pallas_call(
        functools.partial(fwd_kernel, heads, bq),
        grid_spec=pltpu.PrefetchScalarGridSpec(
            num_scalar_prefetch=1, grid=(T // bq,),
            in_specs=[pl.BlockSpec((8, bq), lambda i, f: (0, i)), row(LANES), row(LANES), row(LANES), row(3 * hc)],
            out_specs=[row(3 * hc), row(hc), pl.BlockSpec((8, bq), lambda i, f: (0, i))],
            scratch_shapes=[pltpu.VMEM((T, hc), BF), pltpu.VMEM((hc, T), BF), pltpu.VMEM((heads, T, bq), F32)]),
        out_shape=[jax.ShapeDtypeStruct((T, 3 * hc), BF), jax.ShapeDtypeStruct((T, hc), BF), jax.ShapeDtypeStruct((8, T), F32)],
        compiler_params=pltpu.CompilerParams(dimension_semantics=("arbitrary",)),
        cost_estimate=pl.CostEstimate(flops=2 * T * T * hc * 2, bytes_accessed=T * hc * 24, transcendentals=T * T * heads // 2),
        name="attend_fwd",
    )(first, low8, *tables, proj)


def bwd_kernel(heads, bq, count, first_ref, low_ref, cos_ref, s1_ref, s2_ref, qkv_ref, ctx_ref, lse_ref, gc_ref,
               gp_ref, bias_ref, dk_s, dv_s, dq_s):
    step = pl.program_id(0)
    i = count - 1 - step
    hc = heads * HD
    rows = pl.ds(pl.multiple_of(i * bq, bq), bq)

    @pl.when(step == 0)
    def _():
        dk_s[...] = jnp.zeros_like(dk_s)
        dv_s[...] = jnp.zeros_like(dv_s)
        bias_ref[...] = jnp.zeros_like(bias_ref)

    low = low_ref[0:1, rows]
    q = qkv_ref[rows, :hc]
    g = gc_ref[rows, :]
    prod = (g.astype(F32) * ctx_ref[rows, :].astype(F32)).T
    deltas = [jnp.sum(prod[h * HD:(h + 1) * HD, :], axis=0, keepdims=True) for h in range(heads)]
    lses = [lse_ref[h:h + 1, rows] for h in range(heads)]
    qm = [head_mask(q, h) for h in range(heads)]
    gm = [head_mask(g, h) for h in range(heads)]
    dq_s[...] = jnp.zeros_like(dq_s)

    @pl.loop(first_ref[i], i + 1)
    def _(j):
        cols = pl.ds(pl.multiple_of(j * bq, bq), bq)
        kj = qkv_ref[cols, hc:2 * hc]
        vj = qkv_ref[cols, 2 * hc:]
        kt = kj.T
        bias = block_bias(i, j, bq, low)
        dk = dk_s[cols, :]
        dv = dv_s[cols, :]
        for h in range(heads):
            s = nt(kj, qm[h]) * 0.125 + bias
            p = jnp.exp(s - lses[h])
            dp = nt(vj, gm[h])
            ds = (p * (dp - deltas[h]) * 0.125).astype(BF)
            dv = dv + nn(p.astype(BF), gm[h])
            dk = dk + nn(ds, qm[h])
            dq_s[h * HD:(h + 1) * HD, :] += nn(kt[h * HD:(h + 1) * HD, :], ds)
        dk_s[cols, :] = dk
        dv_s[cols, :] = dv

    c, s1, s2 = cos_ref[rows, :], s1_ref[rows, :], s2_ref[rows, :]
    dq = dq_s[...].T
    dk = dk_s[rows, :]
    dv = dv_s[rows, :]

    def emit(x, base):
        gp_ref[:, base: base + x.shape[1]] = x.astype(BF)
        bias_ref[:, base: base + x.shape[1]] += jnp.sum(x.reshape(bq // 8, 8, x.shape[1]), axis=0)

    for src, base in ((dq, 0), (dk, hc)):
        for t in range(hc // LANES):
            emit(turn(src[:, t * LANES:(t + 1) * LANES], c, -s1, -s2), base + t * LANES)
    emit(dv, 2 * hc)


def attend_bwd(qkv, ctx, lse, gc, tables, low8, first, heads, bq):
    T = qkv.shape[0]; hc = heads * HD; count = T // bq
    full = lambda r, w: pl.BlockSpec((r, w), lambda i, f: (0, 0))
    return pl.pallas_call(
        functools.partial(bwd_kernel, heads, bq, count),
        grid_spec=pltpu.PrefetchScalarGridSpec(
            num_scalar_prefetch=1, grid=(count,),
            in_specs=[full(8, T), full(T, LANES), full(T, LANES), full(T, LANES), full(T, 3 * hc), full(T, hc), full(8, T), full(T, hc)],
            out_specs=[pl.BlockSpec((bq, 3 * hc), lambda i, f: (count - 1 - i, 0)), full(8, 3 * hc)],
            scratch_shapes=[pltpu.VMEM((T, hc), F32), pltpu.VMEM((T, hc), F32), pltpu.VMEM((hc, bq), F32)]),
        out_shape=[jax.ShapeDtypeStruct((T, 3 * hc), BF), jax.ShapeDtypeStruct((8, 3 * hc), F32)],
        compiler_params=pltpu.CompilerParams(dimension_semantics=("arbitrary",)),
        cost_estimate=pl.CostEstimate(flops=5 * T * T * hc * 2, bytes_accessed=T * hc * 24, transcendentals=T * T * heads // 2),
        name="attend_bwd",
    )(first, low8, *tables, qkv, ctx, lse, gc)


def relate(values, mine, count, axis):
    size = values.shape[axis] // count
    bit = 1
    while bit < count:
        order = [m ^ bit for m in range(count)]
        swapped = jnp.concatenate(
            [lax.slice_in_dim(values, m * size, (m + 1) * size, axis=axis) for m in order], axis=axis
        )
        values = jnp.where((mine & bit) != 0, swapped, values)
        bit *= 2
    return values


def swap_dp(values, rel):
    return lax.ppermute(values, "dp", [(d, d ^ rel) for d in range(lax.axis_size("dp"))])


def fetch(view):
    mine = lax.all_to_all(view, "seq", split_axis=0, concat_axis=0, tiled=True)
    return [mine] + [swap_dp(mine, rel) for rel in range(1, lax.axis_size("dp"))]


def stack_rows(pieces, start, size):
    cols = pieces[0].shape[2]
    return jnp.concatenate([p[:, start : start + size] for p in pieces], axis=0).reshape(-1, cols)


def reduce_dp(parts):
    total = parts[0].astype(F32)
    moved = [swap_dp(parts[rel], rel) for rel in range(1, parts.shape[0])]
    for piece in moved:
        total = total + piece.astype(F32)
    return total.astype(BF)


def send_back(summed):
    return lax.all_to_all(summed, "seq", split_axis=0, concat_axis=0, tiled=True)


def unit_of(values):
    center = values - jnp.mean(values, axis=-1, keepdims=True)
    factor = lax.rsqrt(jnp.mean(center * center, axis=-1, keepdims=True) + EPSILON)
    return center * factor, factor


def norm_back(upstream, unit, factor, gain):
    scaled = upstream * gain
    return factor * (
        scaled
        - jnp.mean(scaled, axis=-1, keepdims=True)
        - unit * jnp.mean(scaled * unit, axis=-1, keepdims=True)
    )


def dot(left, right, dims):
    return lax.dot_general(left, right, (dims, ((), ())), preferred_element_type=F32)


NN = ((1,), (0,))
NT = ((1,), (1,))
TN = ((0,), (0,))


def own_rows(partial):
    return lax.psum_scatter(partial.astype(BF), "seq", scatter_dimension=0, tiled=True).astype(F32)


def every(values):
    return lax.all_gather(values, "seq", axis=0, tiled=True)


def chip_shift(values, k, groups):
    return lax.ppermute(values, "seq", [(s, (s + 2 * k) % groups) for s in range(groups)])


def core_swap(values, groups):
    return lax.ppermute(values, "seq", [(s, s ^ 1) for s in range(groups)])


def own_rows_beside(partial, me, groups):
    chips = groups // 2
    tokens = partial.shape[0] // groups
    blocks = partial.reshape(chips, 2, tokens, partial.shape[1])
    core = me % 2
    theirs = lax.dynamic_index_in_dim(blocks, 1 - core, 1, keepdims=False)
    ours = lax.dynamic_index_in_dim(blocks, core, 1, keepdims=False)
    moved = core_swap(theirs, groups)
    pair = (ours.astype(F32) + moved.astype(F32)).astype(BF)
    chip = me // 2
    total = lax.dynamic_index_in_dim(pair, chip, 0, keepdims=False).astype(F32)
    for k in range(1, chips):
        part = lax.dynamic_index_in_dim(pair, (chip + k) % chips, 0, keepdims=False)
        total = total + chip_shift(part, k, groups).astype(F32)
    return total


def layer(
    inputs,
    position,
    upstream,
    attn_gain,
    attn_shift,
    qkv_weight,
    qkv_bias,
    out_weight,
    ffn_gain,
    ffn_shift,
    gate_weight,
    up_weight,
    down_weight,
):
    tokens, width = inputs.shape
    groups = lax.axis_size("seq")
    copies = lax.axis_size("dp")
    me = lax.axis_index("seq")
    mine = lax.axis_index("dp")
    length = tokens * groups
    heads = HEADS // groups
    hc = heads * HD
    rows = qkv_weight.shape[0]
    nbias = qkv_bias.shape[0]
    bq = 256

    own = relate(inputs, mine, copies, 1)
    own_up = relate(upstream, mine, copies, 1)
    x_all = every(own)

    def by_group(weight, parts=1):
        cols = weight.shape[1] // (parts * groups)
        view = weight.reshape(rows, parts, groups, cols).transpose(2, 0, 1, 3)
        return view.reshape(groups, rows, parts * cols)

    small = jnp.concatenate(
        [
            attn_gain,
            attn_shift,
            ffn_gain,
            ffn_shift,
            qkv_bias,
            (position // 256).astype(BF),
            (position % 256).astype(BF),
        ]
    )
    extra = jnp.zeros((8, 3 * hc), BF).at[0, : small.shape[0]].set(small)
    view_qkv = jnp.concatenate(
        [by_group(qkv_weight, 3), jnp.broadcast_to(extra[None], (groups, 8, 3 * hc))], axis=1
    )
    pieces_qkv = fetch(view_qkv)
    weight_qkv = stack_rows(pieces_qkv, 0, rows)
    weight_out = stack_rows(fetch(by_group(out_weight)), 0, rows)
    spot = pieces_qkv[0][:, rows, 4 * rows + nbias : 4 * rows + nbias + 2 * tokens]
    positions = (
        spot[:, :tokens].astype(jnp.int32) * 256 + spot[:, tokens:].astype(jnp.int32)
    ).reshape(length)
    everyone = jnp.stack([p[:, rows, : 4 * rows + nbias] for p in pieces_qkv]).astype(F32)
    gain_one, shift_one, gain_two, shift_two = [
        everyone[:, :, n * rows : (n + 1) * rows].reshape(1, width) for n in range(4)
    ]
    bias_full = relate(everyone[:, :, 4 * rows :].reshape(-1), mine, copies, 0)
    chosen = (jnp.arange(groups, dtype=jnp.int32) == me).astype(F32)
    bias_mine = jnp.sum(bias_full.reshape(3, groups, hc) * chosen[None, :, None], axis=1).reshape(1, -1)

    tables = rotary_rows(positions)
    lowest = jnp.arange(length, dtype=jnp.int32) - positions
    low8 = jnp.broadcast_to(lowest[None], (8, length))
    first = (jnp.min(lowest.reshape(length // bq, bq), axis=1) // bq).astype(jnp.int32)

    view_gu = jnp.concatenate([by_group(gate_weight), by_group(up_weight)], axis=1)
    view_gu, view_down, own_up, x_all = lax.optimization_barrier(
        (view_gu, by_group(down_weight), own_up, x_all)
    )
    up_all = every(own_up)
    pieces_gu = fetch(view_gu)
    weight_gate = stack_rows(pieces_gu, 0, rows)
    weight_up = stack_rows(pieces_gu, rows, rows)
    weight_down = stack_rows(fetch(view_down), 0, rows)

    unit_all, _ = unit_of(x_all.astype(F32))
    normed_one = (unit_all * gain_one + shift_one).astype(BF)
    projected = dot(normed_one, weight_qkv, NN) + bias_mine
    qkv, context, lse = attend_fwd(projected, tables, low8, first, heads, bq)
    flat = own.astype(F32)
    middle = flat + own_rows(dot(context, weight_out, NT))
    unit_two, factor_two = unit_of(middle)
    normed_two = (unit_two * gain_two + shift_two).astype(BF)
    normed_two = every(normed_two)
    gate = dot(normed_two, weight_gate, NN)
    upward = dot(normed_two, weight_up, NN)
    sig = jax.nn.sigmoid(gate)
    silu = gate * sig
    hidden = (silu * upward).astype(BF)
    grad_hidden = dot(up_all, weight_down, NN)
    grad_gate = (grad_hidden * upward * sig * (1.0 + gate * (1.0 - sig))).astype(BF)
    grad_up = (grad_hidden * silu).astype(BF)
    grad_normed_two = own_rows(dot(grad_gate, weight_gate, NT) + dot(grad_up, weight_up, NT))
    down_part = dot(hidden, weight_down, NT).astype(BF)
    grad_gate_weight = dot(normed_two, grad_gate, TN).astype(BF)
    grad_up_weight = dot(normed_two, grad_up, TN).astype(BF)
    grad_down_weight = dot(up_all, hidden, TN).astype(BF)

    def by_owner(grad):
        return grad.reshape(copies, groups, rows, grad.shape[1])

    sum_ffn = jnp.concatenate(
        [
            reduce_dp(by_owner(grad_gate_weight)),
            reduce_dp(by_owner(grad_up_weight)),
            reduce_dp(by_owner(grad_down_weight)),
        ],
        axis=1,
    )
    sum_ffn = send_back(sum_ffn).transpose(1, 0, 2)

    grad_middle = own_up.astype(F32) + norm_back(grad_normed_two, unit_two, factor_two, gain_two)
    grad_mixed, down_part = lax.optimization_barrier((grad_middle.astype(BF), down_part))
    output = (middle + own_rows_beside(down_part, me, groups)).astype(BF)
    grad_mixed = every(grad_mixed)
    grad_context = dot(grad_mixed, weight_out, NN).astype(BF)
    grad_projected, bias_part = attend_bwd(qkv, context, lse, grad_context, tables, low8, first, heads, bq)
    dqkv = dot(grad_projected, weight_qkv, NT).astype(BF)
    grad_normed_one = own_rows(dqkv)

    bias_part = jnp.sum(bias_part, axis=0).reshape(3, 1, hc) * chosen[None, :, None]
    bias_part = relate(bias_part.reshape(-1), mine, copies, 0).reshape(copies, groups, nbias)
    parts = [
        jnp.sum(dqkv.astype(F32) * unit_all, axis=0),
        jnp.sum(dqkv.astype(F32), axis=0),
        jnp.sum(grad_normed_two * unit_two, axis=0),
        jnp.sum(grad_normed_two, axis=0),
    ]
    parts = [p.reshape(copies, groups, 1, rows) for p in parts] + [bias_part[:, :, None]]
    parts = jnp.concatenate(parts, axis=3)
    parts = jnp.pad(parts, ((0, 0), (0, 0), (0, 7), (0, 3 * hc - parts.shape[3]))).astype(BF)

    grad_out_weight = dot(grad_mixed, context, TN).astype(BF)
    sum_out = reduce_dp(by_owner(grad_out_weight))
    grad_qkv_weight = dot(normed_one, grad_projected, TN).astype(BF)
    sum_qkv = reduce_dp(jnp.concatenate([by_owner(grad_qkv_weight), parts], axis=2))
    sum_attn = jnp.concatenate([sum_qkv, jnp.pad(sum_out, ((0, 0), (0, 8), (0, 0)))], axis=2)
    sum_attn = send_back(sum_attn)
    total = jnp.sum(sum_attn[:, rows].astype(F32), axis=0)
    sums = [total[n * rows : (n + 1) * rows] for n in range(4)] + [total[4 * rows : 4 * rows + nbias]]
    sum_attn = sum_attn[:, :rows].transpose(1, 0, 2)
    sum_qkv = sum_attn[:, :, : 3 * hc]
    sum_out = sum_attn[:, :, 3 * hc :]
    unit_one, factor_one = unit_of(flat)
    grad_input = grad_middle + norm_back(grad_normed_one, unit_one, factor_one, gain_one)

    def wide(value):
        return value.astype(F32).reshape(rows, -1)

    wide_qkv = sum_qkv.reshape(rows, groups, 3, hc).transpose(0, 2, 1, 3)
    return (
        relate(output, mine, copies, 1)[None],
        relate(grad_input, mine, copies, 1)[None],
        sums[0],
        sums[1],
        wide(wide_qkv),
        sums[4],
        wide(sum_out),
        sums[2],
        sums[3],
        wide(sum_ffn[:rows]),
        wide(sum_ffn[rows : 2 * rows]),
        wide(sum_ffn[2 * rows :]),
    )


def local(
    residual_in,
    attn_gain,
    attn_shift,
    qkv_weight,
    qkv_bias,
    out_weight,
    ffn_gain,
    ffn_shift,
    gate_weight,
    up_weight,
    down_weight,
    positions,
    cotangent,
):
    return layer(
        residual_in[0],
        positions[0],
        cotangent[0],
        attn_gain,
        attn_shift,
        qkv_weight,
        qkv_bias,
        out_weight,
        ffn_gain,
        ffn_shift,
        gate_weight,
        up_weight,
        down_weight,
    )


def solution(mesh):
    both = ("dp", "seq")
    in_specs = (
        P("dp", "seq", None),
        P(both),
        P(both),
        P(both, None),
        P(both),
        P(both, None),
        P(both),
        P(both),
        P(both, None),
        P(both, None),
        P(both, None),
        P("dp", "seq"),
        P("dp", "seq", None),
    )
    out_specs = (
        P("dp", "seq", None),
        P("dp", "seq", None),
        P(both),
        P(both),
        P(both, None),
        P(both),
        P(both, None),
        P(both),
        P(both),
        P(both, None),
        P(both, None),
        P(both, None),
    )
    return jax.shard_map(local, mesh=mesh, in_specs=in_specs, out_specs=out_specs, check_vma=False)
```

profile of v0, /device:TPU:0, one launch (start us, length us, event | category | flops | bytes accessed | tf_op | source)
XLA Modules:
  0.0 789.6 jit_solution(3672976959725419837)
XLA Ops:
  20.7 11.2 %all-to-all-done.1 = bf16[8,64,256]{2,1,0:T(8,128)(2,1)} async-done(((bf16[8,64,256]{2,1,0:T(8,128)(2,1)}), bf16[8,64,256]{2,1,0:T(8,128)(2,1)}, u32[]{:S(2)}, u32[]{:S(2)}) %all-to-all-start.1) | async-done | bytes 262176 | tf_op jit(solution)/shard_map/all_to_all | solution.py:231
  54.0 25.1 %all-to-all-done = bf16[8,72,768]{2,1,0:T(8,128)(2,1)} async-done(((bf16[8,72,768]{2,1,0:T(8,128)(2,1)}), bf16[8,72,768]{2,1,0:T(8,128)(2,1)}, u32[]{:S(2)}, u32[]{:S(2)}) %all-to-all-start) | async-done | bytes 884768 | tf_op jit(solution)/shard_map/all_to_all | solution.py:231
  88.2 15.9 %collective-permute-done.2 = bf16[8,72,768]{2,0,1:T(8,128)(2,1)} collective-permute-done((bf16[8,72,768]{2,0,1:T(8,128)(2,1)S(1)}, bf16[8,72,768]{2,0,1:T(8,128)(2,1)}, u32[]{:S(2)}, u32[]{:S(2)}) %collective-permute-start.2) | collective-permute-done | bytes 884768 | tf_op jit(solution)/shard_map/ppermute | solution.py:227
  104.8 16.9 %collective-permute-done.1 = bf16[8,72,768]{2,0,1:T(8,128)(2,1)} collective-permute-done((bf16[8,72,768]{2,0,1:T(8,128)(2,1)S(1)}, bf16[8,72,768]{2,0,1:T(8,128)(2,1)}, u32[]{:S(2)}, u32[]{:S(2)}) %collective-permute-start.1) | collective-permute-done | bytes 884768 | tf_op jit(solution)/shard_map/ppermute | solution.py:227
  142.7 9.6 %attend_fwd.1 = (bf16[1024,768]{1,0:T(8,128)(2,1)}, bf16[1024,256]{1,0:T(8,128)(2,1)}, f32[8,1024]{1,0:T(8,128)}) custom-call(s32[4]{0:T(128)} %and_select_fusion.2.first_ref, s32[8,1024]{1,0:T(8,128)} %broadcast_in_dim.28.low_ref, f32[1024,128]{1,0:T(8,128)} %get-tuple-element.133.cos_ref, f32[1024,128]{1,0:T(8,128)} %get-tuple-element.132.s1_ref, ...), custom_call_target="tpu_custom_call" | custom-call | flops 1073741824 | bytes 6291456 | tf_op jit(solution)/shard_map/attend_fwd/pallas_call | solution.py:124
  157.0 49.2 %reduce-scatter.4.cloned.1.call-done = bf16[128,2048]{1,0:T(8,128)(2,1)} async-done(((bf16[1024,2048]{1,0:T(8,128)(2,1)}), bf16[128,2048]{1,0:T(8,128)(2,1)}) %reduce-scatter.4.cloned.1.call-update) | async-done | bytes 524304 | tf_op jit(solution)/shard_map/reduce_scatter | solution.py:277
  210.9 40.0 %all_to_all.30 = bf16[8,64,704]{2,1,0:T(8,128)(2,1)S(1)} all-to-all(bf16[8,64,704]{2,1,0:T(8,128)(2,1)S(1)} %bitcast.180), channel_id=1, replica_groups=mesh['dp'=4,'seq'=8] {'seq'}, dimensions={0} | all-to-all | bytes 1441792 | tf_op jit(solution)/shard_map/all_to_all | solution.py:231
  258.5 40.5 %all-to-all-done.3 = bf16[8,128,704]{1,2,0:T(8,128)(2,1)S(1)} async-done(((bf16[8,128,704]{1,2,0:T(8,128)(2,1)}), bf16[8,128,704]{1,2,0:T(8,128)(2,1)S(1)}, u32[]{:S(2)}, u32[]{:S(2)}) %all-to-all-start.3) | async-done | bytes 1441824 | tf_op jit(solution)/shard_map/all_to_all | solution.py:231
  305.5 44.9 %collective-permute-done.7 = bf16[8,64,704]{2,1,0:T(8,128)(2,1)S(1)} collective-permute-done((bf16[8,64,704]{2,1,0:T(8,128)(2,1)S(1)}, bf16[8,64,704]{2,1,0:T(8,128)(2,1)S(1)}, u32[]{:S(2)}, u32[]{:S(2)}) %collective-permute-start.7) | collective-permute-done | bytes 720928 | tf_op jit(solution)/shard_map/ppermute | solution.py:227
  354.4 26.9 %collective-permute-done.10 = bf16[8,128,704]{1,2,0:T(8,128)(2,1)S(1)} collective-permute-done((bf16[8,128,704]{1,2,0:T(8,128)(2,1)S(1)}, bf16[8,128,704]{1,2,0:T(8,128)(2,1)S(1)}, u32[]{:S(2)}, u32[]{:S(2)}) %collective-permute-start.10) | collective-permute-done | bytes 1441824 | tf_op jit(solution)/shard_map/ppermute | solution.py:227
  388.0 6.7 copy.137
  394.7 6.8 copy.138
  412.6 9.6 %multiply_convert_fusion = (bf16[1024,704]{0,1:T(8,128)(2,1)}, bf16[1024,704]{0,1:T(8,128)(2,1)S(1)}, bf16[1024,704]{0,1:T(8,128)(2,1)S(1)}) fusion(f32[1024,704]{0,1:T(8,128)} %fusion.82, f32[1024,704]{0,1:T(8,128)S(1)} %fusion.83, bf16[1024,2048]{1,0:T(8,128)(2,1)} %all-gather.7.cloned.1.call-done, bf16[2048,704]{1,0:T(8,128)(2,1)} %bitcast.173), kind=kOutput, calls=%fused_computation.27 | convolution fusion | flops 2963603456 | bytes 17170432 | tf_op jit(solution)/shard_map/dot_general | solution.py:268
  432.6 7.1 convolution_convert_fusion
  439.7 39.8 %reduce-scatter.6.cloned.1.call-done = bf16[128,2048]{1,0:T(8,128)(2,1)} async-done(((bf16[1024,2048]{1,0:T(8,128)(2,1)}), bf16[128,2048]{1,0:T(8,128)(2,1)}) %reduce-scatter.6.cloned.1.call-update) | async-done | bytes 524304 | tf_op jit(solution)/shard_map/reduce_scatter | solution.py:277
  517.4 20.3 %collective-permute-done.29 = bf16[8,64,704]{2,1,0:T(8,128)(2,1)} collective-permute-done((bf16[8,64,704]{2,1,0:T(8,128)(2,1)}, bf16[8,64,704]{2,1,0:T(8,128)(2,1)}, u32[]{:S(2)}, u32[]{:S(2)}) %collective-permute-start.29) | collective-permute-done | bytes 720928 | tf_op jit(solution)/shard_map/ppermute | solution.py:227
  539.1 7.4 convolution_convert_fusion.5
  580.4 14.1 %attend_bwd.1 = (bf16[1024,768]{1,0:T(8,128)(2,1)}, f32[8,768]{1,0:T(8,128)}) custom-call(s32[4]{0:T(128)} %and_select_fusion.2.first_ref, s32[8,1024]{1,0:T(8,128)} %broadcast_in_dim.28.low_ref, f32[1024,128]{1,0:T(8,128)} %get-tuple-element.133.cos_ref, f32[1024,128]{1,0:T(8,128)} %get-tuple-element.132.s1_ref, f32[1024,128]{1,0:T(8,128)} %get-tuple-element.131.s2_ref, ...), custom_call_target="tpu_custom_call" | custom-call | flops 2684354560 | bytes 6291456 | tf_op jit(solution)/shard_map/attend_bwd/pallas_call | solution.py:199
  594.4 9.1 %fusion.6 = (bf16[2048]{0:T(1024)(128)(2,1)S(1)}, bf16[1024,2048]{1,0:T(8,128)(2,1)}) fusion(bf16[1024,2048]{1,0:T(8,128)(2,1)} %all-gather.5.cloned.1.call-done, f32[1024]{0:T(1024)S(1)} %copy-done.38, f32[1024]{0:T(1024)S(1)} %copy-done.27, bf16[1024,768]{1,0:T(8,128)(2,1)} %get-tuple-element.44, bf16[2048,768]{1,0:T(8,128)(2,1)} %bitcast.171), kind=kOutput, calls=%fused_computation.8 | convolution fusion | flops 3235903488 | bytes 13119488 | tf_op jit(solution)/shard_map/dot_general | solution.py:268
  624.3 6.9 convolution_convert_fusion.3
  645.7 38.0 %collective-permute-done.19 = bf16[8,64,256]{2,1,0:T(8,128)(2,1)S(1)} collective-permute-done((bf16[8,64,256]{2,1,0:T(8,128)(2,1)}, bf16[8,64,256]{2,1,0:T(8,128)(2,1)S(1)}, u32[]{:S(2)}, u32[]{:S(2)}) %collective-permute-start.19) | collective-permute-done | bytes 262176 | tf_op jit(solution)/shard_map/ppermute | solution.py:227
  689.9 6.6 all-to-all-done.5
  727.6 14.6 %all-to-all-done.4 = bf16[8,72,1024]{2,1,0:T(8,128)(2,1)} async-done(((bf16[8,72,1024]{2,1,0:T(8,128)(2,1)}), bf16[8,72,1024]{2,1,0:T(8,128)(2,1)}, u32[]{:S(2)}, u32[]{:S(2)}) %all-to-all-start.4) | async-done | bytes 1179680 | tf_op jit(solution)/shard_map/all_to_all | solution.py:249
  753.3 22.0 %collective-permute-done.14 = bf16[128,2048]{1,0:T(8,128)(2,1)} collective-permute-done((bf16[128,2048]{1,0:T(8,128)(2,1)}, bf16[128,2048]{1,0:T(8,128)(2,1)}, u32[]{:S(2)}, u32[]{:S(2)}) %collective-permute-start.14) | collective-permute-done | bytes 524320 | tf_op jit(solution)/shard_map/ppermute | solution.py:285
  (372 shorter events, 284.6 us)
Async XLA Ops:
  7.2 124.4 %all-gather.5.cloned.1.call-start = ((), (), s32[]{:S(2)}) async-start(), calls=%async_computation.9 | async-start | bytes 4718592 | tf_op jit(solution)/shard_map/all_gather | solution.py:281
  31.9 47.2 %all-to-all-start = ((bf16[8,72,768]{2,1,0:T(8,128)(2,1)}), bf16[8,72,768]{2,1,0:T(8,128)(2,1)}, u32[]{:S(2)}, u32[]{:S(2)}) async-start(bf16[8,72,768]{2,1,0:T(8,128)(2,1)} %pad_maximum_fusion.7), calls=%async_computation | async-start | bytes 1769472 | tf_op jit(solution)/shard_map/all_to_all | solution.py:231
  36.2 169.9 %reduce-scatter.4.cloned.1.call-start = ((), (), s32[]{:S(2)}) async-start(), calls=%async_computation.10 | async-start | bytes 4718592 | tf_op jit(solution)/shard_map/reduce_scatter | solution.py:277
  156.8 244.7 %all-gather.9.cloned.1.call-start = ((), (), s32[]{:S(2)}) async-start(), calls=%async_computation.12 | async-start | bytes 4718592 | tf_op jit(solution)/shard_map/all_gather | solution.py:281
  250.9 48.1 %all-to-all-start.3 = ((bf16[8,128,704]{1,2,0:T(8,128)(2,1)}), bf16[8,128,704]{1,2,0:T(8,128)(2,1)S(1)}, u32[]{:S(2)}, u32[]{:S(2)}) async-start(bf16[8,128,704]{1,2,0:T(8,128)(2,1)} %pad_maximum_fusion.5), calls=%async_computation.4 | async-start | bytes 2883584 | tf_op jit(solution)/shard_map/all_to_all | solution.py:231
  255.5 157.1 %all-gather.7.cloned.1.call-start = ((), (), s32[]{:S(2)}) async-start(), calls=%async_computation.11 | async-start | bytes 4718592 | tf_op jit(solution)/shard_map/all_gather | solution.py:281
  256.0 223.5 %reduce-scatter.6.cloned.1.call-start = ((), (), s32[]{:S(2)}) async-start(), calls=%async_computation.13 | async-start | bytes 4718592 | tf_op jit(solution)/shard_map/reduce_scatter | solution.py:277
  256.1 47.9 %collective-permute-start.8 = (bf16[8,64,704]{2,1,0:T(8,128)(2,1)S(1)}, bf16[8,64,704]{2,1,0:T(8,128)(2,1)S(1)}, u32[]{:S(2)}, u32[]{:S(2)}) collective-permute-start(bf16[8,64,704]{2,1,0:T(8,128)(2,1)S(1)} %all_to_all.30), channel_id=1, source_target_pairs={{0,24},{8,16},{16,8},{24,0},{1,25},{9,17},{17,9},{25,1},{2,26},{10... | collective-permute-start | bytes 2162696 | tf_op jit(solution)/shard_map/ppermute | solution.py:227
  299.0 54.8 %collective-permute-start.11 = (bf16[8,128,704]{1,2,0:T(8,128)(2,1)S(1)}, bf16[8,128,704]{1,2,0:T(8,128)(2,1)S(1)}, u32[]{:S(2)}, u32[]{:S(2)}) collective-permute-start(bf16[8,128,704]{1,2,0:T(8,128)(2,1)S(1)} %all-to-all-done.3), channel_id=1, source_target_pairs={{0,24},{8,16},{16,8},{24,0},{1,25},{9,17},{17,9},{25,1},{2,26},{10... | collective-permute-start | bytes 4325384 | tf_op jit(solution)/shard_map/ppermute | solution.py:227
  301.4 49.0 %collective-permute-start.7 = (bf16[8,64,704]{2,1,0:T(8,128)(2,1)S(1)}, bf16[8,64,704]{2,1,0:T(8,128)(2,1)S(1)}, u32[]{:S(2)}, u32[]{:S(2)}) collective-permute-start(bf16[8,64,704]{2,1,0:T(8,128)(2,1)S(1)} %all_to_all.30), channel_id=1, source_target_pairs={{0,16},{8,24},{16,0},{24,8},{1,17},{9,25},{17,1},{25,9},{2,18},{10... | collective-permute-start | bytes 2162696 | tf_op jit(solution)/shard_map/ppermute | solution.py:227
  302.0 49.3 %collective-permute-start.6 = (bf16[8,64,704]{2,1,0:T(8,128)(2,1)S(1)}, bf16[8,64,704]{2,1,0:T(8,128)(2,1)S(1)}, u32[]{:S(2)}, u32[]{:S(2)}) collective-permute-start(bf16[8,64,704]{2,1,0:T(8,128)(2,1)S(1)} %all_to_all.30), channel_id=1, source_target_pairs={{0,8},{8,0},{16,24},{24,16},{1,9},{9,1},{17,25},{25,17},{2,10},{10... | collective-permute-start | bytes 2162696 | tf_op jit(solution)/shard_map/ppermute | solution.py:227
  302.5 78.7 %collective-permute-start.10 = (bf16[8,128,704]{1,2,0:T(8,128)(2,1)S(1)}, bf16[8,128,704]{1,2,0:T(8,128)(2,1)S(1)}, u32[]{:S(2)}, u32[]{:S(2)}) collective-permute-start(bf16[8,128,704]{1,2,0:T(8,128)(2,1)S(1)} %all-to-all-done.3), channel_id=1, source_target_pairs={{0,16},{8,24},{16,0},{24,8},{1,17},{9,25},{17,1},{25,9},{2,18},{10... | collective-permute-start | bytes 4325384 | tf_op jit(solution)/shard_map/ppermute | solution.py:227
  304.0 77.8 %collective-permute-start.9 = (bf16[8,128,704]{1,2,0:T(8,128)(2,1)S(1)}, bf16[8,128,704]{1,2,0:T(8,128)(2,1)S(1)}, u32[]{:S(2)}, u32[]{:S(2)}) collective-permute-start(bf16[8,128,704]{1,2,0:T(8,128)(2,1)S(1)} %all-to-all-done.3), channel_id=1, source_target_pairs={{0,8},{8,0},{16,24},{24,16},{1,9},{9,1},{17,25},{25,17},{2,10},{10... | collective-permute-start | bytes 4325384 | tf_op jit(solution)/shard_map/ppermute | solution.py:227
  431.2 144.6 %all-gather.11.cloned.1.call-start = ((), (), s32[]{:S(2)}) async-start(), calls=%async_computation.14 | async-start | bytes 4718592 | tf_op jit(solution)/shard_map/all_gather | solution.py:281
  484.4 290.9 %reduce-scatter.8.cloned.1.call-start = ((), (), s32[]{:S(2)}) async-start(), calls=%async_computation.15 | async-start | bytes 4718592 | tf_op jit(solution)/shard_map/reduce_scatter | solution.py:277
  499.1 61.7 %collective-permute-start.30 = (bf16[8,64,704]{2,1,0:T(8,128)(2,1)}, bf16[8,64,704]{2,1,0:T(8,128)(2,1)}, u32[]{:S(2)}, u32[]{:S(2)}) collective-permute-start(bf16[8,64,704]{2,1,0:T(8,128)(2,1)} %bitcast.190), channel_id=1, source_target_pairs={{0,24},{8,16},{16,8},{24,0},{1,25},{9,17},{17,9},{25,1},{2,26},{10... | collective-permute-start | bytes 2162696 | tf_op jit(solution)/shard_map/ppermute | solution.py:227
  500.6 60.9 %collective-permute-start.28 = (bf16[8,64,704]{2,1,0:T(8,128)(2,1)}, bf16[8,64,704]{2,1,0:T(8,128)(2,1)}, u32[]{:S(2)}, u32[]{:S(2)}) collective-permute-start(bf16[8,64,704]{2,1,0:T(8,128)(2,1)} %bitcast.187), channel_id=1, source_target_pairs={{0,8},{8,0},{16,24},{24,16},{1,9},{9,1},{17,25},{25,17},{2,10},{10... | collective-permute-start | bytes 2162696 | tf_op jit(solution)/shard_map/ppermute | solution.py:227
  514.4 56.9 %collective-permute-start.23 = (bf16[8,64,704]{2,1,0:T(8,128)(2,1)}, bf16[8,64,704]{2,1,0:T(8,128)(2,1)}, u32[]{:S(2)}, u32[]{:S(2)}) collective-permute-start(bf16[8,64,704]{2,1,0:T(8,128)(2,1)} %bitcast.191), channel_id=1, source_target_pairs={{0,16},{8,24},{16,0},{24,8},{1,17},{9,25},{17,1},{25,9},{2,18},{10... | collective-permute-start | bytes 2162696 | tf_op jit(solution)/shard_map/ppermute | solution.py:227
  515.9 56.9 %collective-permute-start.24 = (bf16[8,64,704]{2,1,0:T(8,128)(2,1)}, bf16[8,64,704]{2,1,0:T(8,128)(2,1)}, u32[]{:S(2)}, u32[]{:S(2)}) collective-permute-start(bf16[8,64,704]{2,1,0:T(8,128)(2,1)} %bitcast.189), channel_id=1, source_target_pairs={{0,24},{8,16},{16,8},{24,0},{1,25},{9,17},{17,9},{25,1},{2,26},{10... | collective-permute-start | bytes 2162696 | tf_op jit(solution)/shard_map/ppermute | solution.py:227
  607.3 89.2 %all-to-all-start.5 = ((bf16[8,192,704]{2,1,0:T(8,128)(2,1)}), bf16[8,192,704]{2,1,0:T(8,128)(2,1)S(1)}, u32[]{:S(2)}, u32[]{:S(2)}) async-start(bf16[8,192,704]{2,1,0:T(8,128)(2,1)} %pad_maximum_fusion.4), calls=%async_computation.8 | async-start | bytes 4718592 | tf_op jit(solution)/shard_map/all_to_all | solution.py:249
  634.9 51.3 %collective-permute-start.16 = (bf16[8,72,768]{2,1,0:T(8,128)(2,1)}, bf16[8,72,768]{2,1,0:T(8,128)(2,1)}, u32[]{:S(2)}, u32[]{:S(2)}) collective-permute-start(bf16[8,72,768]{2,1,0:T(8,128)(2,1)} %get-tuple-element.55), channel_id=1, source_target_pairs={{0,8},{8,0},{16,24},{24,16},{1,9},{9,1},{17,25},{25,17},{2,10},{10... | collective-permute-start | bytes 2654216 | tf_op jit(solution)/shard_map/ppermute | solution.py:227
  639.0 47.2 %collective-permute-start.18 = (bf16[8,72,768]{2,1,0:T(8,128)(2,1)}, bf16[8,72,768]{2,1,0:T(8,128)(2,1)}, u32[]{:S(2)}, u32[]{:S(2)}) collective-permute-start(bf16[8,72,768]{2,1,0:T(8,128)(2,1)} %get-tuple-element.56), channel_id=1, source_target_pairs={{0,24},{8,16},{16,8},{24,0},{1,25},{9,17},{17,9},{25,1},{2,26},{10... | collective-permute-start | bytes 2654216 | tf_op jit(solution)/shard_map/ppermute | solution.py:227
  639.1 47.2 %collective-permute-start.17 = (bf16[8,72,768]{2,1,0:T(8,128)(2,1)}, bf16[8,72,768]{2,1,0:T(8,128)(2,1)}, u32[]{:S(2)}, u32[]{:S(2)}) collective-permute-start(bf16[8,72,768]{2,1,0:T(8,128)(2,1)} %get-tuple-element.57), channel_id=1, source_target_pairs={{0,16},{8,24},{16,0},{24,8},{1,17},{9,25},{17,1},{25,9},{2,18},{10... | collective-permute-start | bytes 2654216 | tf_op jit(solution)/shard_map/ppermute | solution.py:227
  726.5 48.9 %collective-permute-start.14 = (bf16[128,2048]{1,0:T(8,128)(2,1)}, bf16[128,2048]{1,0:T(8,128)(2,1)}, u32[]{:S(2)}, u32[]{:S(2)}) collective-permute-start(bf16[128,2048]{1,0:T(8,128)(2,1)} %get-tuple-element.75), channel_id=1, source_target_pairs={{0,4},{1,5},{2,6},{3,7},{4,0},{5,1},{6,2},{7,3},{8,12},{9,13},{10,... | collective-permute-start | bytes 1572872 | tf_op jit(solution)/shard_map/ppermute | solution.py:285
  (75 other events, 1499.3 us)
Sparse Core Ops, SparseCore 0:
  10.9 71.0 all-gather.4
  156.9 49.2 reduce-scatter.3
  211.1 79.9 all-gather.8
  292.5 45.0 all-gather.6
  431.4 48.1 reduce-scatter.5
  484.5 45.3 all-gather.10
  603.7 91.0 reduce-scatter.7
where the time goes:
time: 795 us; the launch traced here: 790 us
  waiting for transfers between devices  386 us (49%)
  local copies, waits for them, and re-layouts  99.8 us (13%)
  matrix products  90.1 us (11%)
  other arithmetic  70 us (9%)
  starting transfers between devices  63.9 us (8%)
  blocking collectives  40 us (5%)
  Pallas kernels  23.7 us (3%)
  between operations  15.7 us (2%)
    ppermute x27, waiting for transfers between devices, swap_dp(): lax.ppermute(values, 'dp', [(d, d ^ rel) for d in range(lax.axis_size('dp...  177 us
    dot_general x15, matrix products, dot(): lax.dot_general(left, right, (dims, ((), ())), preferred_element_type=F32)  90.1 us
    reduce_scatter x3, waiting for transfers between devices, own_rows(): lax.psum_scatter(partial.astype(BF), 'seq', scatter_dimension=0, tiled=True)  89 us
    all_to_all x3, waiting for transfers between devices, fetch(): mine = lax.all_to_all(view, 'seq', split_axis=0, concat_axis=0, tiled=True)  76.8 us
    all_to_all x1, blocking collectives, fetch(): mine = lax.all_to_all(view, 'seq', split_axis=0, concat_axis=0, tiled=True)  40 us
    ppermute x27, starting transfers between devices, swap_dp(): lax.ppermute(values, 'dp', [(d, d ^ rel) for d in range(lax.axis_size('dp...  35.4 us
    ppermute x3, waiting for transfers between devices, chip_shift(): lax.ppermute(values, 'seq', [(s, (s + 2 * k) % groups) for s in range(gro...  22 us
    all_to_all x2, waiting for transfers between devices, send_back(): lax.all_to_all(summed, 'seq', split_axis=0, concat_axis=0, tiled=True)  21.2 us
  transfers between devices with their start and end apart: 43, of which 19 were waited for; matrix products, arithmetic and copies ran while one was open for 26% of the time, Pallas kernels for 2%

commit v1 on v0

--- a/solution.py
+++ b/solution.py
@@ -227,8 +227,11 @@
     return lax.ppermute(values, "dp", [(d, d ^ rel) for d in range(lax.axis_size("dp"))])
 
 
-def fetch(view):
-    mine = lax.all_to_all(view, "seq", split_axis=0, concat_axis=0, tiled=True)
+def take(view):
+    return lax.all_to_all(view, "seq", split_axis=0, concat_axis=0, tiled=True)
+
+
+def spread(mine):
     return [mine] + [swap_dp(mine, rel) for rel in range(1, lax.axis_size("dp"))]
 
 
@@ -239,7 +242,7 @@
 
 def reduce_dp(parts):
     total = parts[0].astype(F32)
-    moved = [swap_dp(parts[rel], rel) for rel in range(1, parts.shape[0])]
+    moved = [swap_dp(parts[rel], rel) for rel in range(1, len(parts))]
     for piece in moved:
         total = total + piece.astype(F32)
     return total.astype(BF)
@@ -299,11 +302,11 @@
     moved = core_swap(theirs, groups)
     pair = (ours.astype(F32) + moved.astype(F32)).astype(BF)
     chip = me // 2
-    total = lax.dynamic_index_in_dim(pair, chip, 0, keepdims=False).astype(F32)
-    for k in range(1, chips):
-        part = lax.dynamic_index_in_dim(pair, (chip + k) % chips, 0, keepdims=False)
-        total = total + chip_shift(part, k, groups).astype(F32)
-    return total
+    moved = [
+        chip_shift(lax.dynamic_index_in_dim(pair, (chip + k) % chips, 0, keepdims=False), k, groups)
+        for k in range(1, chips)
+    ]
+    return [lax.dynamic_index_in_dim(pair, chip, 0, keepdims=False)] + moved
 
 
 def layer(
@@ -335,7 +338,6 @@
 
     own = relate(inputs, mine, copies, 1)
     own_up = relate(upstream, mine, copies, 1)
-    x_all = every(own)
 
     def by_group(weight, parts=1):
         cols = weight.shape[1] // (parts * groups)
@@ -357,9 +359,13 @@
     view_qkv = jnp.concatenate(
         [by_group(qkv_weight, 3), jnp.broadcast_to(extra[None], (groups, 8, 3 * hc))], axis=1
     )
-    pieces_qkv = fetch(view_qkv)
+    taken, own = lax.optimization_barrier((take(view_qkv), own))
+    x_all = every(own)
+    pieces_qkv = spread(taken)
     weight_qkv = stack_rows(pieces_qkv, 0, rows)
-    weight_out = stack_rows(fetch(by_group(out_weight)), 0, rows)
+    taken, own_up = lax.optimization_barrier((take(by_group(out_weight)), own_up))
+    up_all = every(own_up)
+    weight_out = stack_rows(spread(taken), 0, rows)
     spot = pieces_qkv[0][:, rows, 4 * rows + nbias : 4 * rows + nbias + 2 * tokens]
     positions = (
         spot[:, :tokens].astype(jnp.int32) * 256 + spot[:, tokens:].astype(jnp.int32)
@@ -378,16 +384,13 @@
     first = (jnp.min(lowest.reshape(length // bq, bq), axis=1) // bq).astype(jnp.int32)
 
     view_gu = jnp.concatenate([by_group(gate_weight), by_group(up_weight)], axis=1)
-    view_gu, view_down, own_up, x_all = lax.optimization_barrier(
-        (view_gu, by_group(down_weight), own_up, x_all)
-    )
-    up_all = every(own_up)
-    pieces_gu = fetch(view_gu)
+    view_gu, view_down, x_all = lax.optimization_barrier((view_gu, by_group(down_weight), x_all))
+    pieces_gu = spread(take(view_gu))
     weight_gate = stack_rows(pieces_gu, 0, rows)
     weight_up = stack_rows(pieces_gu, rows, rows)
-    weight_down = stack_rows(fetch(view_down), 0, rows)
-
-    unit_all, _ = unit_of(x_all.astype(F32))
+    weight_down = stack_rows(spread(take(view_down)), 0, rows)
+
+    unit_all, unused = unit_of(x_all.astype(F32))
     normed_one = (unit_all * gain_one + shift_one).astype(BF)
     projected = dot(normed_one, weight_qkv, NN) + bias_mine
     qkv, context, lse = attend_fwd(projected, tables, low8, first, heads, bq)
@@ -406,31 +409,37 @@
     grad_up = (grad_hidden * silu).astype(BF)
     grad_normed_two = own_rows(dot(grad_gate, weight_gate, NT) + dot(grad_up, weight_up, NT))
     down_part = dot(hidden, weight_down, NT).astype(BF)
-    grad_gate_weight = dot(normed_two, grad_gate, TN).astype(BF)
-    grad_up_weight = dot(normed_two, grad_up, TN).astype(BF)
-    grad_down_weight = dot(up_all, hidden, TN).astype(BF)
-
-    def by_owner(grad):
-        return grad.reshape(copies, groups, rows, grad.shape[1])
-
+    block = width // copies
+
+    def by_owner(left, right):
+        return [
+            dot(left[:, m * block : (m + 1) * block], right, TN).astype(BF).reshape(groups, rows, -1)
+            for m in range(copies)
+        ]
+
+    grad_gate_weight = by_owner(normed_two, grad_gate)
+    grad_up_weight = by_owner(normed_two, grad_up)
+    grad_down_weight = by_owner(up_all, hidden)
     sum_ffn = jnp.concatenate(
-        [
-            reduce_dp(by_owner(grad_gate_weight)),
-            reduce_dp(by_owner(grad_up_weight)),
-            reduce_dp(by_owner(grad_down_weight)),
-        ],
+        [reduce_dp(grad_gate_weight), reduce_dp(grad_up_weight), reduce_dp(grad_down_weight)],
         axis=1,
     )
     sum_ffn = send_back(sum_ffn).transpose(1, 0, 2)
 
     grad_middle = own_up.astype(F32) + norm_back(grad_normed_two, unit_two, factor_two, gain_two)
-    grad_mixed, down_part = lax.optimization_barrier((grad_middle.astype(BF), down_part))
-    output = (middle + own_rows_beside(down_part, me, groups)).astype(BF)
+    grad_mixed = grad_middle.astype(BF)
+    down_sum = own_rows_beside(down_part, me, groups)
     grad_mixed = every(grad_mixed)
     grad_context = dot(grad_mixed, weight_out, NN).astype(BF)
     grad_projected, bias_part = attend_bwd(qkv, context, lse, grad_context, tables, low8, first, heads, bq)
     dqkv = dot(grad_projected, weight_qkv, NT).astype(BF)
     grad_normed_one = own_rows(dqkv)
+
+    late, unused = lax.optimization_barrier((down_sum[0], bias_part))
+    total = late.astype(F32)
+    for piece in down_sum[1:]:
+        total = total + piece.astype(F32)
+    output = (middle + total).astype(BF)
 
     bias_part = jnp.sum(bias_part, axis=0).reshape(3, 1, hc) * chosen[None, :, None]
     bias_part = relate(bias_part.reshape(-1), mine, copies, 0).reshape(copies, groups, nbias)
@@ -444,10 +453,9 @@
     parts = jnp.concatenate(parts, axis=3)
     parts = jnp.pad(parts, ((0, 0), (0, 0), (0, 7), (0, 3 * hc - parts.shape[3]))).astype(BF)
 
-    grad_out_weight = dot(grad_mixed, context, TN).astype(BF)
-    sum_out = reduce_dp(by_owner(grad_out_weight))
-    grad_qkv_weight = dot(normed_one, grad_projected, TN).astype(BF)
-    sum_qkv = reduce_dp(jnp.concatenate([by_owner(grad_qkv_weight), parts], axis=2))
+    sum_out = reduce_dp(by_owner(grad_mixed, context))
+    grad_qkv_weight = by_owner(normed_one, grad_projected)
+    sum_qkv = reduce_dp([jnp.concatenate([grad_qkv_weight[m], parts[m]], axis=1) for m in range(copies)])
     sum_attn = jnp.concatenate([sum_qkv, jnp.pad(sum_out, ((0, 0), (0, 8), (0, 0)))], axis=2)
     sum_attn = send_back(sum_attn)
     total = jnp.sum(sum_attn[:, rows].astype(F32), axis=0)

time: 795 us -> 802 us (level)
    ppermute x3, waiting for transfers between devices: 22 us -> 0.01 us  [chip_shift(): lax.ppermute(values, 'seq', [(s, (s + 2 * k) % groups) for s in range(gro...]
    slice x10 -> x0, local copies, waits for them, and re-layouts: 18.3 us -> none  [reduce_dp(): moved = [swap_dp(parts[rel], rel) for rel in range(1, parts.shape[0])]]
    all_to_all x2, waiting for transfers between devices: 21.2 us -> 35.1 us  [send_back(): lax.all_to_all(summed, 'seq', split_axis=0, concat_axis=0, tiled=True)]
    convert_element_type x0 -> x9, local copies, waits for them, and re-layouts: none -> 13.8 us  [by_owner(): dot(left[:, m * block:(m + 1) * block], right, TN).astype(BF)]
    reduce_scatter x3, waiting for transfers between devices: 89 us -> 99.4 us  [own_rows(): lax.psum_scatter(partial.astype(BF), 'seq', scatter_dimension=0, tiled=True)]
    dot_general x15 -> x30, matrix products: 90.1 us -> 97.3 us  [dot(): lax.dot_general(left, right, (dims, ((), ())), preferred_element_type=F32)]
  transfers between devices with their start and end apart: 43 -> 43, of which waited for: 19 -> 17; matrix products, arithmetic and copies ran while one was open for 26% -> 25% of each run, Pallas kernels for 2% -> 2%
where the time goes in v1:
time: 802 us; the launch traced here: 791 us
  waiting for transfers between devices  388 us (48%)
  matrix products  97.3 us (12%)
  local copies, waits for them, and re-layouts  96 us (12%)
  starting transfers between devices  66.4 us (8%)
  other arithmetic  63.4 us (8%)
  blocking collectives  40 us (5%)
  Pallas kernels  23.3 us (3%)
  between operations  15.8 us (2%)
    ppermute x27, waiting for transfers between devices, swap_dp(): lax.ppermute(values, 'dp', [(d, d ^ rel) for d in range(lax.axis_size('dp...  177 us
    reduce_scatter x3, waiting for transfers between devices, own_rows(): lax.psum_scatter(partial.astype(BF), 'seq', scatter_dimension=0, tiled=True)  99.4 us
    dot_general x30, matrix products, dot(): lax.dot_general(left, right, (dims, ((), ())), preferred_element_type=F32)  97.3 us
    all_to_all x3, waiting for transfers between devices, take(): return lax.all_to_all(view, 'seq', split_axis=0, concat_axis=0, tiled=True)  76.6 us
    all_to_all x1, blocking collectives, take(): return lax.all_to_all(view, 'seq', split_axis=0, concat_axis=0, tiled=True)  40 us
    ppermute x27, starting transfers between devices, swap_dp(): lax.ppermute(values, 'dp', [(d, d ^ rel) for d in range(lax.axis_size('dp...  37.4 us
    all_to_all x2, waiting for transfers between devices, send_back(): lax.all_to_all(summed, 'seq', split_axis=0, concat_axis=0, tiled=True)  35.1 us
    reshape x10, local copies, waits for them, and re-layouts, wide(): return value.astype(F32).reshape(rows, -1)  19.7 us
  transfers between devices with their start and end apart: 43, of which 17 were waited for; matrix products, arithmetic and copies ran while one was open for 25% of the time, Pallas kernels for 2%

profile of v1, /device:TPU:0, one launch (start us, length us, event | category | flops | bytes accessed | tf_op | source)
XLA Modules:
  0.0 790.6 jit_solution(15262829712219198451)
XLA Ops:
  14.9 6.4 all-to-all-start
  22.5 21.8 %all-to-all-done = bf16[8,72,768]{2,1,0:T(8,128)(2,1)S(1)} async-done(((bf16[8,72,768]{2,1,0:T(8,128)(2,1)}), bf16[8,72,768]{2,1,0:T(8,128)(2,1)S(1)}, u32[]{:S(2)}, u32[]{:S(2)}) %all-to-all-start) | async-done | bytes 884768 | tf_op jit(solution)/shard_map/all_to_all | solution.py:231
  50.7 13.4 %all-to-all-done.1 = bf16[8,64,256]{2,1,0:T(8,128)(2,1)} async-done(((bf16[8,64,256]{2,1,0:T(8,128)(2,1)}), bf16[8,64,256]{2,1,0:T(8,128)(2,1)}, u32[]{:S(2)}, u32[]{:S(2)}) %all-to-all-start.1) | async-done | bytes 262176 | tf_op jit(solution)/shard_map/all_to_all | solution.py:231
  87.4 15.8 %collective-permute-done.2 = bf16[8,72,768]{2,0,1:T(8,128)(2,1)} collective-permute-done((bf16[8,72,768]{2,0,1:T(8,128)(2,1)S(1)}, bf16[8,72,768]{2,0,1:T(8,128)(2,1)}, u32[]{:S(2)}, u32[]{:S(2)}) %collective-permute-start.2) | collective-permute-done | bytes 884768 | tf_op jit(solution)/shard_map/ppermute | solution.py:227
  103.9 15.3 %collective-permute-done.1 = bf16[8,72,768]{2,0,1:T(8,128)(2,1)} collective-permute-done((bf16[8,72,768]{2,0,1:T(8,128)(2,1)S(1)}, bf16[8,72,768]{2,0,1:T(8,128)(2,1)}, u32[]{:S(2)}, u32[]{:S(2)}) %collective-permute-start.1) | collective-permute-done | bytes 884768 | tf_op jit(solution)/shard_map/ppermute | solution.py:227
  141.2 9.3 %attend_fwd.1 = (bf16[1024,768]{1,0:T(8,128)(2,1)}, bf16[1024,256]{1,0:T(8,128)(2,1)}, f32[8,1024]{1,0:T(8,128)}) custom-call(s32[4]{0:T(128)} %and_select_fusion.2.first_ref, s32[8,1024]{1,0:T(8,128)} %broadcast_in_dim.28.low_ref, f32[1024,128]{1,0:T(8,128)} %get-tuple-element.124.cos_ref, f32[1024,128]{1,0:T(8,128)} %get-tuple-element.123.s1_ref, ...), custom_call_target="tpu_custom_call" | custom-call | flops 1073741824 | bytes 6291456 | tf_op jit(solution)/shard_map/attend_fwd/pallas_call | solution.py:124
  155.2 51.4 %reduce-scatter.4.cloned.1.call-done = bf16[128,2048]{1,0:T(8,128)(2,1)} async-done(((bf16[1024,2048]{1,0:T(8,128)(2,1)}), bf16[128,2048]{1,0:T(8,128)(2,1)}) %reduce-scatter.4.cloned.1.call-update) | async-done | bytes 524304 | tf_op jit(solution)/shard_map/reduce_scatter | solution.py:280
  210.4 40.0 %all_to_all.30 = bf16[8,64,704]{2,1,0:T(8,128)(2,1)S(1)} all-to-all(bf16[8,64,704]{2,1,0:T(8,128)(2,1)S(1)} %bitcast.190), channel_id=1, replica_groups=mesh['dp'=4,'seq'=8] {'seq'}, dimensions={0} | all-to-all | bytes 1441792 | tf_op jit(solution)/shard_map/all_to_all | solution.py:231
  257.1 41.4 %all-to-all-done.2 = bf16[8,128,704]{1,2,0:T(8,128)(2,1)S(1)} async-done(((bf16[8,128,704]{1,2,0:T(8,128)(2,1)}), bf16[8,128,704]{1,2,0:T(8,128)(2,1)S(1)}, u32[]{:S(2)}, u32[]{:S(2)}) %all-to-all-start.2) | async-done | bytes 1441824 | tf_op jit(solution)/shard_map/all_to_all | solution.py:231
  304.9 45.8 %collective-permute-done.11 = bf16[8,64,704]{2,1,0:T(8,128)(2,1)S(1)} collective-permute-done((bf16[8,64,704]{2,1,0:T(8,128)(2,1)S(1)}, bf16[8,64,704]{2,1,0:T(8,128)(2,1)S(1)}, u32[]{:S(2)}, u32[]{:S(2)}) %collective-permute-start.11) | collective-permute-done | bytes 720928 | tf_op jit(solution)/shard_map/ppermute | solution.py:227
  350.8 15.9 %collective-permute-done.9 = bf16[8,64,704]{2,1,0:T(8,128)(2,1)S(1)} collective-permute-done((bf16[8,64,704]{2,1,0:T(8,128)(2,1)S(1)}, bf16[8,64,704]{2,1,0:T(8,128)(2,1)S(1)}, u32[]{:S(2)}, u32[]{:S(2)}) %collective-permute-start.9) | collective-permute-done | bytes 720928 | tf_op jit(solution)/shard_map/ppermute | solution.py:227
  371.7 25.9 %collective-permute-done.8 = bf16[8,128,704]{1,2,0:T(8,128)(2,1)S(1)} collective-permute-done((bf16[8,128,704]{1,2,0:T(8,128)(2,1)S(1)}, bf16[8,128,704]{1,2,0:T(8,128)(2,1)S(1)}, u32[]{:S(2)}, u32[]{:S(2)}) %collective-permute-start.8) | collective-permute-done | bytes 1441824 | tf_op jit(solution)/shard_map/ppermute | solution.py:227
  403.8 6.6 copy.145
  410.4 7.0 copy.144
  417.5 8.1 %fusion.95 = f32[1024,704]{0,1:T(8,128)} fusion(bf16[1024,2048]{1,0:T(8,128)(2,1)} %all-gather.7.cloned.1.call-done, bf16[2048,704]{1,0:T(8,128)(2,1)} %bitcast.186), kind=kOutput, calls=%fused_computation.233 | convolution fusion | flops 2952790016 | bytes 9961472 | tf_op jit(solution)/shard_map/dot_general | solution.py:271
  430.4 10.4 %multiply_convert_fusion.1 = (bf16[1024,704]{0,1:T(8,128)(2,1)S(1)}, bf16[1024,704]{0,1:T(8,128)(2,1)S(1)}, bf16[1024,704]{0,1:T(8,128)(2,1)}) fusion(f32[1024,704]{0,1:T(8,128)} %fusion.94, f32[1024,704]{0,1:T(8,128)} %fusion.95, bf16[1024,2048]{1,0:T(8,128)(2,1)} %all-gather.9.cloned.1.call-done, bf16[2048,704]{1,0:T(8,128)(2,1)} %bitcast.184), kind=kOutput, calls=%fused_computation.21 | convolution fusion | flops 2963603456 | bytes 17170432 | tf_op jit(solution)/shard_map/dot_general | solution.py:271
  449.9 48.0 %reduce-scatter.6.cloned.1.call-done = bf16[128,2048]{1,0:T(8,128)(2,1)} async-done(((bf16[1024,2048]{1,0:T(8,128)(2,1)}), bf16[128,2048]{1,0:T(8,128)(2,1)}) %reduce-scatter.6.cloned.1.call-update) | async-done | bytes 524304 | tf_op jit(solution)/shard_map/reduce_scatter | solution.py:280
  574.3 8.6 %collective-permute-done.26 = bf16[8,64,704]{2,1,0:T(8,128)(2,1)} collective-permute-done((bf16[8,64,704]{2,1,0:T(8,128)(2,1)}, bf16[8,64,704]{2,1,0:T(8,128)(2,1)}, u32[]{:S(2)}, u32[]{:S(2)}) %collective-permute-start.26) | collective-permute-done | bytes 720928 | tf_op jit(solution)/shard_map/ppermute | solution.py:227
  590.4 14.0 %attend_bwd.1 = (bf16[1024,768]{1,0:T(8,128)(2,1)}, f32[8,768]{1,0:T(8,128)}) custom-call(s32[4]{0:T(128)} %and_select_fusion.2.first_ref, s32[8,1024]{1,0:T(8,128)} %broadcast_in_dim.28.low_ref, f32[1024,128]{1,0:T(8,128)} %get-tuple-element.124.cos_ref, f32[1024,128]{1,0:T(8,128)} %get-tuple-element.123.s1_ref, f32[1024,128]{1,0:T(8,128)} %get-tuple-element.122.s2_ref, ...), custom_call_target="tpu_custom_call" | custom-call | flops 2684354560 | bytes 6291456 | tf_op jit(solution)/shard_map/attend_bwd/pallas_call | solution.py:199
  604.4 9.1 %fusion.6 = (bf16[2048]{0:T(1024)(128)(2,1)S(1)}, bf16[1024,2048]{1,0:T(8,128)(2,1)}) fusion(bf16[1024,2048]{1,0:T(8,128)(2,1)} %all-gather.5.cloned.1.call-done, f32[1024]{0:T(1024)S(1)} %add_rsqrt_fusion, f32[1024]{0:T(1024)S(1)} %broadcast_multiply_fusion.1, bf16[1024,768]{1,0:T(8,128)(2,1)} %get-tuple-element.49, bf16[2048,768]{1,0:T(8,128)(2,1)} %bitcast.182), kind=kOutput, calls=%fused_computation.8 | convolution fusion | flops 3235903488 | bytes 13119488 | tf_op jit(solution)/shard_map/dot_general | solution.py:271
  641.6 36.1 %collective-permute-done.19 = bf16[8,64,256]{2,1,0:T(8,128)(2,1)S(1)} collective-permute-done((bf16[8,64,256]{2,1,0:T(8,128)(2,1)S(1)}, bf16[8,64,256]{2,1,0:T(8,128)(2,1)S(1)}, u32[]{:S(2)}, u32[]{:S(2)}) %collective-permute-start.19) | collective-permute-done | bytes 262176 | tf_op jit(solution)/shard_map/ppermute | solution.py:227
  690.2 6.1 collective-permute-done.21
  698.1 9.0 %all-to-all-done.5 = bf16[8,192,704]{2,1,0:T(8,128)(2,1)S(1)} async-done(((bf16[8,192,704]{2,1,0:T(8,128)(2,1)}), bf16[8,192,704]{2,1,0:T(8,128)(2,1)S(1)}, u32[]{:S(2)}, u32[]{:S(2)}) %all-to-all-start.5) | async-done | bytes 2162720 | tf_op jit(solution)/shard_map/all_to_all | solution.py:252
  737.7 26.1 %all-to-all-done.4 = bf16[8,72,1024]{2,1,0:T(8,128)(2,1)} async-done(((bf16[8,72,1024]{2,1,0:T(8,128)(2,1)}), bf16[8,72,1024]{2,1,0:T(8,128)(2,1)}, u32[]{:S(2)}, u32[]{:S(2)}) %all-to-all-start.4) | async-done | bytes 1179680 | tf_op jit(solution)/shard_map/all_to_all | solution.py:252
  (382 shorter events, 283.2 us)
Async XLA Ops:
  21.3 107.6 %all-gather.5.cloned.1.call-start = ((), (), s32[]{:S(2)}) async-start(), calls=%async_computation.9 | async-start | bytes 4718592 | tf_op jit(solution)/shard_map/all_gather | solution.py:284
  49.4 157.2 %reduce-scatter.4.cloned.1.call-start = ((), (), s32[]{:S(2)}) async-start(), calls=%async_computation.10 | async-start | bytes 4718592 | tf_op jit(solution)/shard_map/reduce_scatter | solution.py:280
  155.0 262.5 %all-gather.7.cloned.1.call-start = ((), (), s32[]{:S(2)}) async-start(), calls=%async_computation.11 | async-start | bytes 4718592 | tf_op jit(solution)/shard_map/all_gather | solution.py:284
  254.9 175.5 %all-gather.9.cloned.1.call-start = ((), (), s32[]{:S(2)}) async-start(), calls=%async_computation.12 | async-start | bytes 4718592 | tf_op jit(solution)/shard_map/all_gather | solution.py:284
  255.5 242.4 %reduce-scatter.6.cloned.1.call-start = ((), (), s32[]{:S(2)}) async-start(), calls=%async_computation.13 | async-start | bytes 4718592 | tf_op jit(solution)/shard_map/reduce_scatter | solution.py:280
  298.5 72.0 %collective-permute-start.6 = (bf16[8,128,704]{1,2,0:T(8,128)(2,1)S(1)}, bf16[8,128,704]{1,2,0:T(8,128)(2,1)S(1)}, u32[]{:S(2)}, u32[]{:S(2)}) collective-permute-start(bf16[8,128,704]{1,2,0:T(8,128)(2,1)S(1)} %all-to-all-done.2), channel_id=1, source_target_pairs={{0,8},{8,0},{16,24},{24,16},{1,9},{9,1},{17,25},{25,17},{2,10},{10... | collective-permute-start | bytes 4325384 | tf_op jit(solution)/shard_map/ppermute | solution.py:227
  301.4 65.3 %collective-permute-start.9 = (bf16[8,64,704]{2,1,0:T(8,128)(2,1)S(1)}, bf16[8,64,704]{2,1,0:T(8,128)(2,1)S(1)}, u32[]{:S(2)}, u32[]{:S(2)}) collective-permute-start(bf16[8,64,704]{2,1,0:T(8,128)(2,1)S(1)} %all_to_all.30), channel_id=1, source_target_pairs={{0,8},{8,0},{16,24},{24,16},{1,9},{9,1},{17,25},{25,17},{2,10},{10... | collective-permute-start | bytes 2162696 | tf_op jit(solution)/shard_map/ppermute | solution.py:227
  302.9 68.2 %collective-permute-start.7 = (bf16[8,128,704]{1,2,0:T(8,128)(2,1)S(1)}, bf16[8,128,704]{1,2,0:T(8,128)(2,1)S(1)}, u32[]{:S(2)}, u32[]{:S(2)}) collective-permute-start(bf16[8,128,704]{1,2,0:T(8,128)(2,1)S(1)} %all-to-all-done.2), channel_id=1, source_target_pairs={{0,16},{8,24},{16,0},{24,8},{1,17},{9,25},{17,1},{25,9},{2,18},{10... | collective-permute-start | bytes 4325384 | tf_op jit(solution)/shard_map/ppermute | solution.py:227
  303.5 94.1 %collective-permute-start.8 = (bf16[8,128,704]{1,2,0:T(8,128)(2,1)S(1)}, bf16[8,128,704]{1,2,0:T(8,128)(2,1)S(1)}, u32[]{:S(2)}, u32[]{:S(2)}) collective-permute-start(bf16[8,128,704]{1,2,0:T(8,128)(2,1)S(1)} %all-to-all-done.2), channel_id=1, source_target_pairs={{0,24},{8,16},{16,8},{24,0},{1,25},{9,17},{17,9},{25,1},{2,26},{10... | collective-permute-start | bytes 4325384 | tf_op jit(solution)/shard_map/ppermute | solution.py:227
  449.9 136.0 %all-gather.11.cloned.1.call-start = ((), (), s32[]{:S(2)}) async-start(), calls=%async_computation.14 | async-start | bytes 4718592 | tf_op jit(solution)/shard_map/all_gather | solution.py:284
  502.7 274.0 %reduce-scatter.8.cloned.1.call-start = ((), (), s32[]{:S(2)}) async-start(), calls=%async_computation.15 | async-start | bytes 4718592 | tf_op jit(solution)/shard_map/reduce_scatter | solution.py:280
  511.5 57.2 %collective-permute-start.23 = (bf16[8,64,704]{2,1,0:T(8,128)(2,1)}, bf16[8,64,704]{2,1,0:T(8,128)(2,1)}, u32[]{:S(2)}, u32[]{:S(2)}) collective-permute-start(bf16[8,64,704]{2,1,0:T(8,128)(2,1)} %bitcast.51), channel_id=1, source_target_pairs={{0,16},{8,24},{16,0},{24,8},{1,17},{9,25},{17,1},{25,9},{2,18},{10... | collective-permute-start | bytes 2162696 | tf_op jit(solution)/shard_map/ppermute | solution.py:227
  516.7 53.6 %collective-permute-start.24 = (bf16[8,64,704]{2,1,0:T(8,128)(2,1)}, bf16[8,64,704]{2,1,0:T(8,128)(2,1)}, u32[]{:S(2)}, u32[]{:S(2)}) collective-permute-start(bf16[8,64,704]{2,1,0:T(8,128)(2,1)} %bitcast.52), channel_id=1, source_target_pairs={{0,24},{8,16},{16,8},{24,0},{1,25},{9,17},{17,9},{25,1},{2,26},{10... | collective-permute-start | bytes 2162696 | tf_op jit(solution)/shard_map/ppermute | solution.py:227
  520.9 52.8 %collective-permute-start.25 = (bf16[8,64,704]{2,1,0:T(8,128)(2,1)}, bf16[8,64,704]{2,1,0:T(8,128)(2,1)}, u32[]{:S(2)}, u32[]{:S(2)}) collective-permute-start(bf16[8,64,704]{2,1,0:T(8,128)(2,1)} %bitcast.54), channel_id=1, source_target_pairs={{0,8},{8,0},{16,24},{24,16},{1,9},{9,1},{17,25},{25,17},{2,10},{10... | collective-permute-start | bytes 2162696 | tf_op jit(solution)/shard_map/ppermute | solution.py:227
  526.3 56.5 %collective-permute-start.26 = (bf16[8,64,704]{2,1,0:T(8,128)(2,1)}, bf16[8,64,704]{2,1,0:T(8,128)(2,1)}, u32[]{:S(2)}, u32[]{:S(2)}) collective-permute-start(bf16[8,64,704]{2,1,0:T(8,128)(2,1)} %bitcast.55), channel_id=1, source_target_pairs={{0,16},{8,24},{16,0},{24,8},{1,17},{9,25},{17,1},{25,9},{2,18},{10... | collective-permute-start | bytes 2162696 | tf_op jit(solution)/shard_map/ppermute | solution.py:227
  582.8 128.6 %collective-permute-start.12 = (bf16[4,128,2048]{2,1,0:T(8,128)(2,1)}, bf16[4,128,2048]{2,1,0:T(8,128)(2,1)}, u32[]{:S(2)}, u32[]{:S(2)}) collective-permute-start(bf16[4,128,2048]{2,1,0:T(8,128)(2,1)} %dynamic-slice_bitcast_fusion), channel_id=1, source_target_pairs={{0,1},{1,0},{2,3},{3,2},{4,5},{5,4},{6,7},{7,6},{8,9},{9,8},{10,11... | collective-permute-start | bytes 6291464 | tf_op jit(solution)/shard_map/ppermute | solution.py:292
  617.3 89.8 %all-to-all-start.5 = ((bf16[8,192,704]{2,1,0:T(8,128)(2,1)}), bf16[8,192,704]{2,1,0:T(8,128)(2,1)S(1)}, u32[]{:S(2)}, u32[]{:S(2)}) async-start(bf16[8,192,704]{2,1,0:T(8,128)(2,1)} %pad_maximum_fusion.4), calls=%async_computation.8 | async-start | bytes 4718592 | tf_op jit(solution)/shard_map/all_to_all | solution.py:252
  631.0 65.4 %collective-permute-start.16 = (bf16[8,72,768]{2,1,0:T(8,128)(2,1)S(1)}, bf16[8,72,768]{2,1,0:T(8,128)(2,1)S(1)}, u32[]{:S(2)}, u32[]{:S(2)}) collective-permute-start(bf16[8,72,768]{2,1,0:T(8,128)(2,1)S(1)} %pad_maximum_fusion.8), channel_id=1, source_target_pairs={{0,8},{8,0},{16,24},{24,16},{1,9},{9,1},{17,25},{25,17},{2,10},{10... | collective-permute-start | bytes 2654216 | tf_op jit(solution)/shard_map/ppermute | solution.py:227
  632.7 63.7 %collective-permute-start.17 = (bf16[8,72,768]{2,1,0:T(8,128)(2,1)S(1)}, bf16[8,72,768]{2,1,0:T(8,128)(2,1)S(1)}, u32[]{:S(2)}, u32[]{:S(2)}) collective-permute-start(bf16[8,72,768]{2,1,0:T(8,128)(2,1)S(1)} %pad_maximum_fusion.9), channel_id=1, source_target_pairs={{0,16},{8,24},{16,0},{24,8},{1,17},{9,25},{17,1},{25,9},{2,18},{10... | collective-permute-start | bytes 2654216 | tf_op jit(solution)/shard_map/ppermute | solution.py:227
  637.8 58.6 %collective-permute-start.18 = (bf16[8,72,768]{2,1,0:T(8,128)(2,1)S(1)}, bf16[8,72,768]{2,1,0:T(8,128)(2,1)S(1)}, u32[]{:S(2)}, u32[]{:S(2)}) collective-permute-start(bf16[8,72,768]{2,1,0:T(8,128)(2,1)S(1)} %pad_maximum_fusion.10), channel_id=1, source_target_pairs={{0,24},{8,16},{16,8},{24,0},{1,25},{9,17},{17,9},{25,1},{2,26},{10... | collective-permute-start | bytes 2654216 | tf_op jit(solution)/shard_map/ppermute | solution.py:227
  707.1 56.7 %all-to-all-start.4 = ((bf16[8,72,1024]{2,1,0:T(8,128)(2,1)}), bf16[8,72,1024]{2,1,0:T(8,128)(2,1)}, u32[]{:S(2)}, u32[]{:S(2)}) async-start(bf16[8,72,1024]{2,1,0:T(8,128)(2,1)} %fusion.21), calls=%async_computation.7 | async-start | bytes 2359296 | tf_op jit(solution)/shard_map/all_to_all | solution.py:252
  715.8 62.4 %collective-permute-start.13 = (bf16[128,2048]{1,0:T(8,128)(2,1)}, bf16[128,2048]{1,0:T(8,128)(2,1)}, u32[]{:S(2)}, u32[]{:S(2)}) collective-permute-start(bf16[128,2048]{1,0:T(8,128)(2,1)} %get-tuple-element.65), channel_id=1, source_target_pairs={{0,2},{1,3},{2,4},{3,5},{4,6},{5,7},{6,0},{7,1},{8,10},{9,11},{10,... | collective-permute-start | bytes 1572872 | tf_op jit(solution)/shard_map/ppermute | solution.py:288
  717.6 60.6 %collective-permute-start.14 = (bf16[128,2048]{1,0:T(8,128)(2,1)}, bf16[128,2048]{1,0:T(8,128)(2,1)}, u32[]{:S(2)}, u32[]{:S(2)}) collective-permute-start(bf16[128,2048]{1,0:T(8,128)(2,1)} %get-tuple-element.64), channel_id=1, source_target_pairs={{0,4},{1,5},{2,6},{3,7},{4,0},{5,1},{6,2},{7,3},{8,12},{9,13},{10,... | collective-permute-start | bytes 1572872 | tf_op jit(solution)/shard_map/ppermute | solution.py:288
  720.0 58.2 %collective-permute-start.15 = (bf16[128,2048]{1,0:T(8,128)(2,1)}, bf16[128,2048]{1,0:T(8,128)(2,1)}, u32[]{:S(2)}, u32[]{:S(2)}) collective-permute-start(bf16[128,2048]{1,0:T(8,128)(2,1)} %get-tuple-element.63), channel_id=1, source_target_pairs={{0,6},{1,7},{2,0},{3,1},{4,2},{5,3},{6,4},{7,5},{8,14},{9,15},{10,... | collective-permute-start | bytes 1572872 | tf_op jit(solution)/shard_map/ppermute | solution.py:288
  (73 other events, 1236.5 us)
Sparse Core Ops, SparseCore 0:
  44.5 50.1 all-gather.4
  155.1 51.4 reduce-scatter.3
  210.5 79.9 all-gather.6
  292.0 44.9 all-gather.8
  450.0 47.8 reduce-scatter.5
  502.8 45.3 all-gather.10
  613.6 93.2 reduce-scatter.7

commit v2 on v1

--- a/solution.py
+++ b/solution.py
@@ -17,6 +17,9 @@
 MASKED = -1e30
 BF = jnp.bfloat16
 F32 = jnp.float32
+
+DP = "dp"
+SEQ = "seq"
 
 
 def rotary_rows(position):
@@ -129,9 +132,8 @@
             out_specs=[row(3 * hc), row(hc), pl.BlockSpec((8, bq), lambda i, f: (0, i))],
             scratch_shapes=[pltpu.VMEM((T, hc), BF), pltpu.VMEM((hc, T), BF), pltpu.VMEM((heads, T, bq), F32)]),
         out_shape=[jax.ShapeDtypeStruct((T, 3 * hc), BF), jax.ShapeDtypeStruct((T, hc), BF), jax.ShapeDtypeStruct((8, T), F32)],
-        compiler_params=pltpu.CompilerParams(dimension_semantics=("arbitrary",)),
         cost_estimate=pl.CostEstimate(flops=2 * T * T * hc * 2, bytes_accessed=T * hc * 24, transcendentals=T * T * heads // 2),
-        name="attend_fwd",
+        name="af",
     )(first, low8, *tables, proj)
 
 
@@ -204,9 +206,8 @@
             out_specs=[pl.BlockSpec((bq, 3 * hc), lambda i, f: (count - 1 - i, 0)), full(8, 3 * hc)],
             scratch_shapes=[pltpu.VMEM((T, hc), F32), pltpu.VMEM((T, hc), F32), pltpu.VMEM((hc, bq), F32)]),
         out_shape=[jax.ShapeDtypeStruct((T, 3 * hc), BF), jax.ShapeDtypeStruct((8, 3 * hc), F32)],
-        compiler_params=pltpu.CompilerParams(dimension_semantics=("arbitrary",)),
         cost_estimate=pl.CostEstimate(flops=5 * T * T * hc * 2, bytes_accessed=T * hc * 24, transcendentals=T * T * heads // 2),
-        name="attend_bwd",
+        name="ab",
     )(first, low8, *tables, qkv, ctx, lse, gc)
 
 
@@ -224,15 +225,15 @@
 
 
 def swap_dp(values, rel):
-    return lax.ppermute(values, "dp", [(d, d ^ rel) for d in range(lax.axis_size("dp"))])
+    return lax.ppermute(values, DP, [(d, d ^ rel) for d in range(lax.axis_size(DP))])
 
 
 def take(view):
-    return lax.all_to_all(view, "seq", split_axis=0, concat_axis=0, tiled=True)
+    return lax.all_to_all(view, SEQ, split_axis=0, concat_axis=0, tiled=True)
 
 
 def spread(mine):
-    return [mine] + [swap_dp(mine, rel) for rel in range(1, lax.axis_size("dp"))]
+    return [mine] + [swap_dp(mine, rel) for rel in range(1, lax.axis_size(DP))]
 
 
 def stack_rows(pieces, start, size):
@@ -249,7 +250,125 @@
 
 
 def send_back(summed):
-    return lax.all_to_all(summed, "seq", split_axis=0, concat_axis=0, tiled=True)
+    return lax.all_to_all(summed, SEQ, split_axis=0, concat_axis=0, tiled=True)
+
+
+def ffn_kernel(copies, rows, n_ref, u_ref, *refs):
+    pair, down, (act_ref, dx_ref) = refs[:copies], refs[copies : 2 * copies], refs[2 * copies :]
+    block = n_ref.shape[1] // copies
+    cols = pair[0].shape[2]
+
+    def gate_rows(m):
+        return pair[m][:, :rows, :].reshape(block, cols)
+
+    def up_rows(m):
+        return pair[m][:, rows:, :].reshape(block, cols)
+
+    gate = upward = grad = 0.0
+    for m in range(copies):
+        span = slice(m * block, (m + 1) * block)
+        gate = gate + nn(n_ref[:, span], gate_rows(m))
+        upward = upward + nn(n_ref[:, span], up_rows(m))
+        grad = grad + nn(u_ref[:, span], down[m][...].reshape(block, cols))
+    sig = jax.nn.sigmoid(gate)
+    silu = gate * sig
+    grad_gate = (grad * upward * sig * (1.0 + gate * (1.0 - sig))).astype(BF)
+    grad_up = (grad * silu).astype(BF)
+    act_ref[0] = grad_gate
+    act_ref[1] = grad_up
+    act_ref[2] = (silu * upward).astype(BF)
+    for m in range(copies):
+        part = nt(grad_gate, gate_rows(m)) + nt(grad_up, up_rows(m))
+        dx_ref[:, m * block : (m + 1) * block] = part.astype(BF)
+
+
+def whole(array):
+    zero = (0,) * array.ndim
+    return pl.BlockSpec(array.shape, lambda *i: zero, pipeline_mode=pl.Buffered(1))
+
+
+def ffn_both(normed, upstream, pair, down, rows, bq):
+    length, width = normed.shape
+    cols = down[0].shape[2]
+    row = pl.BlockSpec((bq, width), lambda i: (i, 0))
+    return pl.pallas_call(
+        functools.partial(ffn_kernel, len(pair), rows),
+        grid=(length // bq,),
+        in_specs=[row, row] + [whole(w) for w in pair + down],
+        out_specs=[pl.BlockSpec((3, bq, cols), lambda i: (0, i, 0)), row],
+        out_shape=[
+            jax.ShapeDtypeStruct((3, length, cols), BF),
+            jax.ShapeDtypeStruct((length, width), BF),
+        ],
+        cost_estimate=pl.CostEstimate(
+            flops=10 * length * width * cols,
+            bytes_accessed=6 * length * width + 6 * width * cols,
+            transcendentals=length * cols,
+        ),
+        name="ffn",
+    )(normed, upstream, *pair, *down)
+
+
+def down_kernel(copies, h_ref, *refs):
+    out_ref = refs[-1]
+    block = out_ref.shape[1] // copies
+    for m in range(copies):
+        weight = refs[m][...].reshape(block, h_ref.shape[2])
+        out_ref[:, m * block : (m + 1) * block] = nt(h_ref[0], weight).astype(BF)
+
+
+def down_rows(act, down, width, bq):
+    _, length, cols = act.shape
+    return pl.pallas_call(
+        functools.partial(down_kernel, len(down)),
+        grid=(length // bq,),
+        in_specs=[pl.BlockSpec((1, bq, cols), lambda i: (2, i, 0))] + [whole(w) for w in down],
+        out_specs=pl.BlockSpec((bq, width), lambda i: (i, 0)),
+        out_shape=jax.ShapeDtypeStruct((length, width), BF),
+        cost_estimate=pl.CostEstimate(
+            flops=2 * length * width * cols,
+            bytes_accessed=2 * length * width + 2 * width * cols,
+            transcendentals=0,
+        ),
+        name="down",
+    )(act, *down)
+
+
+def grad_kernel(n_ref, u_ref, act_ref, out_ref):
+    kind = pl.program_id(0)
+    groups, _, rows, cols = out_ref.shape
+
+    def emit(left):
+        out_ref[...] = nn(left[...].T, act_ref[0]).astype(BF).reshape(groups, 1, rows, cols)
+
+    @pl.when(kind < 2)
+    def _():
+        emit(n_ref)
+
+    @pl.when(kind == 2)
+    def _():
+        emit(u_ref)
+
+
+def ffn_grads(normed, upstream, act, m, copies, groups):
+    length, width = normed.shape
+    block = width // copies
+    rows = block // groups
+    cols = act.shape[2]
+    side = pl.BlockSpec((length, block), lambda k: (0, m), pipeline_mode=pl.Buffered(1))
+    return pl.pallas_call(
+        grad_kernel,
+        grid=(3,),
+        in_specs=[side, side, pl.BlockSpec((1, length, cols), lambda k: (k, 0, 0))],
+        out_specs=pl.BlockSpec((groups, 1, rows, cols), lambda k: (0, k, 0, 0)),
+        out_shape=jax.ShapeDtypeStruct((groups, 3, rows, cols), BF),
+        cost_estimate=pl.CostEstimate(
+            flops=6 * length * block * cols,
+            bytes_accessed=4 * length * block + 6 * length * cols + 6 * block * cols,
+            transcendentals=0,
+        ),
+        name="gw",
+    )(normed, upstream, act)
 
 
 def unit_of(values):
@@ -277,19 +396,19 @@
 
 
 def own_rows(partial):
-    return lax.psum_scatter(partial.astype(BF), "seq", scatter_dimension=0, tiled=True).astype(F32)
+    return lax.psum_scatter(partial.astype(BF), SEQ, scatter_dimension=0, tiled=True).astype(F32)
 
 
 def every(values):
-    return lax.all_gather(values, "seq", axis=0, tiled=True)
+    return lax.all_gather(values, SEQ, axis=0, tiled=True)
 
 
 def chip_shift(values, k, groups):
-    return lax.ppermute(values, "seq", [(s, (s + 2 * k) % groups) for s in range(groups)])
+    return lax.ppermute(values, SEQ, [(s, (s + 2 * k) % groups) for s in range(groups)])
 
 
 def core_swap(values, groups):
-    return lax.ppermute(values, "seq", [(s, s ^ 1) for s in range(groups)])
+    return lax.ppermute(values, SEQ, [(s, s ^ 1) for s in range(groups)])
 
 
 def own_rows_beside(partial, me, groups):
@@ -325,10 +444,10 @@
     down_weight,
 ):
     tokens, width = inputs.shape
-    groups = lax.axis_size("seq")
-    copies = lax.axis_size("dp")
-    me = lax.axis_index("seq")
-    mine = lax.axis_index("dp")
+    groups = lax.axis_size(SEQ)
+    copies = lax.axis_size(DP)
+    me = lax.axis_index(SEQ)
+    mine = lax.axis_index(DP)
     length = tokens * groups
     heads = HEADS // groups
     hc = heads * HD
@@ -338,6 +457,7 @@
 
     own = relate(inputs, mine, copies, 1)
     own_up = relate(upstream, mine, copies, 1)
+    up_all = every(own_up)
 
     def by_group(weight, parts=1):
         cols = weight.shape[1] // (parts * groups)
@@ -363,9 +483,7 @@
     x_all = every(own)
     pieces_qkv = spread(taken)
     weight_qkv = stack_rows(pieces_qkv, 0, rows)
-    taken, own_up = lax.optimization_barrier((take(by_group(out_weight)), own_up))
-    up_all = every(own_up)
-    weight_out = stack_rows(spread(taken), 0, rows)
+    weight_out = stack_rows(spread(take(by_group(out_weight))), 0, rows)
     spot = pieces_qkv[0][:, rows, 4 * rows + nbias : 4 * rows + nbias + 2 * tokens]
     positions = (
         spot[:, :tokens].astype(jnp.int32) * 256 + spot[:, tokens:].astype(jnp.int32)
@@ -386,9 +504,7 @@
     view_gu = jnp.concatenate([by_group(gate_weight), by_group(up_weight)], axis=1)
     view_gu, view_down, x_all = lax.optimization_barrier((view_gu, by_group(down_weight), x_all))
     pieces_gu = spread(take(view_gu))
-    weight_gate = stack_rows(pieces_gu, 0, rows)
-    weight_up = stack_rows(pieces_gu, rows, rows)
-    weight_down = stack_rows(spread(take(view_down)), 0, rows)
+    pieces_down = spread(take(view_down))
 
     unit_all, unused = unit_of(x_all.astype(F32))
     normed_one = (unit_all * gain_one + shift_one).astype(BF)
@@ -399,16 +515,9 @@
     unit_two, factor_two = unit_of(middle)
     normed_two = (unit_two * gain_two + shift_two).astype(BF)
     normed_two = every(normed_two)
-    gate = dot(normed_two, weight_gate, NN)
-    upward = dot(normed_two, weight_up, NN)
-    sig = jax.nn.sigmoid(gate)
-    silu = gate * sig
-    hidden = (silu * upward).astype(BF)
-    grad_hidden = dot(up_all, weight_down, NN)
-    grad_gate = (grad_hidden * upward * sig * (1.0 + gate * (1.0 - sig))).astype(BF)
-    grad_up = (grad_hidden * silu).astype(BF)
-    grad_normed_two = own_rows(dot(grad_gate, weight_gate, NT) + dot(grad_up, weight_up, NT))
-    down_part = dot(hidden, weight_down, NT).astype(BF)
+    act, dx = ffn_both(normed_two, up_all, pieces_gu, pieces_down, rows, bq)
+    grad_normed_two = own_rows(dx)
+    down_part = down_rows(act, pieces_down, width, bq)
     block = width // copies
 
     def by_owner(left, right):
@@ -417,13 +526,10 @@
             for m in range(copies)
         ]
 
-    grad_gate_weight = by_owner(normed_two, grad_gate)
-    grad_up_weight = by_owner(normed_two, grad_up)
-    grad_down_weight = by_owner(up_all, hidden)
-    sum_ffn = jnp.concatenate(
-        [reduce_dp(grad_gate_weight), reduce_dp(grad_up_weight), reduce_dp(grad_down_weight)],
-        axis=1,
-    )
+    grads = [None] * copies
+    for m in [*range(1, copies), 0]:
+        grads[m] = ffn_grads(normed_two, up_all, act, m, copies, groups)
+    sum_ffn = reduce_dp(grads).reshape(groups, 3 * rows, -1)
     sum_ffn = send_back(sum_ffn).transpose(1, 0, 2)
 
     grad_middle = own_up.astype(F32) + norm_back(grad_normed_two, unit_two, factor_two, gain_two)
@@ -519,25 +625,25 @@
 
 
 def solution(mesh):
-    both = ("dp", "seq")
+    both = (DP, SEQ)
     in_specs = (
-        P("dp", "seq", None),
-        P(both),
-        P(both),
-        P(both, None),
-        P(both),
-        P(both, None),
-        P(both),
-        P(both),
-        P(both, None),
-        P(both, None),
-        P(both, None),
-        P("dp", "seq"),
-        P("dp", "seq", None),
+        P(DP, SEQ, None),
+        P(both),
+        P(both),
+        P(both, None),
+        P(both),
+        P(both, None),
+        P(both),
+        P(both),
+        P(both, None),
+        P(both, None),
+        P(both, None),
+        P(DP, SEQ),
+        P(DP, SEQ, None),
     )
     out_specs = (
-        P("dp", "seq", None),
-        P("dp", "seq", None),
+        P(DP, SEQ, None),
+        P(DP, SEQ, None),
         P(both),
         P(both),
         P(both, None),

time: 802 us -> 762 us (0.950)
  matrix products: 97.3 us -> 32.8 us
  Pallas kernels: 23.3 us -> 81.8 us
  blocking collectives: 40 us -> 70 us
  local copies, waits for them, and re-layouts: 96 us -> 76.9 us
  starting transfers between devices: 66.4 us -> 52.3 us
  waiting for transfers between devices: 388 us -> 374 us
  other arithmetic: 63.4 us -> 53.6 us
    dot_general x30 -> x12, matrix products: 97.3 us -> 32.8 us  [dot(): lax.dot_general(left, right, (dims, ((), ())), preferred_element_type=F32)]
    pallas_call x0 -> x6, Pallas kernels: none -> 58.3 us  [the longest x4 27.2 us: ffn_grads(): pl.pallas_call(grad_kernel, grid=(3,), in_specs=[side, side, pl.BlockSpec...]
    all_to_all x5, waiting for transfers between devices: 112 us -> 69.3 us  [the longest x3 64.8 us: take(): return lax.all_to_all(view, SEQ, split_axis=0, concat_axis=0, tiled=True)]
    all_to_all x1, blocking collectives: 40 us -> 70 us  [take(): return lax.all_to_all(view, SEQ, split_axis=0, concat_axis=0, tiled=True)]
    ppermute x31 -> x25, waiting for transfers between devices: 177 us -> 200 us  [the longest x21 171 us: swap_dp(): lax.ppermute(values, DP, [(d, d ^ rel) for d in range(lax.axis_size(DP))])]
    convert_element_type x12 -> x0, local copies, waits for them, and re-layouts: 20.3 us -> none  [the longest x9 13.8 us: by_owner(): dot(left[:, m * block:(m + 1) * block], right, TN).astype(BF)]
    concatenate x3 -> x1, local copies, waits for them, and re-layouts: 17 us -> 3.38 us  [stack_rows(): jnp.concatenate([p[:, start:start + size] for p in pieces], axis=0)]
    ppermute x31 -> x25, starting transfers between devices: 43.2 us -> 29.9 us  [the longest x21 24.8 us: swap_dp(): lax.ppermute(values, DP, [(d, d ^ rel) for d in range(lax.axis_size(DP))])]
  transfers between devices with their start and end apart: 43 -> 37, of which waited for: 17 -> 20; matrix products, arithmetic and copies ran while one was open for 25% -> 17% of each run, Pallas kernels for 2% -> 6%
where the time goes in v2:
time: 762 us; the launch traced here: 757 us
  waiting for transfers between devices  374 us (49%)
  Pallas kernels  81.8 us (11%)
  local copies, waits for them, and re-layouts  76.9 us (10%)
  blocking collectives  70 us (9%)
  other arithmetic  53.6 us (7%)
  starting transfers between devices  52.3 us (7%)
  matrix products  32.8 us (4%)
  between operations  15.6 us (2%)
    ppermute x21, waiting for transfers between devices, swap_dp(): lax.ppermute(values, DP, [(d, d ^ rel) for d in range(lax.axis_size(DP))])  171 us
    reduce_scatter x3, waiting for transfers between devices, own_rows(): lax.psum_scatter(partial.astype(BF), SEQ, scatter_dimension=0, tiled=True)  99.5 us
    all_to_all x1, blocking collectives, take(): return lax.all_to_all(view, SEQ, split_axis=0, concat_axis=0, tiled=True)  70 us
    all_to_all x3, waiting for transfers between devices, take(): return lax.all_to_all(view, SEQ, split_axis=0, concat_axis=0, tiled=True)  64.8 us
    dot_general x12, matrix products, dot(): lax.dot_general(left, right, (dims, ((), ())), preferred_element_type=F32)  32.8 us
    ppermute x3, waiting for transfers between devices, chip_shift(): lax.ppermute(values, SEQ, [(s, (s + 2 * k) % groups) for s in range(group...  30 us
    pallas_call x4, Pallas kernels, ffn_grads(): pl.pallas_call(grad_kernel, grid=(3,), in_specs=[side, side, pl.BlockSpec...  27.2 us
    ppermute x21, starting transfers between devices, swap_dp(): lax.ppermute(values, DP, [(d, d ^ rel) for d in range(lax.axis_size(DP))])  24.8 us
  transfers between devices with their start and end apart: 37, of which 20 were waited for; matrix products, arithmetic and copies ran while one was open for 17% of the time, Pallas kernels for 6%

profile of v2, /device:TPU:0, one launch (start us, length us, event | category | flops | bytes accessed | tf_op | source)
XLA Modules:
  0.0 756.5 jit_solution(15984666927474378123)
XLA Ops:
  22.5 21.8 %all-to-all-done = bf16[8,72,768]{2,1,0:T(8,128)(2,1)S(1)} async-done(((bf16[8,72,768]{2,1,0:T(8,128)(2,1)}), bf16[8,72,768]{2,1,0:T(8,128)(2,1)S(1)}, u32[]{:S(2)}, u32[]{:S(2)}) %all-to-all-start) | async-done | bytes 884768 | tf_op jit(solution)/shard_map/all_to_all | solution.py:232
  55.9 8.4 %all-to-all-done.1 = bf16[8,64,256]{2,1,0:T(8,128)(2,1)S(1)} async-done(((bf16[8,64,256]{2,1,0:T(8,128)(2,1)}), bf16[8,64,256]{2,1,0:T(8,128)(2,1)S(1)}, u32[]{:S(2)}, u32[]{:S(2)}) %all-to-all-start.1) | async-done | bytes 262176 | tf_op jit(solution)/shard_map/all_to_all | solution.py:232
  91.4 12.9 %collective-permute-done.2 = bf16[8,72,768]{2,0,1:T(8,128)(2,1)} collective-permute-done((bf16[8,72,768]{2,0,1:T(8,128)(2,1)}, bf16[8,72,768]{2,0,1:T(8,128)(2,1)}, u32[]{:S(2)}, u32[]{:S(2)}) %collective-permute-start.2) | collective-permute-done | bytes 884768 | tf_op jit(solution)/shard_map/ppermute | solution.py:228
  105.1 17.2 %collective-permute-done.1 = bf16[8,72,768]{2,0,1:T(8,128)(2,1)} collective-permute-done((bf16[8,72,768]{2,0,1:T(8,128)(2,1)}, bf16[8,72,768]{2,0,1:T(8,128)(2,1)}, u32[]{:S(2)}, u32[]{:S(2)}) %collective-permute-start.1) | collective-permute-done | bytes 884768 | tf_op jit(solution)/shard_map/ppermute | solution.py:228
  146.2 9.5 %af.1 = (bf16[1024,768]{1,0:T(8,128)(2,1)}, bf16[1024,256]{1,0:T(8,128)(2,1)}, f32[8,1024]{1,0:T(8,128)}) custom-call(s32[4]{0:T(128)} %and_select_fusion.2.first_ref, s32[8,1024]{1,0:T(8,128)} %broadcast_in_dim.28.low_ref, f32[1024,128]{1,0:T(8,128)} %get-tuple-element.113.cos_ref, f32[1024,128]{1,0:T(8,128)} %get-tuple-element.112.s1_ref, ...), custom_call_target="tpu_custom_call" | custom-call | flops 1073741824 | bytes 6291456 | tf_op jit(solution)/shard_map/af/pallas_call | solution.py:127
  162.5 49.3 %reduce-scatter.4.cloned.1.call-done = bf16[128,2048]{1,0:T(8,128)(2,1)} async-done(((bf16[1024,2048]{1,0:T(8,128)(2,1)}), bf16[128,2048]{1,0:T(8,128)(2,1)}) %reduce-scatter.4.cloned.1.call-update) | async-done | bytes 524304 | tf_op jit(solution)/shard_map/reduce_scatter | solution.py:399
  217.5 70.0 %all_to_all.30 = bf16[8,128,704]{1,2,0:T(8,128)(2,1)S(1)} all-to-all(bf16[8,128,704]{1,2,0:T(8,128)(2,1)} %copy.110), channel_id=1, replica_groups=mesh['dp'=4,'seq'=8] {'seq'}, dimensions={0} | all-to-all | bytes 2883584 | tf_op jit(solution)/shard_map/all_to_all | solution.py:232
  294.7 34.6 %all-to-all-done.3.refs_4_.refs_0_ = bf16[8,64,704]{2,1,0:T(8,128)(2,1)S(1)} async-done(((bf16[8,64,704]{2,1,0:T(8,128)(2,1)}), bf16[8,64,704]{2,1,0:T(8,128)(2,1)S(1)}, u32[]{:S(2)}, u32[]{:S(2)}) %all-to-all-start.3) | async-done | bytes 720928 | tf_op jit(solution)/shard_map/all_to_all | solution.py:232
  337.0 21.2 %collective-permute-done.7 = bf16[8,128,704]{1,2,0:T(8,128)(2,1)} collective-permute-done((bf16[8,128,704]{1,2,0:T(8,128)(2,1)S(1)}, bf16[8,128,704]{1,2,0:T(8,128)(2,1)}, u32[]{:S(2)}, u32[]{:S(2)}) %collective-permute-start.7) | collective-permute-done | bytes 1441824 | tf_op jit(solution)/shard_map/ppermute | solution.py:228
  363.3 6.6 collective-permute-done.9.refs_5_.refs_1_
  369.9 21.3 %collective-permute-done.10.refs_6_.refs_2_ = bf16[8,64,704]{2,1,0:T(8,128)(2,1)} collective-permute-done((bf16[8,64,704]{2,1,0:T(8,128)(2,1)S(1)}, bf16[8,64,704]{2,1,0:T(8,128)(2,1)}, u32[]{:S(2)}, u32[]{:S(2)}) %collective-permute-start.10) | collective-permute-done | bytes 720928 | tf_op jit(solution)/shard_map/ppermute | solution.py:228
  391.2 23.7 %ffn.1 = (bf16[3,1024,704]{2,1,0:T(8,128)(2,1)}, bf16[1024,2048]{1,0:T(8,128)(2,1)}) custom-call(bf16[1024,2048]{1,0:T(8,128)(2,1)} %all-gather.7.cloned.1.call-done.n_ref, bf16[1024,2048]{1,0:T(8,128)(2,1)} %all-gather.9.cloned.1.call-done.u_ref, bf16[8,128,704]{2,1,0:T(8,128)(2,1)} %copy.111.refs_0_, bf16[8,128,704]{2,1,0:T(8,128)(2,1)} %copy.112.refs_1_, ...), custom_call_target="tpu_custom_call" | custom-call | flops 14763950080 | bytes 21233664 | tf_op jit(solution)/shard_map/ffn/pallas_call | solution.py:294
  415.0 50.2 %reduce-scatter.6.cloned.1.call-done = bf16[128,2048]{1,0:T(8,128)(2,1)} async-done(((bf16[1024,2048]{1,0:T(8,128)(2,1)}), bf16[128,2048]{1,0:T(8,128)(2,1)}) %reduce-scatter.6.cloned.1.call-update) | async-done | bytes 524304 | tf_op jit(solution)/shard_map/reduce_scatter | solution.py:399
  470.1 6.9 gw.7
  479.4 6.7 gw.6
  486.7 6.8 gw.5
  494.0 7.4 down.1
  504.7 6.8 gw.4
  519.7 14.0 %ab.1 = (bf16[1024,768]{1,0:T(8,128)(2,1)}, f32[8,768]{1,0:T(8,128)}) custom-call(s32[4]{0:T(128)} %and_select_fusion.2.first_ref, s32[8,1024]{1,0:T(8,128)} %broadcast_in_dim.28.low_ref, f32[1024,128]{1,0:T(8,128)} %get-tuple-element.113.cos_ref, f32[1024,128]{1,0:T(8,128)} %get-tuple-element.112.s1_ref, f32[1024,128]{1,0:T(8,128)} %get-tuple-element.111.s2_ref, ...), custom_call_target="tpu_custom_call" | custom-call | flops 2684354560 | bytes 6291456 | tf_op jit(solution)/shard_map/ab/pallas_call | solution.py:201
  533.7 9.1 %fusion.6 = (bf16[2048]{0:T(1024)(128)(2,1)S(1)}, bf16[1024,2048]{1,0:T(8,128)(2,1)}) fusion(bf16[1024,2048]{1,0:T(8,128)(2,1)} %all-gather.5.cloned.1.call-done, f32[1024]{0:T(1024)S(1)} %add_rsqrt_fusion, f32[1024]{0:T(1024)S(1)} %broadcast_multiply_fusion.1, bf16[1024,768]{1,0:T(8,128)(2,1)} %get-tuple-element.49, bf16[2048,768]{1,0:T(8,128)(2,1)} %bitcast.136), kind=kOutput, calls=%fused_computation.8 | convolution fusion | flops 3235903488 | bytes 13119488 | tf_op jit(solution)/shard_map/dot_general | solution.py:390
  542.9 37.0 %collective-permute-done.23 = bf16[8,3,64,704]{3,2,1,0:T(8,128)(2,1)} collective-permute-done((bf16[8,3,64,704]{3,2,1,0:T(8,128)(2,1)}, bf16[8,3,64,704]{3,2,1,0:T(8,128)(2,1)}, u32[]{:S(2)}, u32[]{:S(2)}) %collective-permute-start.23) | collective-permute-done | bytes 2162720 | tf_op jit(solution)/shard_map/ppermute | solution.py:228
  615.1 38.6 %collective-permute-done.20 = bf16[8,64,256]{2,1,0:T(8,128)(2,1)S(1)} collective-permute-done((bf16[8,64,256]{2,1,0:T(8,128)(2,1)S(1)}, bf16[8,64,256]{2,1,0:T(8,128)(2,1)S(1)}, u32[]{:S(2)}, u32[]{:S(2)}) %collective-permute-start.20) | collective-permute-done | bytes 262176 | tf_op jit(solution)/shard_map/ppermute | solution.py:228
  654.7 7.2 collective-permute-done.19
  713.9 30.0 %collective-permute-done.14 = bf16[128,2048]{1,0:T(8,128)(2,1)} collective-permute-done((bf16[128,2048]{1,0:T(8,128)(2,1)}, bf16[128,2048]{1,0:T(8,128)(2,1)}, u32[]{:S(2)}, u32[]{:S(2)}) %collective-permute-start.14) | collective-permute-done | bytes 524320 | tf_op jit(solution)/shard_map/ppermute | solution.py:407
  (316 shorter events, 223.6 us)
Async XLA Ops:
  21.3 112.7 %all-gather.5.cloned.1.call-start = ((), (), s32[]{:S(2)}) async-start(), calls=%async_computation.9 | async-start | bytes 4718592 | tf_op jit(solution)/shard_map/all_gather | solution.py:403
  49.6 162.3 %reduce-scatter.4.cloned.1.call-start = ((), (), s32[]{:S(2)}) async-start(), calls=%async_computation.10 | async-start | bytes 4718592 | tf_op jit(solution)/shard_map/reduce_scatter | solution.py:399
  160.1 203.2 %all-gather.9.cloned.1.call-start = ((), (), s32[]{:S(2)}) async-start(), calls=%async_computation.12 | async-start | bytes 4718592 | tf_op jit(solution)/shard_map/all_gather | solution.py:403
  162.3 228.8 %all-gather.7.cloned.1.call-start = ((), (), s32[]{:S(2)}) async-start(), calls=%async_computation.11 | async-start | bytes 4718592 | tf_op jit(solution)/shard_map/all_gather | solution.py:403
  287.5 43.6 %collective-permute-start.6 = (bf16[8,128,704]{1,2,0:T(8,128)(2,1)S(1)}, bf16[8,128,704]{1,2,0:T(8,128)(2,1)}, u32[]{:S(2)}, u32[]{:S(2)}) collective-permute-start(bf16[8,128,704]{1,2,0:T(8,128)(2,1)S(1)} %all_to_all.30), channel_id=1, source_target_pairs={{0,8},{8,0},{16,24},{24,16},{1,9},{9,1},{17,25},{25,17},{2,10},{10... | collective-permute-start | bytes 4325384 | tf_op jit(solution)/shard_map/ppermute | solution.py:228
  289.0 40.3 %all-to-all-start.3 = ((bf16[8,64,704]{2,1,0:T(8,128)(2,1)}), bf16[8,64,704]{2,1,0:T(8,128)(2,1)S(1)}, u32[]{:S(2)}, u32[]{:S(2)}) async-start(bf16[8,64,704]{2,1,0:T(8,128)(2,1)} %bitcast.138), calls=%async_computation.4 | async-start | bytes 1572864 | tf_op jit(solution)/shard_map/all_to_all | solution.py:232
  292.5 172.6 %reduce-scatter.6.cloned.1.call-start = ((), (), s32[]{:S(2)}) async-start(), calls=%async_computation.13 | async-start | bytes 4718592 | tf_op jit(solution)/shard_map/reduce_scatter | solution.py:399
  292.6 65.5 %collective-permute-start.7 = (bf16[8,128,704]{1,2,0:T(8,128)(2,1)S(1)}, bf16[8,128,704]{1,2,0:T(8,128)(2,1)}, u32[]{:S(2)}, u32[]{:S(2)}) collective-permute-start(bf16[8,128,704]{1,2,0:T(8,128)(2,1)S(1)} %all_to_all.30), channel_id=1, source_target_pairs={{0,16},{8,24},{16,0},{24,8},{1,17},{9,25},{17,1},{25,9},{2,18},{10... | collective-permute-start | bytes 4325384 | tf_op jit(solution)/shard_map/ppermute | solution.py:228
  294.1 66.6 %collective-permute-start.8 = (bf16[8,128,704]{1,2,0:T(8,128)(2,1)S(1)}, bf16[8,128,704]{1,2,0:T(8,128)(2,1)}, u32[]{:S(2)}, u32[]{:S(2)}) collective-permute-start(bf16[8,128,704]{1,2,0:T(8,128)(2,1)S(1)} %all_to_all.30), channel_id=1, source_target_pairs={{0,24},{8,16},{16,8},{24,0},{1,25},{9,17},{17,9},{25,1},{2,26},{10... | collective-permute-start | bytes 4325384 | tf_op jit(solution)/shard_map/ppermute | solution.py:228
  329.3 40.6 %collective-permute-start.9 = (bf16[8,64,704]{2,1,0:T(8,128)(2,1)S(1)}, bf16[8,64,704]{2,1,0:T(8,128)(2,1)}, u32[]{:S(2)}, u32[]{:S(2)}) collective-permute-start(bf16[8,64,704]{2,1,0:T(8,128)(2,1)S(1)} %all-to-all-done.3.refs_4_.refs_0_), channel_id=1, source_target_pairs={{0,8},{8,0},{16,24},{24,16},{1,9},{9,1},{17,25},{25,17},{2,10},{10... | collective-permute-start | bytes 2162696 | tf_op jit(solution)/shard_map/ppermute | solution.py:228
  329.7 61.5 %collective-permute-start.10 = (bf16[8,64,704]{2,1,0:T(8,128)(2,1)S(1)}, bf16[8,64,704]{2,1,0:T(8,128)(2,1)}, u32[]{:S(2)}, u32[]{:S(2)}) collective-permute-start(bf16[8,64,704]{2,1,0:T(8,128)(2,1)S(1)} %all-to-all-done.3.refs_4_.refs_0_), channel_id=1, source_target_pairs={{0,16},{8,24},{16,0},{24,8},{1,17},{9,25},{17,1},{25,9},{2,18},{10... | collective-permute-start | bytes 2162696 | tf_op jit(solution)/shard_map/ppermute | solution.py:228
  331.1 60.0 %collective-permute-start.11 = (bf16[8,64,704]{2,1,0:T(8,128)(2,1)S(1)}, bf16[8,64,704]{2,1,0:T(8,128)(2,1)}, u32[]{:S(2)}, u32[]{:S(2)}) collective-permute-start(bf16[8,64,704]{2,1,0:T(8,128)(2,1)S(1)} %all-to-all-done.3.refs_4_.refs_0_), channel_id=1, source_target_pairs={{0,24},{8,16},{16,8},{24,0},{1,25},{9,17},{17,9},{25,1},{2,26},{10... | collective-permute-start | bytes 2162696 | tf_op jit(solution)/shard_map/ppermute | solution.py:228
  414.9 100.6 %all-gather.11.cloned.1.call-start = ((), (), s32[]{:S(2)}) async-start(), calls=%async_computation.14 | async-start | bytes 4718592 | tf_op jit(solution)/shard_map/all_gather | solution.py:403
  470.0 242.4 %reduce-scatter.8.cloned.1.call-start = ((), (), s32[]{:S(2)}) async-start(), calls=%async_computation.15 | async-start | bytes 4718592 | tf_op jit(solution)/shard_map/reduce_scatter | solution.py:399
  477.0 65.9 %collective-permute-start.24 = (bf16[8,3,64,704]{3,2,1,0:T(8,128)(2,1)}, bf16[8,3,64,704]{3,2,1,0:T(8,128)(2,1)}, u32[]{:S(2)}, u32[]{:S(2)}) collective-permute-start(bf16[8,3,64,704]{3,2,1,0:T(8,128)(2,1)} %gw.7), channel_id=1, source_target_pairs={{0,24},{8,16},{16,8},{24,0},{1,25},{9,17},{17,9},{25,1},{2,26},{10... | collective-permute-start | bytes 6488072 | tf_op jit(solution)/shard_map/ppermute | solution.py:228
  486.1 93.8 %collective-permute-start.23 = (bf16[8,3,64,704]{3,2,1,0:T(8,128)(2,1)}, bf16[8,3,64,704]{3,2,1,0:T(8,128)(2,1)}, u32[]{:S(2)}, u32[]{:S(2)}) collective-permute-start(bf16[8,3,64,704]{3,2,1,0:T(8,128)(2,1)} %gw.6), channel_id=1, source_target_pairs={{0,16},{8,24},{16,0},{24,8},{1,17},{9,25},{17,1},{25,9},{2,18},{10... | collective-permute-start | bytes 6488072 | tf_op jit(solution)/shard_map/ppermute | solution.py:228
  493.5 86.5 %collective-permute-start.22 = (bf16[8,3,64,704]{3,2,1,0:T(8,128)(2,1)}, bf16[8,3,64,704]{3,2,1,0:T(8,128)(2,1)}, u32[]{:S(2)}, u32[]{:S(2)}) collective-permute-start(bf16[8,3,64,704]{3,2,1,0:T(8,128)(2,1)} %gw.5), channel_id=1, source_target_pairs={{0,8},{8,0},{16,24},{24,16},{1,9},{9,1},{17,25},{25,17},{2,10},{10... | collective-permute-start | bytes 6488072 | tf_op jit(solution)/shard_map/ppermute | solution.py:228
  504.7 164.7 %collective-permute-start.12 = (bf16[4,128,2048]{2,1,0:T(8,128)(2,1)}, bf16[4,128,2048]{2,1,0:T(8,128)(2,1)}, u32[]{:S(2)}, u32[]{:S(2)}) collective-permute-start(bf16[4,128,2048]{2,1,0:T(8,128)(2,1)} %dynamic-slice_bitcast_fusion), channel_id=1, source_target_pairs={{0,1},{1,0},{2,3},{3,2},{4,5},{5,4},{6,7},{7,6},{8,9},{9,8},{10,11... | collective-permute-start | bytes 6291464 | tf_op jit(solution)/shard_map/ppermute | solution.py:411
  586.1 78.6 %all-to-all-start.5 = ((bf16[8,192,704]{2,1,0:T(8,128)(2,1)}), bf16[8,192,704]{2,1,0:T(8,128)(2,1)S(1)}, u32[]{:S(2)}, u32[]{:S(2)}) async-start(bf16[8,192,704]{2,1,0:T(8,128)(2,1)} %bitcast.129), calls=%async_computation.8 | async-start | bytes 4718592 | tf_op jit(solution)/shard_map/all_to_all | solution.py:253
  606.4 56.6 %collective-permute-start.18 = (bf16[8,72,768]{2,1,0:T(8,128)(2,1)S(1)}, bf16[8,72,768]{2,1,0:T(8,128)(2,1)S(1)}, u32[]{:S(2)}, u32[]{:S(2)}) collective-permute-start(bf16[8,72,768]{2,1,0:T(8,128)(2,1)S(1)} %pad_maximum_fusion.6), channel_id=1, source_target_pairs={{0,24},{8,16},{16,8},{24,0},{1,25},{9,17},{17,9},{25,1},{2,26},{10... | collective-permute-start | bytes 2654216 | tf_op jit(solution)/shard_map/ppermute | solution.py:228
  608.2 54.9 %collective-permute-start.17 = (bf16[8,72,768]{2,1,0:T(8,128)(2,1)S(1)}, bf16[8,72,768]{2,1,0:T(8,128)(2,1)S(1)}, u32[]{:S(2)}, u32[]{:S(2)}) collective-permute-start(bf16[8,72,768]{2,1,0:T(8,128)(2,1)S(1)} %pad_maximum_fusion.5), channel_id=1, source_target_pairs={{0,16},{8,24},{16,0},{24,8},{1,17},{9,25},{17,1},{25,9},{2,18},{10... | collective-permute-start | bytes 2654216 | tf_op jit(solution)/shard_map/ppermute | solution.py:228
  610.8 52.2 %collective-permute-start.16 = (bf16[8,72,768]{2,1,0:T(8,128)(2,1)S(1)}, bf16[8,72,768]{2,1,0:T(8,128)(2,1)S(1)}, u32[]{:S(2)}, u32[]{:S(2)}) collective-permute-start(bf16[8,72,768]{2,1,0:T(8,128)(2,1)S(1)} %pad_maximum_fusion.4), channel_id=1, source_target_pairs={{0,8},{8,0},{16,24},{24,16},{1,9},{9,1},{17,25},{25,17},{2,10},{10... | collective-permute-start | bytes 2654216 | tf_op jit(solution)/shard_map/ppermute | solution.py:228
  677.6 66.3 %collective-permute-start.14 = (bf16[128,2048]{1,0:T(8,128)(2,1)}, bf16[128,2048]{1,0:T(8,128)(2,1)}, u32[]{:S(2)}, u32[]{:S(2)}) collective-permute-start(bf16[128,2048]{1,0:T(8,128)(2,1)} %get-tuple-element.61), channel_id=1, source_target_pairs={{0,4},{1,5},{2,6},{3,7},{4,0},{5,1},{6,2},{7,3},{8,12},{9,13},{10,... | collective-permute-start | bytes 1572872 | tf_op jit(solution)/shard_map/ppermute | solution.py:407
  677.6 66.3 %collective-permute-start.13 = (bf16[128,2048]{1,0:T(8,128)(2,1)}, bf16[128,2048]{1,0:T(8,128)(2,1)}, u32[]{:S(2)}, u32[]{:S(2)}) collective-permute-start(bf16[128,2048]{1,0:T(8,128)(2,1)} %get-tuple-element.62), channel_id=1, source_target_pairs={{0,2},{1,3},{2,4},{3,5},{4,6},{5,7},{6,0},{7,1},{8,10},{9,11},{10,... | collective-permute-start | bytes 1572872 | tf_op jit(solution)/shard_map/ppermute | solution.py:407
  (55 other events, 1501.9 us)
Sparse Core Ops, SparseCore 0:
  44.5 50.3 all-gather.4
  160.2 51.5 reduce-scatter.3
  213.4 76.1 all-gather.8
  291.7 57.1 all-gather.6
  415.0 50.0 reduce-scatter.5
  470.1 45.3 all-gather.10
  543.0 50.3 reduce-scatter.7

commit v3 on v2

--- a/solution.py
+++ b/solution.py
@@ -57,20 +57,31 @@
     return jnp.where((key <= query) & (key >= low_row), 0.0, MASKED)
 
 
-def fwd_kernel(heads, bq, first_ref, low_ref, cos_ref, s1_ref, s2_ref, proj_ref,
-               qkv_ref, ctx_ref, lse_ref, k_s, vt_s, st_s):
+def fwd_kernel(heads, bq, rows, first_ref, low_ref, cos_ref, s1_ref, s2_ref, x_ref, gain_ref, shift_ref, add_ref, *refs):
+    weights = refs[:-7]
+    norm_ref, qkv_ref, ctx_ref, lse_ref, k_s, vt_s, st_s = refs[-7:]
     i = pl.program_id(0)
     hc = heads * HD
+    x = x_ref[...].astype(F32)
+    center = x - jnp.mean(x, axis=-1, keepdims=True)
+    factor = lax.rsqrt(jnp.mean(center * center, axis=-1, keepdims=True) + EPSILON)
+    normed = (center * factor * gain_ref[...] + shift_ref[...]).astype(BF)
+    norm_ref[...] = normed
+    proj = add_ref[...]
+    size = x_ref.shape[1] // len(weights)
+    for n, weight in enumerate(weights):
+        part = weight[:, :rows, :].reshape(size, 3 * hc)
+        proj = proj + nn(normed[:, n * size:(n + 1) * size], part)
     c, s1, s2 = cos_ref[...], s1_ref[...], s2_ref[...]
     parts = []
     for base in (0, hc):
         for t in range(hc // LANES):
-            x = proj_ref[:, base + t * LANES: base + (t + 1) * LANES]
+            x = proj[:, base + t * LANES: base + (t + 1) * LANES]
             parts.append(turn(x, c, s1, s2).astype(BF))
     n = hc // LANES
     q = jnp.concatenate(parts[:n], axis=1) if n > 1 else parts[0]
     k = jnp.concatenate(parts[n:], axis=1) if n > 1 else parts[n]
-    v32 = proj_ref[:, 2 * hc:]
+    v32 = proj[:, 2 * hc:]
     v = v32.astype(BF)
     qkv_ref[:, :hc] = q
     qkv_ref[:, hc:2 * hc] = k
@@ -121,20 +132,23 @@
     lse_ref[...] = jnp.concatenate(lses + pad, axis=0)
 
 
-def attend_fwd(proj, tables, low8, first, heads, bq):
-    T = proj.shape[0]; hc = heads * HD
+def attend_fwd(x, gain, shift, add, weights, rows, tables, low8, first, heads, bq):
+    T, width = x.shape; hc = heads * HD
     row = lambda w: pl.BlockSpec((bq, w), lambda i, f: (i, 0))
     return pl.pallas_call(
-        functools.partial(fwd_kernel, heads, bq),
+        functools.partial(fwd_kernel, heads, bq, rows),
         grid_spec=pltpu.PrefetchScalarGridSpec(
             num_scalar_prefetch=1, grid=(T // bq,),
-            in_specs=[pl.BlockSpec((8, bq), lambda i, f: (0, i)), row(LANES), row(LANES), row(LANES), row(3 * hc)],
-            out_specs=[row(3 * hc), row(hc), pl.BlockSpec((8, bq), lambda i, f: (0, i))],
+            in_specs=[pl.BlockSpec((8, bq), lambda i, f: (0, i)), row(LANES), row(LANES), row(LANES), row(width)]
+            + [whole(w) for w in (gain, shift, add, *weights)],
+            out_specs=[row(width), row(3 * hc), row(hc), pl.BlockSpec((8, bq), lambda i, f: (0, i))],
             scratch_shapes=[pltpu.VMEM((T, hc), BF), pltpu.VMEM((hc, T), BF), pltpu.VMEM((heads, T, bq), F32)]),
-        out_shape=[jax.ShapeDtypeStruct((T, 3 * hc), BF), jax.ShapeDtypeStruct((T, hc), BF), jax.ShapeDtypeStruct((8, T), F32)],
-        cost_estimate=pl.CostEstimate(flops=2 * T * T * hc * 2, bytes_accessed=T * hc * 24, transcendentals=T * T * heads // 2),
+        out_shape=[jax.ShapeDtypeStruct((T, width), BF), jax.ShapeDtypeStruct((T, 3 * hc), BF),
+                   jax.ShapeDtypeStruct((T, hc), BF), jax.ShapeDtypeStruct((8, T), F32)],
+        cost_estimate=pl.CostEstimate(flops=4 * T * T * hc + 6 * T * width * hc, bytes_accessed=T * hc * 24 + 4 * T * width,
+                                      transcendentals=T * T * heads // 2),
         name="af",
-    )(first, low8, *tables, proj)
+    )(first, low8, *tables, x, gain, shift, add, *weights)
 
 
 def bwd_kernel(heads, bq, count, first_ref, low_ref, cos_ref, s1_ref, s2_ref, qkv_ref, ctx_ref, lse_ref, gc_ref,
@@ -234,6 +248,17 @@
 
 def spread(mine):
     return [mine] + [swap_dp(mine, rel) for rel in range(1, lax.axis_size(DP))]
+
+
+def spread_halves(mine):
+    half = mine.shape[0] // 2
+    count = lax.axis_size(DP)
+    bits = [1 << n for n in range(count.bit_length() - 1)]
+    low, high = {0: mine[:half]}, {0: mine[half:]}
+    for one, other in zip(bits, bits[::-1]):
+        low.update({rel ^ one: swap_dp(piece, one) for rel, piece in list(low.items())})
+        high.update({rel ^ other: swap_dp(piece, other) for rel, piece in list(high.items())})
+    return [(low[rel], high[rel]) for rel in range(count)]
 
 
 def stack_rows(pieces, start, size):
@@ -309,20 +334,22 @@
     )(normed, upstream, *pair, *down)
 
 
-def down_kernel(copies, h_ref, *refs):
-    out_ref = refs[-1]
-    block = out_ref.shape[1] // copies
-    for m in range(copies):
-        weight = refs[m][...].reshape(block, h_ref.shape[2])
-        out_ref[:, m * block : (m + 1) * block] = nt(h_ref[0], weight).astype(BF)
-
-
-def down_rows(act, down, width, bq):
-    _, length, cols = act.shape
+def back_kernel(rows, x_ref, *refs):
+    weights, out_ref = refs[:-1], refs[-1]
+    cols = weights[0].shape[2]
+    size = out_ref.shape[1] // len(weights)
+    x = x_ref[...].reshape(out_ref.shape[0], cols)
+    for n, weight in enumerate(weights):
+        part = weight[:, :rows, :].reshape(size, cols)
+        out_ref[:, n * size : (n + 1) * size] = nt(x, part).astype(BF)
+
+
+def back_rows(x, kind, weights, rows, width, bq):
+    _, length, cols = x.shape
     return pl.pallas_call(
-        functools.partial(down_kernel, len(down)),
+        functools.partial(back_kernel, rows),
         grid=(length // bq,),
-        in_specs=[pl.BlockSpec((1, bq, cols), lambda i: (2, i, 0))] + [whole(w) for w in down],
+        in_specs=[pl.BlockSpec((1, bq, cols), lambda i: (kind, i, 0))] + [whole(w) for w in weights],
         out_specs=pl.BlockSpec((bq, width), lambda i: (i, 0)),
         out_shape=jax.ShapeDtypeStruct((length, width), BF),
         cost_estimate=pl.CostEstimate(
@@ -330,8 +357,8 @@
             bytes_accessed=2 * length * width + 2 * width * cols,
             transcendentals=0,
         ),
-        name="down",
-    )(act, *down)
+        name="back",
+    )(x, *weights)
 
 
 def grad_kernel(n_ref, u_ref, act_ref, out_ref):
@@ -369,6 +396,27 @@
         ),
         name="gw",
     )(normed, upstream, act)
+
+
+def wide_kernel(parts, back_ref, *outs):
+    rows = outs[0].shape[0]
+    groups = back_ref.shape[0]
+    for out, pieces in zip(outs, parts):
+        for start, at, cols, base, step in pieces:
+            for s in range(groups):
+                value = back_ref[s, start : start + rows, at : at + cols]
+                out[:, base + s * step : base + s * step + cols] = value.astype(F32)
+
+
+def widen(back, rows, parts):
+    groups = back.shape[0]
+    shapes = [jax.ShapeDtypeStruct((rows, groups * sum(p[2] for p in pieces)), F32) for pieces in parts]
+    return pl.pallas_call(
+        functools.partial(wide_kernel, parts),
+        out_shape=shapes,
+        cost_estimate=pl.CostEstimate(flops=0, bytes_accessed=3 * back.size * 2, transcendentals=0),
+        name="wide",
+    )(back)
 
 
 def unit_of(values):
@@ -457,7 +505,6 @@
 
     own = relate(inputs, mine, copies, 1)
     own_up = relate(upstream, mine, copies, 1)
-    up_all = every(own_up)
 
     def by_group(weight, parts=1):
         cols = weight.shape[1] // (parts * groups)
@@ -481,14 +528,16 @@
     )
     taken, own = lax.optimization_barrier((take(view_qkv), own))
     x_all = every(own)
-    pieces_qkv = spread(taken)
-    weight_qkv = stack_rows(pieces_qkv, 0, rows)
+    pieces_qkv = [piece for pair in spread_halves(taken) for piece in pair]
+    own_up, unused = lax.optimization_barrier((own_up, taken))
+    up_all = every(own_up)
     weight_out = stack_rows(spread(take(by_group(out_weight))), 0, rows)
-    spot = pieces_qkv[0][:, rows, 4 * rows + nbias : 4 * rows + nbias + 2 * tokens]
+    spot = taken[:, rows, 4 * rows + nbias : 4 * rows + nbias + 2 * tokens]
     positions = (
         spot[:, :tokens].astype(jnp.int32) * 256 + spot[:, tokens:].astype(jnp.int32)
     ).reshape(length)
-    everyone = jnp.stack([p[:, rows, : 4 * rows + nbias] for p in pieces_qkv]).astype(F32)
+    everyone = jnp.concatenate([p[:, rows, : 4 * rows + nbias] for p in pieces_qkv]).astype(F32)
+    everyone = everyone.reshape(copies, groups, -1)
     gain_one, shift_one, gain_two, shift_two = [
         everyone[:, :, n * rows : (n + 1) * rows].reshape(1, width) for n in range(4)
     ]
@@ -506,10 +555,9 @@
     pieces_gu = spread(take(view_gu))
     pieces_down = spread(take(view_down))
 
-    unit_all, unused = unit_of(x_all.astype(F32))
-    normed_one = (unit_all * gain_one + shift_one).astype(BF)
-    projected = dot(normed_one, weight_qkv, NN) + bias_mine
-    qkv, context, lse = attend_fwd(projected, tables, low8, first, heads, bq)
+    normed_one, qkv, context, lse = attend_fwd(
+        x_all, gain_one, shift_one, bias_mine, pieces_qkv, rows, tables, low8, first, heads, bq
+    )
     flat = own.astype(F32)
     middle = flat + own_rows(dot(context, weight_out, NT))
     unit_two, factor_two = unit_of(middle)
@@ -517,7 +565,7 @@
     normed_two = every(normed_two)
     act, dx = ffn_both(normed_two, up_all, pieces_gu, pieces_down, rows, bq)
     grad_normed_two = own_rows(dx)
-    down_part = down_rows(act, pieces_down, width, bq)
+    down_part = back_rows(act, 2, pieces_down, rows, width, bq)
     block = width // copies
 
     def by_owner(left, right):
@@ -530,7 +578,7 @@
     for m in [*range(1, copies), 0]:
         grads[m] = ffn_grads(normed_two, up_all, act, m, copies, groups)
     sum_ffn = reduce_dp(grads).reshape(groups, 3 * rows, -1)
-    sum_ffn = send_back(sum_ffn).transpose(1, 0, 2)
+    sum_ffn = send_back(sum_ffn)
 
     grad_middle = own_up.astype(F32) + norm_back(grad_normed_two, unit_two, factor_two, gain_two)
     grad_mixed = grad_middle.astype(BF)
@@ -538,7 +586,7 @@
     grad_mixed = every(grad_mixed)
     grad_context = dot(grad_mixed, weight_out, NN).astype(BF)
     grad_projected, bias_part = attend_bwd(qkv, context, lse, grad_context, tables, low8, first, heads, bq)
-    dqkv = dot(grad_projected, weight_qkv, NT).astype(BF)
+    dqkv = back_rows(grad_projected[None], 0, pieces_qkv, rows, width, bq)
     grad_normed_one = own_rows(dqkv)
 
     late, unused = lax.optimization_barrier((down_sum[0], bias_part))
@@ -547,6 +595,9 @@
         total = total + piece.astype(F32)
     output = (middle + total).astype(BF)
 
+    grad_qkv_weight = by_owner(normed_one, grad_projected)
+    x_late, unused = lax.optimization_barrier((x_all, grad_qkv_weight[0]))
+    unit_all, unused = unit_of(x_late.astype(F32))
     bias_part = jnp.sum(bias_part, axis=0).reshape(3, 1, hc) * chosen[None, :, None]
     bias_part = relate(bias_part.reshape(-1), mine, copies, 0).reshape(copies, groups, nbias)
     parts = [
@@ -557,38 +608,41 @@
     ]
     parts = [p.reshape(copies, groups, 1, rows) for p in parts] + [bias_part[:, :, None]]
     parts = jnp.concatenate(parts, axis=3)
-    parts = jnp.pad(parts, ((0, 0), (0, 0), (0, 7), (0, 3 * hc - parts.shape[3]))).astype(BF)
-
-    sum_out = reduce_dp(by_owner(grad_mixed, context))
-    grad_qkv_weight = by_owner(normed_one, grad_projected)
-    sum_qkv = reduce_dp([jnp.concatenate([grad_qkv_weight[m], parts[m]], axis=1) for m in range(copies)])
-    sum_attn = jnp.concatenate([sum_qkv, jnp.pad(sum_out, ((0, 0), (0, 8), (0, 0)))], axis=2)
+    parts = jnp.pad(parts, ((0, 0), (0, 0), (0, 0), (0, 8 * hc - parts.shape[3]))).astype(BF)
+    parts = parts.reshape(copies, groups, 8, hc)
+
+    sum_qkv = reduce_dp(grad_qkv_weight)
+    grad_out_weight = by_owner(grad_mixed, context)
+    sum_out = reduce_dp([jnp.concatenate([grad_out_weight[m], parts[m]], axis=1) for m in range(copies)])
+    sum_attn = jnp.concatenate([jnp.pad(sum_qkv, ((0, 0), (0, 8), (0, 0))), sum_out], axis=2)
     sum_attn = send_back(sum_attn)
-    total = jnp.sum(sum_attn[:, rows].astype(F32), axis=0)
+    total = jnp.sum(sum_attn[:, rows:, 3 * hc :].astype(F32), axis=0).reshape(-1)
     sums = [total[n * rows : (n + 1) * rows] for n in range(4)] + [total[4 * rows : 4 * rows + nbias]]
-    sum_attn = sum_attn[:, :rows].transpose(1, 0, 2)
-    sum_qkv = sum_attn[:, :, : 3 * hc]
-    sum_out = sum_attn[:, :, 3 * hc :]
+    wide_qkv, wide_out = widen(
+        sum_attn,
+        rows,
+        (tuple((0, n * hc, hc, n * width, hc) for n in range(3)), ((0, 3 * hc, hc, 0, hc),)),
+    )
     unit_one, factor_one = unit_of(flat)
     grad_input = grad_middle + norm_back(grad_normed_one, unit_one, factor_one, gain_one)
 
-    def wide(value):
-        return value.astype(F32).reshape(rows, -1)
-
-    wide_qkv = sum_qkv.reshape(rows, groups, 3, hc).transpose(0, 2, 1, 3)
+    cols = sum_ffn.shape[2]
+    wide_gate, wide_up, wide_down = widen(
+        sum_ffn, rows, tuple(((n * rows, 0, cols, 0, cols),) for n in range(3))
+    )
     return (
         relate(output, mine, copies, 1)[None],
         relate(grad_input, mine, copies, 1)[None],
         sums[0],
         sums[1],
-        wide(wide_qkv),
+        wide_qkv,
         sums[4],
-        wide(sum_out),
+        wide_out,
         sums[2],
         sums[3],
-        wide(sum_ffn[:rows]),
-        wide(sum_ffn[rows : 2 * rows]),
-        wide(sum_ffn[2 * rows :]),
+        wide_gate,
+        wide_up,
+        wide_down,
     )
 
 

time: 762 us -> 767 us (level)
  local copies, waits for them, and re-layouts: 76.9 us -> 41.6 us
  waiting for transfers between devices: 374 us -> 405 us
  Pallas kernels: 81.8 us -> 102 us
  matrix products: 32.8 us -> 20.8 us
  other arithmetic: 53.6 us -> 44.3 us
    pallas_call x2 -> x5, Pallas kernels: 16.9 us -> 38.1 us  [the longest x1 16.4 us: attend_fwd(): pl.pallas_call(functools.partial(fwd_kernel, heads, bq, rows), grid_spec=...]
    reshape x10 -> x2, local copies, waits for them, and re-layouts: 19.7 us -> 1.36 us  [layer(): everyone[:, :, n * rows:(n + 1) * rows].reshape(1, width)]
    ppermute x21 -> x24, waiting for transfers between devices: 171 us -> 186 us  [swap_dp(): lax.ppermute(values, DP, [(d, d ^ rel) for d in range(lax.axis_size(DP))])]
    all_to_all x2, waiting for transfers between devices: 4.52 us -> 16.6 us  [send_back(): return lax.all_to_all(summed, SEQ, split_axis=0, concat_axis=0, tiled=True)]
    dot_general x12 -> x10, matrix products: 32.8 us -> 20.8 us  [dot(): lax.dot_general(left, right, (dims, ((), ())), preferred_element_type=F32)]
    ppermute x3, waiting for transfers between devices: 30 us -> 38.3 us  [chip_shift(): lax.ppermute(values, SEQ, [(s, (s + 2 * k) % groups) for s in range(group...]
    ppermute x21 -> x24, starting transfers between devices: 24.8 us -> 29.8 us  [swap_dp(): lax.ppermute(values, DP, [(d, d ^ rel) for d in range(lax.axis_size(DP))])]
  transfers between devices with their start and end apart: 37 -> 40, of which waited for: 20 -> 22; matrix products, arithmetic and copies ran while one was open for 17% -> 11% of each run, Pallas kernels for 6% -> 8%
where the time goes in v3:
time: 767 us; the launch traced here: 757 us
  waiting for transfers between devices  405 us (53%)
  Pallas kernels  102 us (13%)
  blocking collectives  70.1 us (9%)
  starting transfers between devices  58.1 us (8%)
  other arithmetic  44.3 us (6%)
  local copies, waits for them, and re-layouts  41.6 us (5%)
  matrix products  20.8 us (3%)
  between operations  15.2 us (2%)
    ppermute x24, waiting for transfers between devices, swap_dp(): lax.ppermute(values, DP, [(d, d ^ rel) for d in range(lax.axis_size(DP))])  186 us
    reduce_scatter x3, waiting for transfers between devices, own_rows(): lax.psum_scatter(partial.astype(BF), SEQ, scatter_dimension=0, tiled=True)  97.6 us
    all_to_all x1, blocking collectives, take(): return lax.all_to_all(view, SEQ, split_axis=0, concat_axis=0, tiled=True)  70.1 us
    all_to_all x3, waiting for transfers between devices, take(): return lax.all_to_all(view, SEQ, split_axis=0, concat_axis=0, tiled=True)  65.8 us
    ppermute x3, waiting for transfers between devices, chip_shift(): lax.ppermute(values, SEQ, [(s, (s + 2 * k) % groups) for s in range(group...  38.3 us
    ppermute x24, starting transfers between devices, swap_dp(): lax.ppermute(values, DP, [(d, d ^ rel) for d in range(lax.axis_size(DP))])  29.8 us
    pallas_call x4, Pallas kernels, ffn_grads(): pl.pallas_call(grad_kernel, grid=(3,), in_specs=[side, side, pl.BlockSpec...  26.9 us
    pallas_call x1, Pallas kernels, ffn_both(): pl.pallas_call(functools.partial(ffn_kernel, len(pair), rows), grid=(leng...  23.5 us
  transfers between devices with their start and end apart: 40, of which 22 were waited for; matrix products, arithmetic and copies ran while one was open for 11% of the time, Pallas kernels for 8%

profile of v3, /device:TPU:0, one launch (start us, length us, event | category | flops | bytes accessed | tf_op | source)
XLA Modules:
  0.0 756.8 jit_solution(16070351003126048908)
XLA Ops:
  23.0 21.5 %all-to-all-done = bf16[8,72,768]{2,1,0:T(8,128)(2,1)S(1)} async-done(((bf16[8,72,768]{2,1,0:T(8,128)(2,1)}), bf16[8,72,768]{2,1,0:T(8,128)(2,1)S(1)}, u32[]{:S(2)}, u32[]{:S(2)}) %all-to-all-start) | async-done | bytes 884768 | tf_op jit(solution)/shard_map/all_to_all | solution.py:246
  55.9 8.6 %all-to-all-done.1 = bf16[8,64,256]{2,1,0:T(8,128)(2,1)S(1)} async-done(((bf16[8,64,256]{2,1,0:T(8,128)(2,1)}), bf16[8,64,256]{2,1,0:T(8,128)(2,1)S(1)}, u32[]{:S(2)}, u32[]{:S(2)}) %all-to-all-start.1) | async-done | bytes 262176 | tf_op jit(solution)/shard_map/all_to_all | solution.py:246
  84.9 8.6 %collective-permute-done.3.refs_5_ = bf16[4,72,768]{2,1,0:T(8,128)(2,1)} collective-permute-done((bf16[4,72,768]{2,1,0:T(8,128)(2,1)S(1)}, bf16[4,72,768]{2,1,0:T(8,128)(2,1)}, u32[]{:S(2)}, u32[]{:S(2)}) %collective-permute-start.3) | collective-permute-done | bytes 442400 | tf_op jit(solution)/shard_map/ppermute | solution.py:242
  95.1 9.4 %collective-permute-done.refs_2_ = bf16[4,72,768]{2,1,0:T(8,128)(2,1)} collective-permute-done((bf16[4,72,768]{2,1,0:T(8,128)(2,1)}, bf16[4,72,768]{2,1,0:T(8,128)(2,1)}, u32[]{:S(2)}, u32[]{:S(2)}) %collective-permute-start) | collective-permute-done | bytes 442400 | tf_op jit(solution)/shard_map/ppermute | solution.py:242
  118.8 16.4 %af.1 = (bf16[1024,2048]{1,0:T(8,128)(2,1)}, bf16[1024,768]{1,0:T(8,128)(2,1)}, bf16[1024,256]{1,0:T(8,128)(2,1)}, f32[8,1024]{1,0:T(8,128)}) custom-call(s32[4]{0:T(128)} %and_select_fusion.2.first_ref, s32[8,1024]{1,0:T(8,128)} %broadcast_in_dim.30.low_ref, f32[1024,128]{1,0:T(8,128)} %get-tuple-element.134.cos_ref, ...), custom_call_target="tpu_custom_call" | custom-call | flops 4294967296 | bytes 14680064 | tf_op jit(solution)/shard_map/af/pallas_call | solution.py:138
  141.3 49.5 %reduce-scatter.4.cloned.1.call-done = bf16[128,2048]{1,0:T(8,128)(2,1)} async-done(((bf16[1024,2048]{1,0:T(8,128)(2,1)}), bf16[128,2048]{1,0:T(8,128)(2,1)}) %reduce-scatter.4.cloned.1.call-update) | async-done | bytes 524304 | tf_op jit(solution)/shard_map/reduce_scatter | solution.py:447
  196.5 70.1 %all_to_all.30 = bf16[8,128,704]{1,2,0:T(8,128)(2,1)S(1)} all-to-all(bf16[8,128,704]{1,2,0:T(8,128)(2,1)} %copy.124), channel_id=1, replica_groups=mesh['dp'=4,'seq'=8] {'seq'}, dimensions={0} | all-to-all | bytes 2883584 | tf_op jit(solution)/shard_map/all_to_all | solution.py:246
  273.7 35.6 %all-to-all-done.3.refs_4_.refs_0_ = bf16[8,64,704]{2,1,0:T(8,128)(2,1)S(1)} async-done(((bf16[8,64,704]{2,1,0:T(8,128)(2,1)}), bf16[8,64,704]{2,1,0:T(8,128)(2,1)S(1)}, u32[]{:S(2)}, u32[]{:S(2)}) %all-to-all-start.3) | async-done | bytes 720928 | tf_op jit(solution)/shard_map/all_to_all | solution.py:246
  317.0 16.0 %collective-permute-done.10 = bf16[8,128,704]{1,2,0:T(8,128)(2,1)} collective-permute-done((bf16[8,128,704]{1,2,0:T(8,128)(2,1)S(1)}, bf16[8,128,704]{1,2,0:T(8,128)(2,1)}, u32[]{:S(2)}, u32[]{:S(2)}) %collective-permute-start.10) | collective-permute-done | bytes 1441824 | tf_op jit(solution)/shard_map/ppermute | solution.py:242
  338.1 11.7 %collective-permute-done.14.refs_7_.refs_3_ = bf16[8,64,704]{2,1,0:T(8,128)(2,1)} collective-permute-done((bf16[8,64,704]{2,1,0:T(8,128)(2,1)S(1)}, bf16[8,64,704]{2,1,0:T(8,128)(2,1)}, u32[]{:S(2)}, u32[]{:S(2)}) %collective-permute-start.14) | collective-permute-done | bytes 720928 | tf_op jit(solution)/shard_map/ppermute | solution.py:242
  349.8 15.9 %collective-permute-done.13.refs_6_.refs_2_ = bf16[8,64,704]{2,1,0:T(8,128)(2,1)} collective-permute-done((bf16[8,64,704]{2,1,0:T(8,128)(2,1)S(1)}, bf16[8,64,704]{2,1,0:T(8,128)(2,1)}, u32[]{:S(2)}, u32[]{:S(2)}) %collective-permute-start.13) | collective-permute-done | bytes 720928 | tf_op jit(solution)/shard_map/ppermute | solution.py:242
  365.8 23.5 %ffn.1 = (bf16[3,1024,704]{2,1,0:T(8,128)(2,1)}, bf16[1024,2048]{1,0:T(8,128)(2,1)}) custom-call(bf16[1024,2048]{1,0:T(8,128)(2,1)} %all-gather.7.cloned.1.call-done.n_ref, bf16[1024,2048]{1,0:T(8,128)(2,1)} %all-gather.9.cloned.1.call-done.u_ref, bf16[8,128,704]{2,1,0:T(8,128)(2,1)} %copy.125.refs_0_, bf16[8,128,704]{2,1,0:T(8,128)(2,1)} %copy.126.refs_1_, ...), custom_call_target="tpu_custom_call" | custom-call | flops 14763950080 | bytes 21233664 | tf_op jit(solution)/shard_map/ffn/pallas_call | solution.py:319
  389.6 48.1 %reduce-scatter.6.cloned.1.call-done = bf16[128,2048]{1,0:T(8,128)(2,1)} async-done(((bf16[1024,2048]{1,0:T(8,128)(2,1)}), bf16[128,2048]{1,0:T(8,128)(2,1)}) %reduce-scatter.6.cloned.1.call-update) | async-done | bytes 524304 | tf_op jit(solution)/shard_map/reduce_scatter | solution.py:447
  450.7 6.7 gw.6
  458.9 6.8 gw.7
  466.2 6.7 gw.4
  473.0 7.4 back.2
  483.7 19.9 %collective-permute-done.25 = bf16[8,3,64,704]{3,2,1,0:T(8,128)(2,1)S(1)} collective-permute-done((bf16[8,3,64,704]{3,2,1,0:T(8,128)(2,1)}, bf16[8,3,64,704]{3,2,1,0:T(8,128)(2,1)S(1)}, u32[]{:S(2)}, u32[]{:S(2)}) %collective-permute-start.25) | collective-permute-done | bytes 2162720 | tf_op jit(solution)/shard_map/ppermute | solution.py:242
  503.6 55.9 %collective-permute-done.26 = bf16[8,3,64,704]{3,2,1,0:T(8,128)(2,1)} collective-permute-done((bf16[8,3,64,704]{3,2,1,0:T(8,128)(2,1)}, bf16[8,3,64,704]{3,2,1,0:T(8,128)(2,1)}, u32[]{:S(2)}, u32[]{:S(2)}) %collective-permute-start.26) | collective-permute-done | bytes 2162720 | tf_op jit(solution)/shard_map/ppermute | solution.py:242
  575.2 13.8 %ab.1 = (bf16[1024,768]{1,0:T(8,128)(2,1)}, f32[8,768]{1,0:T(8,128)}) custom-call(s32[4]{0:T(128)} %and_select_fusion.2.first_ref, s32[8,1024]{1,0:T(8,128)} %broadcast_in_dim.30.low_ref, f32[1024,128]{1,0:T(8,128)} %get-tuple-element.134.cos_ref, f32[1024,128]{1,0:T(8,128)} %get-tuple-element.133.s1_ref, f32[1024,128]{1,0:T(8,128)} %get-tuple-element.132.s2_ref, ...), custom_call_target="tpu_custom_call" | custom-call | flops 2684354560 | bytes 6291456 | tf_op jit(solution)/shard_map/ab/pallas_call | solution.py:215
  589.0 7.5 back.3
  631.6 32.1 %collective-permute-done.22 = bf16[8,72,256]{2,1,0:T(8,128)(2,1)S(1)} collective-permute-done((bf16[8,72,256]{2,1,0:T(8,128)(2,1)S(1)}, bf16[8,72,256]{2,1,0:T(8,128)(2,1)S(1)}, u32[]{:S(2)}, u32[]{:S(2)}) %collective-permute-start.22) | collective-permute-done | bytes 294944 | tf_op jit(solution)/shard_map/ppermute | solution.py:242
  683.6 16.5 %all-to-all-done.4.back_ref = bf16[8,72,1024]{2,1,0:T(8,128)(2,1)} async-done(((bf16[8,72,1024]{2,1,0:T(8,128)(2,1)}), bf16[8,72,1024]{2,1,0:T(8,128)(2,1)}, u32[]{:S(2)}, u32[]{:S(2)}) %all-to-all-start.4) | async-done | bytes 1179680 | tf_op jit(solution)/shard_map/all_to_all | solution.py:278
  706.2 38.3 %collective-permute-done.17 = bf16[128,2048]{1,0:T(8,128)(2,1)} collective-permute-done((bf16[128,2048]{1,0:T(8,128)(2,1)}, bf16[128,2048]{1,0:T(8,128)(2,1)}, u32[]{:S(2)}, u32[]{:S(2)}) %collective-permute-start.17) | collective-permute-done | bytes 524320 | tf_op jit(solution)/shard_map/ppermute | solution.py:455
  (288 shorter events, 195.0 us)
Async XLA Ops:
  21.4 96.7 %all-gather.5.cloned.1.call-start = ((), (), s32[]{:S(2)}) async-start(), calls=%async_computation.9 | async-start | bytes 4718592 | tf_op jit(solution)/shard_map/all_gather | solution.py:451
  49.7 141.1 %reduce-scatter.4.cloned.1.call-start = ((), (), s32[]{:S(2)}) async-start(), calls=%async_computation.10 | async-start | bytes 4718592 | tf_op jit(solution)/shard_map/reduce_scatter | solution.py:447
  139.9 198.2 %all-gather.9.cloned.1.call-start = ((), (), s32[]{:S(2)}) async-start(), calls=%async_computation.12 | async-start | bytes 4718592 | tf_op jit(solution)/shard_map/all_gather | solution.py:451
  140.9 224.9 %all-gather.7.cloned.1.call-start = ((), (), s32[]{:S(2)}) async-start(), calls=%async_computation.11 | async-start | bytes 4718592 | tf_op jit(solution)/shard_map/all_gather | solution.py:451
  266.5 44.7 %collective-permute-start.11 = (bf16[8,128,704]{1,2,0:T(8,128)(2,1)S(1)}, bf16[8,128,704]{1,2,0:T(8,128)(2,1)}, u32[]{:S(2)}, u32[]{:S(2)}) collective-permute-start(bf16[8,128,704]{1,2,0:T(8,128)(2,1)S(1)} %all_to_all.30), channel_id=1, source_target_pairs={{0,24},{8,16},{16,8},{24,0},{1,25},{9,17},{17,9},{25,1},{2,26},{10... | collective-permute-start | bytes 4325384 | tf_op jit(solution)/shard_map/ppermute | solution.py:242
  268.9 40.4 %all-to-all-start.3 = ((bf16[8,64,704]{2,1,0:T(8,128)(2,1)}), bf16[8,64,704]{2,1,0:T(8,128)(2,1)S(1)}, u32[]{:S(2)}, u32[]{:S(2)}) async-start(bf16[8,64,704]{2,1,0:T(8,128)(2,1)} %bitcast.163), calls=%async_computation.4 | async-start | bytes 1572864 | tf_op jit(solution)/shard_map/all_to_all | solution.py:246
  272.5 165.3 %reduce-scatter.6.cloned.1.call-start = ((), (), s32[]{:S(2)}) async-start(), calls=%async_computation.13 | async-start | bytes 4718592 | tf_op jit(solution)/shard_map/reduce_scatter | solution.py:447
  272.5 60.4 %collective-permute-start.10 = (bf16[8,128,704]{1,2,0:T(8,128)(2,1)S(1)}, bf16[8,128,704]{1,2,0:T(8,128)(2,1)}, u32[]{:S(2)}, u32[]{:S(2)}) collective-permute-start(bf16[8,128,704]{1,2,0:T(8,128)(2,1)S(1)} %all_to_all.30), channel_id=1, source_target_pairs={{0,16},{8,24},{16,0},{24,8},{1,17},{9,25},{17,1},{25,9},{2,18},{10... | collective-permute-start | bytes 4325384 | tf_op jit(solution)/shard_map/ppermute | solution.py:242
  273.1 62.4 %collective-permute-start.9 = (bf16[8,128,704]{1,2,0:T(8,128)(2,1)S(1)}, bf16[8,128,704]{1,2,0:T(8,128)(2,1)}, u32[]{:S(2)}, u32[]{:S(2)}) collective-permute-start(bf16[8,128,704]{1,2,0:T(8,128)(2,1)S(1)} %all_to_all.30), channel_id=1, source_target_pairs={{0,8},{8,0},{16,24},{24,16},{1,9},{9,1},{17,25},{25,17},{2,10},{10... | collective-permute-start | bytes 4325384 | tf_op jit(solution)/shard_map/ppermute | solution.py:242
  309.3 40.5 %collective-permute-start.14 = (bf16[8,64,704]{2,1,0:T(8,128)(2,1)S(1)}, bf16[8,64,704]{2,1,0:T(8,128)(2,1)}, u32[]{:S(2)}, u32[]{:S(2)}) collective-permute-start(bf16[8,64,704]{2,1,0:T(8,128)(2,1)S(1)} %all-to-all-done.3.refs_4_.refs_0_), channel_id=1, source_target_pairs={{0,24},{8,16},{16,8},{24,0},{1,25},{9,17},{17,9},{25,1},{2,26},{10... | collective-permute-start | bytes 2162696 | tf_op jit(solution)/shard_map/ppermute | solution.py:242
  309.6 56.2 %collective-permute-start.13 = (bf16[8,64,704]{2,1,0:T(8,128)(2,1)S(1)}, bf16[8,64,704]{2,1,0:T(8,128)(2,1)}, u32[]{:S(2)}, u32[]{:S(2)}) collective-permute-start(bf16[8,64,704]{2,1,0:T(8,128)(2,1)S(1)} %all-to-all-done.3.refs_4_.refs_0_), channel_id=1, source_target_pairs={{0,16},{8,24},{16,0},{24,8},{1,17},{9,25},{17,1},{25,9},{2,18},{10... | collective-permute-start | bytes 2162696 | tf_op jit(solution)/shard_map/ppermute | solution.py:242
  311.3 54.6 %collective-permute-start.12 = (bf16[8,64,704]{2,1,0:T(8,128)(2,1)S(1)}, bf16[8,64,704]{2,1,0:T(8,128)(2,1)}, u32[]{:S(2)}, u32[]{:S(2)}) collective-permute-start(bf16[8,64,704]{2,1,0:T(8,128)(2,1)S(1)} %all-to-all-done.3.refs_4_.refs_0_), channel_id=1, source_target_pairs={{0,8},{8,0},{16,24},{24,16},{1,9},{9,1},{17,25},{25,17},{2,10},{10... | collective-permute-start | bytes 2162696 | tf_op jit(solution)/shard_map/ppermute | solution.py:242
  389.4 181.3 %all-gather.11.cloned.1.call-start = ((), (), s32[]{:S(2)}) async-start(), calls=%async_computation.14 | async-start | bytes 4718592 | tf_op jit(solution)/shard_map/all_gather | solution.py:451
  449.3 54.3 %collective-permute-start.25 = (bf16[8,3,64,704]{3,2,1,0:T(8,128)(2,1)}, bf16[8,3,64,704]{3,2,1,0:T(8,128)(2,1)S(1)}, u32[]{:S(2)}, u32[]{:S(2)}) collective-permute-start(bf16[8,3,64,704]{3,2,1,0:T(8,128)(2,1)} %gw.5), channel_id=1, source_target_pairs={{0,8},{8,0},{16,24},{24,16},{1,9},{9,1},{17,25},{25,17},{2,10},{10... | collective-permute-start | bytes 6488072 | tf_op jit(solution)/shard_map/ppermute | solution.py:242
  457.4 102.1 %collective-permute-start.26 = (bf16[8,3,64,704]{3,2,1,0:T(8,128)(2,1)}, bf16[8,3,64,704]{3,2,1,0:T(8,128)(2,1)}, u32[]{:S(2)}, u32[]{:S(2)}) collective-permute-start(bf16[8,3,64,704]{3,2,1,0:T(8,128)(2,1)} %gw.6), channel_id=1, source_target_pairs={{0,16},{8,24},{16,0},{24,8},{1,17},{9,25},{17,1},{25,9},{2,18},{10... | collective-permute-start | bytes 6488072 | tf_op jit(solution)/shard_map/ppermute | solution.py:242
  465.7 93.9 %collective-permute-start.27 = (bf16[8,3,64,704]{3,2,1,0:T(8,128)(2,1)}, bf16[8,3,64,704]{3,2,1,0:T(8,128)(2,1)}, u32[]{:S(2)}, u32[]{:S(2)}) collective-permute-start(bf16[8,3,64,704]{3,2,1,0:T(8,128)(2,1)} %gw.7), channel_id=1, source_target_pairs={{0,24},{8,16},{16,8},{24,0},{1,25},{9,17},{17,9},{25,1},{2,26},{10... | collective-permute-start | bytes 6488072 | tf_op jit(solution)/shard_map/ppermute | solution.py:242
  564.9 100.5 %all-to-all-start.5 = ((bf16[8,192,704]{2,1,0:T(8,128)(2,1)}), bf16[8,192,704]{2,1,0:T(8,128)(2,1)S(1)}, u32[]{:S(2)}, u32[]{:S(2)}) async-start(bf16[8,192,704]{2,1,0:T(8,128)(2,1)} %bitcast.158), calls=%async_computation.8 | async-start | bytes 4718592 | tf_op jit(solution)/shard_map/all_to_all | solution.py:278
  568.9 135.9 %reduce-scatter.8.cloned.1.call-start = ((), (), s32[]{:S(2)}) async-start(), calls=%async_computation.15 | async-start | bytes 4718592 | tf_op jit(solution)/shard_map/reduce_scatter | solution.py:447
  619.8 44.0 %collective-permute-start.19 = (bf16[8,64,768]{2,1,0:T(8,128)(2,1)S(1)}, bf16[8,64,768]{2,1,0:T(8,128)(2,1)S(1)}, u32[]{:S(2)}, u32[]{:S(2)}) collective-permute-start(bf16[8,64,768]{2,1,0:T(8,128)(2,1)S(1)} %bitcast.202), channel_id=1, source_target_pairs={{0,8},{8,0},{16,24},{24,16},{1,9},{9,1},{17,25},{25,17},{2,10},{10... | collective-permute-start | bytes 2359304 | tf_op jit(solution)/shard_map/ppermute | solution.py:242
  621.2 42.5 %collective-permute-start.20 = (bf16[8,64,768]{2,1,0:T(8,128)(2,1)S(1)}, bf16[8,64,768]{2,1,0:T(8,128)(2,1)S(1)}, u32[]{:S(2)}, u32[]{:S(2)}) collective-permute-start(bf16[8,64,768]{2,1,0:T(8,128)(2,1)S(1)} %bitcast.201), channel_id=1, source_target_pairs={{0,16},{8,24},{16,0},{24,8},{1,17},{9,25},{17,1},{25,9},{2,18},{10... | collective-permute-start | bytes 2359304 | tf_op jit(solution)/shard_map/ppermute | solution.py:242
  623.2 40.6 %collective-permute-start.21 = (bf16[8,64,768]{2,1,0:T(8,128)(2,1)S(1)}, bf16[8,64,768]{2,1,0:T(8,128)(2,1)S(1)}, u32[]{:S(2)}, u32[]{:S(2)}) collective-permute-start(bf16[8,64,768]{2,1,0:T(8,128)(2,1)S(1)} %bitcast.200), channel_id=1, source_target_pairs={{0,24},{8,16},{16,8},{24,0},{1,25},{9,17},{17,9},{25,1},{2,26},{10... | collective-permute-start | bytes 2359304 | tf_op jit(solution)/shard_map/ppermute | solution.py:242
  623.8 46.3 %collective-permute-start.15 = (bf16[4,128,2048]{2,1,0:T(8,128)(2,1)}, bf16[4,128,2048]{2,1,0:T(8,128)(2,1)}, u32[]{:S(2)}, u32[]{:S(2)}) collective-permute-start(bf16[4,128,2048]{2,1,0:T(8,128)(2,1)} %dynamic-slice_bitcast_fusion), channel_id=1, source_target_pairs={{0,1},{1,0},{2,3},{3,2},{4,5},{5,4},{6,7},{7,6},{8,9},{9,8},{10,11... | collective-permute-start | bytes 6291464 | tf_op jit(solution)/shard_map/ppermute | solution.py:459
  678.4 66.1 %collective-permute-start.17 = (bf16[128,2048]{1,0:T(8,128)(2,1)}, bf16[128,2048]{1,0:T(8,128)(2,1)}, u32[]{:S(2)}, u32[]{:S(2)}) collective-permute-start(bf16[128,2048]{1,0:T(8,128)(2,1)} %get-tuple-element.74), channel_id=1, source_target_pairs={{0,4},{1,5},{2,6},{3,7},{4,0},{5,1},{6,2},{7,3},{8,12},{9,13},{10,... | collective-permute-start | bytes 1572872 | tf_op jit(solution)/shard_map/ppermute | solution.py:455
  678.4 66.1 %collective-permute-start.16 = (bf16[128,2048]{1,0:T(8,128)(2,1)}, bf16[128,2048]{1,0:T(8,128)(2,1)}, u32[]{:S(2)}, u32[]{:S(2)}) collective-permute-start(bf16[128,2048]{1,0:T(8,128)(2,1)} %get-tuple-element.75), channel_id=1, source_target_pairs={{0,2},{1,3},{2,4},{3,5},{4,6},{5,7},{6,0},{7,1},{8,10},{9,11},{10,... | collective-permute-start | bytes 1572872 | tf_op jit(solution)/shard_map/ppermute | solution.py:455
  (42 other events, 934.5 us)
Sparse Core Ops, SparseCore 0:
  44.6 50.3 all-gather.4
  140.0 50.7 reduce-scatter.3
  192.4 76.1 all-gather.8
  270.7 58.0 all-gather.6
  389.5 48.2 reduce-scatter.5
  442.7 45.3 all-gather.10
  596.6 63.5 reduce-scatter.7

commit v4 on v3

--- a/solution.py
+++ b/solution.py
@@ -459,6 +459,37 @@
     return lax.ppermute(values, SEQ, [(s, s ^ 1) for s in range(groups)])
 
 
+def place_kernel(spot_ref, *refs):
+    out_ref = refs[-1]
+    for n, piece in enumerate(refs[:-1]):
+
+        @pl.when(pl.program_id(0) == n)
+        def _():
+            out_ref[...] = piece[...]
+
+
+def every_beside(values, me, groups):
+    chips = groups // 2
+    tokens, width = values.shape
+    held = [values] + [chip_shift(values, k, groups) for k in range(1, chips)]
+    other = [core_swap(piece, groups) for piece in held]
+    steps = jnp.arange(groups, dtype=jnp.int32)
+    who = jnp.where(steps < chips, me, me + 1 - 2 * (me % 2))
+    spots = (who - 2 * (steps % chips) + groups) % groups
+    return pl.pallas_call(
+        place_kernel,
+        grid_spec=pltpu.PrefetchScalarGridSpec(
+            num_scalar_prefetch=1,
+            grid=(groups,),
+            in_specs=[whole(values)] * groups,
+            out_specs=pl.BlockSpec((tokens, width), lambda n, spot: (spot[n], 0)),
+        ),
+        out_shape=jax.ShapeDtypeStruct((groups * tokens, width), values.dtype),
+        cost_estimate=pl.CostEstimate(flops=0, bytes_accessed=4 * groups * tokens * width, transcendentals=0),
+        name="place",
+    )(spots.astype(jnp.int32), *held, *other)
+
+
 def own_rows_beside(partial, me, groups):
     chips = groups // 2
     tokens = partial.shape[0] // groups
@@ -529,8 +560,6 @@
     taken, own = lax.optimization_barrier((take(view_qkv), own))
     x_all = every(own)
     pieces_qkv = [piece for pair in spread_halves(taken) for piece in pair]
-    own_up, unused = lax.optimization_barrier((own_up, taken))
-    up_all = every(own_up)
     weight_out = stack_rows(spread(take(by_group(out_weight))), 0, rows)
     spot = taken[:, rows, 4 * rows + nbias : 4 * rows + nbias + 2 * tokens]
     positions = (
@@ -551,7 +580,10 @@
     first = (jnp.min(lowest.reshape(length // bq, bq), axis=1) // bq).astype(jnp.int32)
 
     view_gu = jnp.concatenate([by_group(gate_weight), by_group(up_weight)], axis=1)
-    view_gu, view_down, x_all = lax.optimization_barrier((view_gu, by_group(down_weight), x_all))
+    view_gu, view_down, own_up, x_all = lax.optimization_barrier(
+        (view_gu, by_group(down_weight), own_up, x_all)
+    )
+    up_all = every_beside(own_up, me, groups)
     pieces_gu = spread(take(view_gu))
     pieces_down = spread(take(view_down))
 
@@ -580,9 +612,9 @@
     sum_ffn = reduce_dp(grads).reshape(groups, 3 * rows, -1)
     sum_ffn = send_back(sum_ffn)
 
+    down_sum = own_rows_beside(down_part, me, groups)
     grad_middle = own_up.astype(F32) + norm_back(grad_normed_two, unit_two, factor_two, gain_two)
     grad_mixed = grad_middle.astype(BF)
-    down_sum = own_rows_beside(down_part, me, groups)
     grad_mixed = every(grad_mixed)
     grad_context = dot(grad_mixed, weight_out, NN).astype(BF)
     grad_projected, bias_part = attend_bwd(qkv, context, lse, grad_context, tables, low8, first, heads, bq)

time: 767 us -> 802 us (1.046)
  waiting for transfers between devices: 405 us -> 481 us
  blocking collectives: 70.1 us -> 0 us
  starting transfers between devices: 58.1 us -> 81.5 us
    all_to_all x1 -> x0, blocking collectives: 70.1 us -> none  [take(): return lax.all_to_all(view, SEQ, split_axis=0, concat_axis=0, tiled=True)]
    ppermute x3 -> x6, waiting for transfers between devices: 38.3 us -> 87.8 us  [chip_shift(): lax.ppermute(values, SEQ, [(s, (s + 2 * k) % groups) for s in range(group...]
    all_to_all x3 -> x4, waiting for transfers between devices: 65.8 us -> 92 us  [take(): return lax.all_to_all(view, SEQ, split_axis=0, concat_axis=0, tiled=True)]
    all_to_all x3 -> x4, starting transfers between devices: 13.4 us -> 28.2 us  [take(): return lax.all_to_all(view, SEQ, split_axis=0, concat_axis=0, tiled=True)]
  transfers between devices with their start and end apart: 40 -> 47, of which waited for: 22 -> 23; matrix products, arithmetic and copies ran while one was open for 11% -> 10% of each run, Pallas kernels for 8% -> 9%
where the time goes in v4:
time: 802 us; the launch traced here: 792 us
  waiting for transfers between devices  481 us (60%)
  Pallas kernels  109 us (14%)
  starting transfers between devices  81.5 us (10%)
  other arithmetic  43.1 us (5%)
  local copies, waits for them, and re-layouts  42.2 us (5%)
  matrix products  20.5 us (3%)
  between operations  15.3 us (2%)
    ppermute x24, waiting for transfers between devices, swap_dp(): lax.ppermute(values, DP, [(d, d ^ rel) for d in range(lax.axis_size(DP))])  183 us
    reduce_scatter x3, waiting for transfers between devices, own_rows(): lax.psum_scatter(partial.astype(BF), SEQ, scatter_dimension=0, tiled=True)  99.7 us
    all_to_all x4, waiting for transfers between devices, take(): return lax.all_to_all(view, SEQ, split_axis=0, concat_axis=0, tiled=True)  92 us
    ppermute x6, waiting for transfers between devices, chip_shift(): lax.ppermute(values, SEQ, [(s, (s + 2 * k) % groups) for s in range(group...  87.8 us
    ppermute x24, starting transfers between devices, swap_dp(): lax.ppermute(values, DP, [(d, d ^ rel) for d in range(lax.axis_size(DP))])  29.7 us
    all_to_all x4, starting transfers between devices, take(): return lax.all_to_all(view, SEQ, split_axis=0, concat_axis=0, tiled=True)  28.2 us
    pallas_call x4, Pallas kernels, ffn_grads(): pl.pallas_call(grad_kernel, grid=(3,), in_specs=[side, side, pl.BlockSpec...  26.9 us
    pallas_call x1, Pallas kernels, ffn_both(): pl.pallas_call(functools.partial(ffn_kernel, len(pair), rows), grid=(leng...  23.6 us
  transfers between devices with their start and end apart: 47, of which 23 were waited for; matrix products, arithmetic and copies ran while one was open for 10% of the time, Pallas kernels for 9%

profile of v4, /device:TPU:0, one launch (start us, length us, event | category | flops | bytes accessed | tf_op | source)
XLA Modules:
  0.0 792.0 jit_solution(17266440861214194836)
XLA Ops:
  22.5 21.8 %all-to-all-done = bf16[8,72,768]{2,1,0:T(8,128)(2,1)S(1)} async-done(((bf16[8,72,768]{2,1,0:T(8,128)(2,1)}), bf16[8,72,768]{2,1,0:T(8,128)(2,1)S(1)}, u32[]{:S(2)}, u32[]{:S(2)}) %all-to-all-start) | async-done | bytes 884768 | tf_op jit(solution)/shard_map/all_to_all | solution.py:246
  55.3 7.7 all-to-all-done.1
  82.1 8.1 %collective-permute-done.3.refs_5_ = bf16[4,72,768]{2,1,0:T(8,128)(2,1)} collective-permute-done((bf16[4,72,768]{2,1,0:T(8,128)(2,1)}, bf16[4,72,768]{2,1,0:T(8,128)(2,1)}, u32[]{:S(2)}, u32[]{:S(2)}) %collective-permute-start.3) | collective-permute-done | bytes 442400 | tf_op jit(solution)/shard_map/ppermute | solution.py:242
  91.7 9.4 %collective-permute-done.refs_2_ = bf16[4,72,768]{2,1,0:T(8,128)(2,1)} collective-permute-done((bf16[4,72,768]{2,1,0:T(8,128)(2,1)}, bf16[4,72,768]{2,1,0:T(8,128)(2,1)}, u32[]{:S(2)}, u32[]{:S(2)}) %collective-permute-start) | collective-permute-done | bytes 442400 | tf_op jit(solution)/shard_map/ppermute | solution.py:242
  114.0 16.4 %af.1 = (bf16[1024,2048]{1,0:T(8,128)(2,1)}, bf16[1024,768]{1,0:T(8,128)(2,1)}, bf16[1024,256]{1,0:T(8,128)(2,1)}, f32[8,1024]{1,0:T(8,128)}) custom-call(s32[4]{0:T(128)} %and_select_fusion.4.first_ref, s32[8,1024]{1,0:T(8,128)} %broadcast_in_dim.62.low_ref, f32[1024,128]{1,0:T(8,128)} %get-tuple-element.134.cos_ref, ...), custom_call_target="tpu_custom_call" | custom-call | flops 4294967296 | bytes 14680064 | tf_op jit(solution)/shard_map/af/pallas_call | solution.py:138
  135.1 53.5 %reduce-scatter.4.cloned.1.call-done = bf16[128,2048]{1,0:T(8,128)(2,1)} async-done(((bf16[1024,2048]{1,0:T(8,128)(2,1)}), bf16[128,2048]{1,0:T(8,128)(2,1)}) %reduce-scatter.4.cloned.1.call-update) | async-done | bytes 524304 | tf_op jit(solution)/shard_map/reduce_scatter | solution.py:447
  201.6 62.4 %all-to-all-done.2 = bf16[8,128,704]{1,2,0:T(8,128)(2,1)S(1)} async-done(((bf16[8,128,704]{1,2,0:T(8,128)(2,1)}), bf16[8,128,704]{1,2,0:T(8,128)(2,1)S(1)}, u32[]{:S(2)}, u32[]{:S(2)}) %all-to-all-start.2) | async-done | bytes 1441824 | tf_op jit(solution)/shard_map/all_to_all | solution.py:246
  266.4 14.8 %all-to-all-start.3 = ((bf16[8,64,704]{2,1,0:T(8,128)(2,1)}), bf16[8,64,704]{2,1,0:T(8,128)(2,1)}, u32[]{:S(2)}, u32[]{:S(2)}) async-start(bf16[8,64,704]{2,1,0:T(8,128)(2,1)} %bitcast.161), calls=%async_computation.4 | async-start | bytes 1572864 | tf_op jit(solution)/shard_map/all_to_all | solution.py:246
  286.4 49.5 %collective-permute-done.10.refs_2_ = bf16[128,2048]{1,0:T(8,128)(2,1)S(1)} collective-permute-done((bf16[128,2048]{1,0:T(8,128)(2,1)S(1)}, bf16[128,2048]{1,0:T(8,128)(2,1)S(1)}, u32[]{:S(2)}, u32[]{:S(2)}) %collective-permute-start.10) | collective-permute-done | bytes 524320 | tf_op jit(solution)/shard_map/ppermute | solution.py:455
  355.6 14.8 %collective-permute-done.16 = bf16[8,128,704]{1,2,0:T(8,128)(2,1)} collective-permute-done((bf16[8,128,704]{1,2,0:T(8,128)(2,1)S(1)}, bf16[8,128,704]{1,2,0:T(8,128)(2,1)}, u32[]{:S(2)}, u32[]{:S(2)}) %collective-permute-start.16) | collective-permute-done | bytes 1441824 | tf_op jit(solution)/shard_map/ppermute | solution.py:242
  373.0 14.3 %collective-permute-done.21.refs_7_.refs_3_ = bf16[8,64,704]{2,1,0:T(8,128)(2,1)} collective-permute-done((bf16[8,64,704]{2,1,0:T(8,128)(2,1)}, bf16[8,64,704]{2,1,0:T(8,128)(2,1)}, u32[]{:S(2)}, u32[]{:S(2)}) %collective-permute-start.21) | collective-permute-done | bytes 720928 | tf_op jit(solution)/shard_map/ppermute | solution.py:242
  387.3 15.4 %collective-permute-done.19.refs_5_.refs_1_ = bf16[8,64,704]{2,1,0:T(8,128)(2,1)} collective-permute-done((bf16[8,64,704]{2,1,0:T(8,128)(2,1)}, bf16[8,64,704]{2,1,0:T(8,128)(2,1)}, u32[]{:S(2)}, u32[]{:S(2)}) %collective-permute-start.19) | collective-permute-done | bytes 720928 | tf_op jit(solution)/shard_map/ppermute | solution.py:242
  402.7 23.6 %ffn.1 = (bf16[3,1024,704]{2,1,0:T(8,128)(2,1)}, bf16[1024,2048]{1,0:T(8,128)(2,1)}) custom-call(bf16[1024,2048]{1,0:T(8,128)(2,1)} %all-gather.6.cloned.1.call-done.n_ref, bf16[1024,2048]{1,0:T(8,128)(2,1)} %place.1.u_ref, bf16[8,128,704]{2,1,0:T(8,128)(2,1)} %copy.125.refs_0_, bf16[8,128,704]{2,1,0:T(8,128)(2,1)} %copy.126.refs_1_, ...), custom_call_target="tpu_custom_call" | custom-call | flops 14763950080 | bytes 21233664 | tf_op jit(solution)/shard_map/ffn/pallas_call | solution.py:319
  426.7 46.2 %reduce-scatter.6.cloned.1.call-done = bf16[128,2048]{1,0:T(8,128)(2,1)} async-done(((bf16[1024,2048]{1,0:T(8,128)(2,1)}), bf16[128,2048]{1,0:T(8,128)(2,1)}) %reduce-scatter.6.cloned.1.call-update) | async-done | bytes 524304 | tf_op jit(solution)/shard_map/reduce_scatter | solution.py:447
  485.9 6.7 gw.6
  494.1 6.8 gw.7
  508.1 7.4 back.2
  518.9 19.9 %collective-permute-done.32 = bf16[8,3,64,704]{3,2,1,0:T(8,128)(2,1)S(1)} collective-permute-done((bf16[8,3,64,704]{3,2,1,0:T(8,128)(2,1)}, bf16[8,3,64,704]{3,2,1,0:T(8,128)(2,1)S(1)}, u32[]{:S(2)}, u32[]{:S(2)}) %collective-permute-start.32) | collective-permute-done | bytes 2162720 | tf_op jit(solution)/shard_map/ppermute | solution.py:242
  538.7 56.0 %collective-permute-done.33 = bf16[8,3,64,704]{3,2,1,0:T(8,128)(2,1)} collective-permute-done((bf16[8,3,64,704]{3,2,1,0:T(8,128)(2,1)}, bf16[8,3,64,704]{3,2,1,0:T(8,128)(2,1)}, u32[]{:S(2)}, u32[]{:S(2)}) %collective-permute-start.33) | collective-permute-done | bytes 2162720 | tf_op jit(solution)/shard_map/ppermute | solution.py:242
  610.4 13.8 %ab.1 = (bf16[1024,768]{1,0:T(8,128)(2,1)}, f32[8,768]{1,0:T(8,128)}) custom-call(s32[4]{0:T(128)} %and_select_fusion.4.first_ref, s32[8,1024]{1,0:T(8,128)} %broadcast_in_dim.62.low_ref, f32[1024,128]{1,0:T(8,128)} %get-tuple-element.134.cos_ref, f32[1024,128]{1,0:T(8,128)} %get-tuple-element.133.s1_ref, f32[1024,128]{1,0:T(8,128)} %get-tuple-element.132.s2_ref, ...), custom_call_target="tpu_custom_call" | custom-call | flops 2684354560 | bytes 6291456 | tf_op jit(solution)/shard_map/ab/pallas_call | solution.py:215
  624.2 7.5 back.3
  666.8 32.0 %collective-permute-done.29 = bf16[8,72,256]{2,1,0:T(8,128)(2,1)S(1)} collective-permute-done((bf16[8,72,256]{2,1,0:T(8,128)(2,1)S(1)}, bf16[8,72,256]{2,1,0:T(8,128)(2,1)S(1)}, u32[]{:S(2)}, u32[]{:S(2)}) %collective-permute-start.29) | collective-permute-done | bytes 294944 | tf_op jit(solution)/shard_map/ppermute | solution.py:242
  718.9 16.5 %all-to-all-done.4.back_ref = bf16[8,72,1024]{2,1,0:T(8,128)(2,1)} async-done(((bf16[8,72,1024]{2,1,0:T(8,128)(2,1)}), bf16[8,72,1024]{2,1,0:T(8,128)(2,1)}, u32[]{:S(2)}, u32[]{:S(2)}) %all-to-all-start.4) | async-done | bytes 1179680 | tf_op jit(solution)/shard_map/all_to_all | solution.py:278
  741.5 38.3 %collective-permute-done.24 = bf16[128,2048]{1,0:T(8,128)(2,1)} collective-permute-done((bf16[128,2048]{1,0:T(8,128)(2,1)}, bf16[128,2048]{1,0:T(8,128)(2,1)}, u32[]{:S(2)}, u32[]{:S(2)}) %collective-permute-start.24) | collective-permute-done | bytes 524320 | tf_op jit(solution)/shard_map/ppermute | solution.py:455
  (336 shorter events, 213.7 us)
Async XLA Ops:
  21.3 92.1 %all-gather.4.cloned.1.call-start = ((), (), s32[]{:S(2)}) async-start(), calls=%async_computation.9 | async-start | bytes 4718592 | tf_op jit(solution)/shard_map/all_gather | solution.py:451
  48.8 139.9 %reduce-scatter.4.cloned.1.call-start = ((), (), s32[]{:S(2)}) async-start(), calls=%async_computation.10 | async-start | bytes 4718592 | tf_op jit(solution)/shard_map/reduce_scatter | solution.py:447
  134.7 268.0 %all-gather.6.cloned.1.call-start = ((), (), s32[]{:S(2)}) async-start(), calls=%async_computation.11 | async-start | bytes 4718592 | tf_op jit(solution)/shard_map/all_gather | solution.py:451
  194.3 69.7 %all-to-all-start.2 = ((bf16[8,128,704]{1,2,0:T(8,128)(2,1)}), bf16[8,128,704]{1,2,0:T(8,128)(2,1)S(1)}, u32[]{:S(2)}, u32[]{:S(2)}) async-start(bf16[8,128,704]{1,2,0:T(8,128)(2,1)} %copy.124), calls=%async_computation.3 | async-start | bytes 2883584 | tf_op jit(solution)/shard_map/all_to_all | solution.py:246
  197.9 87.8 %collective-permute-start.11 = (bf16[128,2048]{1,0:T(8,128)(2,1)S(1)}, bf16[128,2048]{1,0:T(8,128)(2,1)S(1)}, u32[]{:S(2)}, u32[]{:S(2)}) collective-permute-start(bf16[128,2048]{1,0:T(8,128)(2,1)S(1)} %maximum_select_fusion.5.refs_0_), channel_id=1, source_target_pairs={{0,6},{1,7},{2,0},{3,1},{4,2},{5,3},{6,4},{7,5},{8,14},{9,15},{10,... | collective-permute-start | bytes 1572872 | tf_op jit(solution)/shard_map/ppermute | solution.py:455
  264.0 77.2 %collective-permute-start.18 = (bf16[8,128,704]{1,2,0:T(8,128)(2,1)S(1)}, bf16[8,128,704]{1,2,0:T(8,128)(2,1)}, u32[]{:S(2)}, u32[]{:S(2)}) collective-permute-start(bf16[8,128,704]{1,2,0:T(8,128)(2,1)S(1)} %all-to-all-done.2), channel_id=1, source_target_pairs={{0,24},{8,16},{16,8},{24,0},{1,25},{9,17},{17,9},{25,1},{2,26},{10... | collective-permute-start | bytes 4325384 | tf_op jit(solution)/shard_map/ppermute | solution.py:242
  266.4 72.0 %all-to-all-start.3 = ((bf16[8,64,704]{2,1,0:T(8,128)(2,1)}), bf16[8,64,704]{2,1,0:T(8,128)(2,1)}, u32[]{:S(2)}, u32[]{:S(2)}) async-start(bf16[8,64,704]{2,1,0:T(8,128)(2,1)} %bitcast.161), calls=%async_computation.4 | async-start | bytes 1572864 | tf_op jit(solution)/shard_map/all_to_all | solution.py:246
  281.2 191.6 %reduce-scatter.6.cloned.1.call-start = ((), (), s32[]{:S(2)}) async-start(), calls=%async_computation.12 | async-start | bytes 4718592 | tf_op jit(solution)/shard_map/reduce_scatter | solution.py:447
  281.7 54.1 %collective-permute-start.10 = (bf16[128,2048]{1,0:T(8,128)(2,1)S(1)}, bf16[128,2048]{1,0:T(8,128)(2,1)S(1)}, u32[]{:S(2)}, u32[]{:S(2)}) collective-permute-start(bf16[128,2048]{1,0:T(8,128)(2,1)S(1)} %maximum_select_fusion.5.refs_0_), channel_id=1, source_target_pairs={{0,4},{1,5},{2,6},{3,7},{4,0},{5,1},{6,2},{7,3},{8,12},{9,13},{10,... | collective-permute-start | bytes 1572872 | tf_op jit(solution)/shard_map/ppermute | solution.py:455
  284.3 52.2 %collective-permute-start.9 = (bf16[128,2048]{1,0:T(8,128)(2,1)S(1)}, bf16[128,2048]{1,0:T(8,128)(2,1)}, u32[]{:S(2)}, u32[]{:S(2)}) collective-permute-start(bf16[128,2048]{1,0:T(8,128)(2,1)S(1)} %maximum_select_fusion.5.refs_0_), channel_id=1, source_target_pairs={{0,2},{1,3},{2,4},{3,5},{4,6},{5,7},{6,0},{7,1},{8,10},{9,11},{10,... | collective-permute-start | bytes 1572872 | tf_op jit(solution)/shard_map/ppermute | solution.py:455
  285.7 50.7 %collective-permute-start.15 = (bf16[128,2048]{1,0:T(8,128)(2,1)S(1)}, bf16[128,2048]{1,0:T(8,128)(2,1)S(1)}, u32[]{:S(2)}, u32[]{:S(2)}) collective-permute-start(bf16[128,2048]{1,0:T(8,128)(2,1)S(1)} %collective-permute-done.11.refs_3_), channel_id=1, source_target_pairs={{0,1},{1,0},{2,3},{3,2},{4,5},{5,4},{6,7},{7,6},{8,9},{9,8},{10,11... | collective-permute-start | bytes 1572872 | tf_op jit(solution)/shard_map/ppermute | solution.py:459
  285.8 67.3 %collective-permute-start.17 = (bf16[8,128,704]{1,2,0:T(8,128)(2,1)S(1)}, bf16[8,128,704]{1,2,0:T(8,128)(2,1)}, u32[]{:S(2)}, u32[]{:S(2)}) collective-permute-start(bf16[8,128,704]{1,2,0:T(8,128)(2,1)S(1)} %all-to-all-done.2), channel_id=1, source_target_pairs={{0,16},{8,24},{16,0},{24,8},{1,17},{9,25},{17,1},{25,9},{2,18},{10... | collective-permute-start | bytes 4325384 | tf_op jit(solution)/shard_map/ppermute | solution.py:242
  338.4 48.9 %collective-permute-start.21 = (bf16[8,64,704]{2,1,0:T(8,128)(2,1)}, bf16[8,64,704]{2,1,0:T(8,128)(2,1)}, u32[]{:S(2)}, u32[]{:S(2)}) collective-permute-start(bf16[8,64,704]{2,1,0:T(8,128)(2,1)} %all-to-all-done.3.refs_4_.refs_0_), channel_id=1, source_target_pairs={{0,24},{8,16},{16,8},{24,0},{1,25},{9,17},{17,9},{25,1},{2,26},{10... | collective-permute-start | bytes 2162696 | tf_op jit(solution)/shard_map/ppermute | solution.py:242
  339.8 47.5 %collective-permute-start.20 = (bf16[8,64,704]{2,1,0:T(8,128)(2,1)}, bf16[8,64,704]{2,1,0:T(8,128)(2,1)}, u32[]{:S(2)}, u32[]{:S(2)}) collective-permute-start(bf16[8,64,704]{2,1,0:T(8,128)(2,1)} %all-to-all-done.3.refs_4_.refs_0_), channel_id=1, source_target_pairs={{0,16},{8,24},{16,0},{24,8},{1,17},{9,25},{17,1},{25,9},{2,18},{10... | collective-permute-start | bytes 2162696 | tf_op jit(solution)/shard_map/ppermute | solution.py:242
  341.3 61.4 %collective-permute-start.19 = (bf16[8,64,704]{2,1,0:T(8,128)(2,1)}, bf16[8,64,704]{2,1,0:T(8,128)(2,1)}, u32[]{:S(2)}, u32[]{:S(2)}) collective-permute-start(bf16[8,64,704]{2,1,0:T(8,128)(2,1)} %all-to-all-done.3.refs_4_.refs_0_), channel_id=1, source_target_pairs={{0,8},{8,0},{16,24},{24,16},{1,9},{9,1},{17,25},{25,17},{2,10},{10... | collective-permute-start | bytes 2162696 | tf_op jit(solution)/shard_map/ppermute | solution.py:242
  426.4 179.4 %all-gather.8.cloned.1.call-start = ((), (), s32[]{:S(2)}) async-start(), calls=%async_computation.13 | async-start | bytes 4718592 | tf_op jit(solution)/shard_map/all_gather | solution.py:451
  484.4 54.4 %collective-permute-start.32 = (bf16[8,3,64,704]{3,2,1,0:T(8,128)(2,1)}, bf16[8,3,64,704]{3,2,1,0:T(8,128)(2,1)S(1)}, u32[]{:S(2)}, u32[]{:S(2)}) collective-permute-start(bf16[8,3,64,704]{3,2,1,0:T(8,128)(2,1)} %gw.5), channel_id=1, source_target_pairs={{0,8},{8,0},{16,24},{24,16},{1,9},{9,1},{17,25},{25,17},{2,10},{10... | collective-permute-start | bytes 6488072 | tf_op jit(solution)/shard_map/ppermute | solution.py:242
  492.6 102.1 %collective-permute-start.33 = (bf16[8,3,64,704]{3,2,1,0:T(8,128)(2,1)}, bf16[8,3,64,704]{3,2,1,0:T(8,128)(2,1)}, u32[]{:S(2)}, u32[]{:S(2)}) collective-permute-start(bf16[8,3,64,704]{3,2,1,0:T(8,128)(2,1)} %gw.6), channel_id=1, source_target_pairs={{0,16},{8,24},{16,0},{24,8},{1,17},{9,25},{17,1},{25,9},{2,18},{10... | collective-permute-start | bytes 6488072 | tf_op jit(solution)/shard_map/ppermute | solution.py:242
  500.9 93.9 %collective-permute-start.34 = (bf16[8,3,64,704]{3,2,1,0:T(8,128)(2,1)}, bf16[8,3,64,704]{3,2,1,0:T(8,128)(2,1)}, u32[]{:S(2)}, u32[]{:S(2)}) collective-permute-start(bf16[8,3,64,704]{3,2,1,0:T(8,128)(2,1)} %gw.7), channel_id=1, source_target_pairs={{0,24},{8,16},{16,8},{24,0},{1,25},{9,17},{17,9},{25,1},{2,26},{10... | collective-permute-start | bytes 6488072 | tf_op jit(solution)/shard_map/ppermute | solution.py:242
  600.0 100.6 %all-to-all-start.5 = ((bf16[8,192,704]{2,1,0:T(8,128)(2,1)}), bf16[8,192,704]{2,1,0:T(8,128)(2,1)S(1)}, u32[]{:S(2)}, u32[]{:S(2)}) async-start(bf16[8,192,704]{2,1,0:T(8,128)(2,1)} %bitcast.156), calls=%async_computation.8 | async-start | bytes 4718592 | tf_op jit(solution)/shard_map/all_to_all | solution.py:278
  604.1 136.0 %reduce-scatter.8.cloned.1.call-start = ((), (), s32[]{:S(2)}) async-start(), calls=%async_computation.14 | async-start | bytes 4718592 | tf_op jit(solution)/shard_map/reduce_scatter | solution.py:447
  659.0 46.4 %collective-permute-start.22 = (bf16[4,128,2048]{2,1,0:T(8,128)(2,1)}, bf16[4,128,2048]{2,1,0:T(8,128)(2,1)}, u32[]{:S(2)}, u32[]{:S(2)}) collective-permute-start(bf16[4,128,2048]{2,1,0:T(8,128)(2,1)} %dynamic-slice_bitcast_fusion), channel_id=1, source_target_pairs={{0,1},{1,0},{2,3},{3,2},{4,5},{5,4},{6,7},{7,6},{8,9},{9,8},{10,11... | collective-permute-start | bytes 6291464 | tf_op jit(solution)/shard_map/ppermute | solution.py:459
  713.7 66.1 %collective-permute-start.24 = (bf16[128,2048]{1,0:T(8,128)(2,1)}, bf16[128,2048]{1,0:T(8,128)(2,1)}, u32[]{:S(2)}, u32[]{:S(2)}) collective-permute-start(bf16[128,2048]{1,0:T(8,128)(2,1)} %get-tuple-element.74), channel_id=1, source_target_pairs={{0,4},{1,5},{2,6},{3,7},{4,0},{5,1},{6,2},{7,3},{8,12},{9,13},{10,... | collective-permute-start | bytes 1572872 | tf_op jit(solution)/shard_map/ppermute | solution.py:455
  713.7 66.1 %collective-permute-start.23 = (bf16[128,2048]{1,0:T(8,128)(2,1)}, bf16[128,2048]{1,0:T(8,128)(2,1)}, u32[]{:S(2)}, u32[]{:S(2)}) collective-permute-start(bf16[128,2048]{1,0:T(8,128)(2,1)} %get-tuple-element.75), channel_id=1, source_target_pairs={{0,2},{1,3},{2,4},{3,5},{4,6},{5,7},{6,0},{7,1},{8,10},{9,11},{10,... | collective-permute-start | bytes 1572872 | tf_op jit(solution)/shard_map/ppermute | solution.py:455
  (66 other events, 1750.5 us)
Sparse Core Ops, SparseCore 0:
  44.5 49.5 all-gather.3
  134.9 53.7 reduce-scatter.3
  192.6 77.6 all-gather.5
  426.5 46.2 reduce-scatter.5
  477.8 45.3 all-gather.7
  631.8 63.5 reduce-scatter.7

commit v5 on v4

--- a/solution.py
+++ b/solution.py
@@ -490,7 +490,7 @@
     )(spots.astype(jnp.int32), *held, *other)
 
 
-def own_rows_beside(partial, me, groups):
+def own_rows_beside(partial, me, groups, after):
     chips = groups // 2
     tokens = partial.shape[0] // groups
     blocks = partial.reshape(chips, 2, tokens, partial.shape[1])
@@ -499,6 +499,7 @@
     ours = lax.dynamic_index_in_dim(blocks, core, 1, keepdims=False)
     moved = core_swap(theirs, groups)
     pair = (ours.astype(F32) + moved.astype(F32)).astype(BF)
+    pair, _ = lax.optimization_barrier((pair, after))
     chip = me // 2
     moved = [
         chip_shift(lax.dynamic_index_in_dim(pair, (chip + k) % chips, 0, keepdims=False), k, groups)
@@ -580,11 +581,11 @@
     first = (jnp.min(lowest.reshape(length // bq, bq), axis=1) // bq).astype(jnp.int32)
 
     view_gu = jnp.concatenate([by_group(gate_weight), by_group(up_weight)], axis=1)
-    view_gu, view_down, own_up, x_all = lax.optimization_barrier(
-        (view_gu, by_group(down_weight), own_up, x_all)
-    )
-    up_all = every_beside(own_up, me, groups)
-    pieces_gu = spread(take(view_gu))
+    view_down, x_all = lax.optimization_barrier((by_group(down_weight), x_all))
+    taken_gu = take(view_gu)
+    up_sent, unused = lax.optimization_barrier((own_up, taken_gu))
+    up_all = every_beside(up_sent, me, groups)
+    pieces_gu = spread(taken_gu)
     pieces_down = spread(take(view_down))
 
     normed_one, qkv, context, lse = attend_fwd(
@@ -612,10 +613,10 @@
     sum_ffn = reduce_dp(grads).reshape(groups, 3 * rows, -1)
     sum_ffn = send_back(sum_ffn)
 
-    down_sum = own_rows_beside(down_part, me, groups)
     grad_middle = own_up.astype(F32) + norm_back(grad_normed_two, unit_two, factor_two, gain_two)
     grad_mixed = grad_middle.astype(BF)
     grad_mixed = every(grad_mixed)
+    down_sum = own_rows_beside(down_part, me, groups, grad_mixed)
     grad_context = dot(grad_mixed, weight_out, NN).astype(BF)
     grad_projected, bias_part = attend_bwd(qkv, context, lse, grad_context, tables, low8, first, heads, bq)
     dqkv = back_rows(grad_projected[None], 0, pieces_qkv, rows, width, bq)

time: 802 us -> 795 us (level)
  starting transfers between devices: 81.5 us -> 70.2 us
    all_to_all x4, starting transfers between devices: 28.2 us -> 17.6 us  [take(): return lax.all_to_all(view, SEQ, split_axis=0, concat_axis=0, tiled=True)]
    all_to_all x4, waiting for transfers between devices: 92 us -> 102 us  [take(): return lax.all_to_all(view, SEQ, split_axis=0, concat_axis=0, tiled=True)]
  transfers between devices with their start and end apart: 47 -> 47, of which waited for: 23 -> 24; matrix products, arithmetic and copies ran while one was open for 10% -> 10% of each run, Pallas kernels for 9% -> 9%
where the time goes in v5:
time: 795 us; the launch traced here: 787 us
  waiting for transfers between devices  488 us (61%)
  Pallas kernels  109 us (14%)
  starting transfers between devices  70.2 us (9%)
  other arithmetic  45.3 us (6%)
  local copies, waits for them, and re-layouts  38.8 us (5%)
  matrix products  20.5 us (3%)
  between operations  15.4 us (2%)
    ppermute x24, waiting for transfers between devices, swap_dp(): lax.ppermute(values, DP, [(d, d ^ rel) for d in range(lax.axis_size(DP))])  184 us
    all_to_all x4, waiting for transfers between devices, take(): return lax.all_to_all(view, SEQ, split_axis=0, concat_axis=0, tiled=True)  102 us
    reduce_scatter x3, waiting for transfers between devices, own_rows(): lax.psum_scatter(partial.astype(BF), SEQ, scatter_dimension=0, tiled=True)  101 us
    ppermute x6, waiting for transfers between devices, chip_shift(): lax.ppermute(values, SEQ, [(s, (s + 2 * k) % groups) for s in range(group...  86.9 us
    ppermute x24, starting transfers between devices, swap_dp(): lax.ppermute(values, DP, [(d, d ^ rel) for d in range(lax.axis_size(DP))])  32 us
    pallas_call x4, Pallas kernels, ffn_grads(): pl.pallas_call(grad_kernel, grid=(3,), in_specs=[side, side, pl.BlockSpec...  26.9 us
    pallas_call x1, Pallas kernels, ffn_both(): pl.pallas_call(functools.partial(ffn_kernel, len(pair), rows), grid=(leng...  23.6 us
    dot_general x10, matrix products, dot(): lax.dot_general(left, right, (dims, ((), ())), preferred_element_type=F32)  20.5 us
  transfers between devices with their start and end apart: 47, of which 24 were waited for; matrix products, arithmetic and copies ran while one was open for 10% of the time, Pallas kernels for 9%

profile of v5, /device:TPU:0, one launch (start us, length us, event | category | flops | bytes accessed | tf_op | source)
XLA Modules:
  0.0 786.9 jit_solution(17599524933616800728)
XLA Ops:
  22.5 21.8 %all-to-all-done = bf16[8,72,768]{2,1,0:T(8,128)(2,1)S(1)} async-done(((bf16[8,72,768]{2,1,0:T(8,128)(2,1)}), bf16[8,72,768]{2,1,0:T(8,128)(2,1)S(1)}, u32[]{:S(2)}, u32[]{:S(2)}) %all-to-all-start) | async-done | bytes 884768 | tf_op jit(solution)/shard_map/all_to_all | solution.py:246
  48.7 14.2 %all-to-all-done.1 = bf16[8,64,256]{2,1,0:T(8,128)(2,1)S(1)} async-done(((bf16[8,64,256]{2,1,0:T(8,128)(2,1)}), bf16[8,64,256]{2,1,0:T(8,128)(2,1)S(1)}, u32[]{:S(2)}, u32[]{:S(2)}) %all-to-all-start.1) | async-done | bytes 262176 | tf_op jit(solution)/shard_map/all_to_all | solution.py:246
  81.3 8.5 %collective-permute-done.3.refs_5_ = bf16[4,72,768]{2,1,0:T(8,128)(2,1)S(1)} collective-permute-done((bf16[4,72,768]{2,1,0:T(8,128)(2,1)S(1)}, bf16[4,72,768]{2,1,0:T(8,128)(2,1)S(1)}, u32[]{:S(2)}, u32[]{:S(2)}) %collective-permute-start.3) | collective-permute-done | bytes 442400 | tf_op jit(solution)/shard_map/ppermute | solution.py:242
  91.4 9.4 %collective-permute-done.refs_2_ = bf16[4,72,768]{2,1,0:T(8,128)(2,1)} collective-permute-done((bf16[4,72,768]{2,1,0:T(8,128)(2,1)S(1)}, bf16[4,72,768]{2,1,0:T(8,128)(2,1)}, u32[]{:S(2)}, u32[]{:S(2)}) %collective-permute-start) | collective-permute-done | bytes 442400 | tf_op jit(solution)/shard_map/ppermute | solution.py:242
  113.8 16.4 %af.1 = (bf16[1024,2048]{1,0:T(8,128)(2,1)}, bf16[1024,768]{1,0:T(8,128)(2,1)}, bf16[1024,256]{1,0:T(8,128)(2,1)}, f32[8,1024]{1,0:T(8,128)}) custom-call(s32[4]{0:T(128)} %and_select_fusion.4.first_ref, s32[8,1024]{1,0:T(8,128)} %broadcast_in_dim.62.low_ref, f32[1024,128]{1,0:T(8,128)} %get-tuple-element.134.cos_ref, ...), custom_call_target="tpu_custom_call" | custom-call | flops 4294967296 | bytes 14680064 | tf_op jit(solution)/shard_map/af/pallas_call | solution.py:138
  135.0 53.2 %reduce-scatter.4.cloned.1.call-done = bf16[128,2048]{1,0:T(8,128)(2,1)} async-done(((bf16[1024,2048]{1,0:T(8,128)(2,1)}), bf16[128,2048]{1,0:T(8,128)(2,1)}) %reduce-scatter.4.cloned.1.call-update) | async-done | bytes 524304 | tf_op jit(solution)/shard_map/reduce_scatter | solution.py:447
  201.4 65.5 %all-to-all-done.2 = bf16[8,128,704]{1,2,0:T(8,128)(2,1)S(1)} async-done(((bf16[8,128,704]{1,2,0:T(8,128)(2,1)}), bf16[8,128,704]{1,2,0:T(8,128)(2,1)S(1)}, u32[]{:S(2)}, u32[]{:S(2)}) %all-to-all-start.2) | async-done | bytes 1441824 | tf_op jit(solution)/shard_map/all_to_all | solution.py:246
  284.3 44.9 %collective-permute-done.10.refs_2_ = bf16[128,2048]{1,0:T(8,128)(2,1)S(1)} collective-permute-done((bf16[128,2048]{1,0:T(8,128)(2,1)S(1)}, bf16[128,2048]{1,0:T(8,128)(2,1)S(1)}, u32[]{:S(2)}, u32[]{:S(2)}) %collective-permute-start.10) | collective-permute-done | bytes 524320 | tf_op jit(solution)/shard_map/ppermute | solution.py:455
  350.0 13.7 %collective-permute-done.16 = bf16[8,128,704]{1,2,0:T(8,128)(2,1)} collective-permute-done((bf16[8,128,704]{1,2,0:T(8,128)(2,1)S(1)}, bf16[8,128,704]{1,2,0:T(8,128)(2,1)}, u32[]{:S(2)}, u32[]{:S(2)}) %collective-permute-start.16) | collective-permute-done | bytes 1441824 | tf_op jit(solution)/shard_map/ppermute | solution.py:242
  366.3 15.3 %collective-permute-done.21.refs_7_.refs_3_ = bf16[8,64,704]{2,1,0:T(8,128)(2,1)} collective-permute-done((bf16[8,64,704]{2,1,0:T(8,128)(2,1)}, bf16[8,64,704]{2,1,0:T(8,128)(2,1)}, u32[]{:S(2)}, u32[]{:S(2)}) %collective-permute-start.21) | collective-permute-done | bytes 720928 | tf_op jit(solution)/shard_map/ppermute | solution.py:242
  381.5 14.4 %collective-permute-done.19.refs_5_.refs_1_ = bf16[8,64,704]{2,1,0:T(8,128)(2,1)} collective-permute-done((bf16[8,64,704]{2,1,0:T(8,128)(2,1)}, bf16[8,64,704]{2,1,0:T(8,128)(2,1)}, u32[]{:S(2)}, u32[]{:S(2)}) %collective-permute-start.19) | collective-permute-done | bytes 720928 | tf_op jit(solution)/shard_map/ppermute | solution.py:242
  396.0 23.6 %ffn.1 = (bf16[3,1024,704]{2,1,0:T(8,128)(2,1)}, bf16[1024,2048]{1,0:T(8,128)(2,1)}) custom-call(bf16[1024,2048]{1,0:T(8,128)(2,1)} %all-gather.6.cloned.1.call-done.n_ref, bf16[1024,2048]{1,0:T(8,128)(2,1)} %place.1.u_ref, bf16[8,128,704]{2,1,0:T(8,128)(2,1)} %copy.125.refs_0_, bf16[8,128,704]{2,1,0:T(8,128)(2,1)} %copy.126.refs_1_, ...), custom_call_target="tpu_custom_call" | custom-call | flops 14763950080 | bytes 21233664 | tf_op jit(solution)/shard_map/ffn/pallas_call | solution.py:319
  419.9 47.8 %reduce-scatter.6.cloned.1.call-done = bf16[128,2048]{1,0:T(8,128)(2,1)} async-done(((bf16[1024,2048]{1,0:T(8,128)(2,1)}), bf16[128,2048]{1,0:T(8,128)(2,1)}) %reduce-scatter.6.cloned.1.call-update) | async-done | bytes 524304 | tf_op jit(solution)/shard_map/reduce_scatter | solution.py:447
  480.8 6.7 gw.6
  489.0 6.8 gw.7
  496.3 6.7 gw.4
  503.0 7.4 back.2
  513.8 19.9 %collective-permute-done.32 = bf16[8,3,64,704]{3,2,1,0:T(8,128)(2,1)S(1)} collective-permute-done((bf16[8,3,64,704]{3,2,1,0:T(8,128)(2,1)}, bf16[8,3,64,704]{3,2,1,0:T(8,128)(2,1)S(1)}, u32[]{:S(2)}, u32[]{:S(2)}) %collective-permute-start.32) | collective-permute-done | bytes 2162720 | tf_op jit(solution)/shard_map/ppermute | solution.py:242
  533.6 56.0 %collective-permute-done.33 = bf16[8,3,64,704]{3,2,1,0:T(8,128)(2,1)} collective-permute-done((bf16[8,3,64,704]{3,2,1,0:T(8,128)(2,1)}, bf16[8,3,64,704]{3,2,1,0:T(8,128)(2,1)}, u32[]{:S(2)}, u32[]{:S(2)}) %collective-permute-start.33) | collective-permute-done | bytes 2162720 | tf_op jit(solution)/shard_map/ppermute | solution.py:242
  605.3 13.8 %ab.1 = (bf16[1024,768]{1,0:T(8,128)(2,1)}, f32[8,768]{1,0:T(8,128)}) custom-call(s32[4]{0:T(128)} %and_select_fusion.4.first_ref, s32[8,1024]{1,0:T(8,128)} %broadcast_in_dim.62.low_ref, f32[1024,128]{1,0:T(8,128)} %get-tuple-element.134.cos_ref, f32[1024,128]{1,0:T(8,128)} %get-tuple-element.133.s1_ref, f32[1024,128]{1,0:T(8,128)} %get-tuple-element.132.s2_ref, ...), custom_call_target="tpu_custom_call" | custom-call | flops 2684354560 | bytes 6291456 | tf_op jit(solution)/shard_map/ab/pallas_call | solution.py:215
  619.1 7.5 back.3
  661.6 32.0 %collective-permute-done.29 = bf16[8,72,256]{2,1,0:T(8,128)(2,1)S(1)} collective-permute-done((bf16[8,72,256]{2,1,0:T(8,128)(2,1)S(1)}, bf16[8,72,256]{2,1,0:T(8,128)(2,1)S(1)}, u32[]{:S(2)}, u32[]{:S(2)}) %collective-permute-start.29) | collective-permute-done | bytes 294944 | tf_op jit(solution)/shard_map/ppermute | solution.py:242
  716.7 13.6 %all-to-all-done.4.back_ref = bf16[8,72,1024]{2,1,0:T(8,128)(2,1)} async-done(((bf16[8,72,1024]{2,1,0:T(8,128)(2,1)}), bf16[8,72,1024]{2,1,0:T(8,128)(2,1)}, u32[]{:S(2)}, u32[]{:S(2)}) %all-to-all-start.4) | async-done | bytes 1179680 | tf_op jit(solution)/shard_map/all_to_all | solution.py:278
  736.4 38.3 %collective-permute-done.24 = bf16[128,2048]{1,0:T(8,128)(2,1)} collective-permute-done((bf16[128,2048]{1,0:T(8,128)(2,1)}, bf16[128,2048]{1,0:T(8,128)(2,1)}, u32[]{:S(2)}, u32[]{:S(2)}) %collective-permute-start.24) | collective-permute-done | bytes 524320 | tf_op jit(solution)/shard_map/ppermute | solution.py:455
  (336 shorter events, 214.0 us)
Async XLA Ops:
  21.3 91.9 %all-gather.4.cloned.1.call-start = ((), (), s32[]{:S(2)}) async-start(), calls=%async_computation.9 | async-start | bytes 4718592 | tf_op jit(solution)/shard_map/all_gather | solution.py:451
  48.6 139.5 %reduce-scatter.4.cloned.1.call-start = ((), (), s32[]{:S(2)}) async-start(), calls=%async_computation.10 | async-start | bytes 4718592 | tf_op jit(solution)/shard_map/reduce_scatter | solution.py:447
  134.6 261.4 %all-gather.6.cloned.1.call-start = ((), (), s32[]{:S(2)}) async-start(), calls=%async_computation.11 | async-start | bytes 4718592 | tf_op jit(solution)/shard_map/all_gather | solution.py:451
  197.4 69.4 %all-to-all-start.2 = ((bf16[8,128,704]{1,2,0:T(8,128)(2,1)}), bf16[8,128,704]{1,2,0:T(8,128)(2,1)S(1)}, u32[]{:S(2)}, u32[]{:S(2)}) async-start(bf16[8,128,704]{1,2,0:T(8,128)(2,1)} %copy.124), calls=%async_computation.3 | async-start | bytes 2883584 | tf_op jit(solution)/shard_map/all_to_all | solution.py:246
  267.8 67.2 %collective-permute-start.18 = (bf16[8,128,704]{1,2,0:T(8,128)(2,1)S(1)}, bf16[8,128,704]{1,2,0:T(8,128)(2,1)}, u32[]{:S(2)}, u32[]{:S(2)}) collective-permute-start(bf16[8,128,704]{1,2,0:T(8,128)(2,1)S(1)} %all-to-all-done.2), channel_id=1, source_target_pairs={{0,24},{8,16},{16,8},{24,0},{1,25},{9,17},{17,9},{25,1},{2,26},{10... | collective-permute-start | bytes 4325384 | tf_op jit(solution)/shard_map/ppermute | solution.py:242
  270.3 62.4 %all-to-all-start.3 = ((bf16[8,64,704]{2,1,0:T(8,128)(2,1)}), bf16[8,64,704]{2,1,0:T(8,128)(2,1)}, u32[]{:S(2)}, u32[]{:S(2)}) async-start(bf16[8,64,704]{2,1,0:T(8,128)(2,1)} %bitcast.161), calls=%async_computation.4 | async-start | bytes 1572864 | tf_op jit(solution)/shard_map/all_to_all | solution.py:246
  274.6 193.1 %reduce-scatter.6.cloned.1.call-start = ((), (), s32[]{:S(2)}) async-start(), calls=%async_computation.12 | async-start | bytes 4718592 | tf_op jit(solution)/shard_map/reduce_scatter | solution.py:447
  274.9 54.2 %collective-permute-start.10 = (bf16[128,2048]{1,0:T(8,128)(2,1)S(1)}, bf16[128,2048]{1,0:T(8,128)(2,1)S(1)}, u32[]{:S(2)}, u32[]{:S(2)}) collective-permute-start(bf16[128,2048]{1,0:T(8,128)(2,1)S(1)} %maximum_select_fusion.5.refs_0_), channel_id=1, source_target_pairs={{0,4},{1,5},{2,6},{3,7},{4,0},{5,1},{6,2},{7,3},{8,12},{9,13},{10,... | collective-permute-start | bytes 1572872 | tf_op jit(solution)/shard_map/ppermute | solution.py:455
  277.5 53.2 %collective-permute-start.9 = (bf16[128,2048]{1,0:T(8,128)(2,1)S(1)}, bf16[128,2048]{1,0:T(8,128)(2,1)}, u32[]{:S(2)}, u32[]{:S(2)}) collective-permute-start(bf16[128,2048]{1,0:T(8,128)(2,1)S(1)} %maximum_select_fusion.5.refs_0_), channel_id=1, source_target_pairs={{0,2},{1,3},{2,4},{3,5},{4,6},{5,7},{6,0},{7,1},{8,10},{9,11},{10,... | collective-permute-start | bytes 1572872 | tf_op jit(solution)/shard_map/ppermute | solution.py:455
  282.7 48.0 %collective-permute-start.15 = (bf16[128,2048]{1,0:T(8,128)(2,1)S(1)}, bf16[128,2048]{1,0:T(8,128)(2,1)S(1)}, u32[]{:S(2)}, u32[]{:S(2)}) collective-permute-start(bf16[128,2048]{1,0:T(8,128)(2,1)S(1)} %collective-permute-done.11.refs_3_), channel_id=1, source_target_pairs={{0,1},{1,0},{2,3},{3,2},{4,5},{5,4},{6,7},{7,6},{8,9},{9,8},{10,11... | collective-permute-start | bytes 1572872 | tf_op jit(solution)/shard_map/ppermute | solution.py:459
  282.7 64.7 %collective-permute-start.17 = (bf16[8,128,704]{1,2,0:T(8,128)(2,1)S(1)}, bf16[8,128,704]{1,2,0:T(8,128)(2,1)}, u32[]{:S(2)}, u32[]{:S(2)}) collective-permute-start(bf16[8,128,704]{1,2,0:T(8,128)(2,1)S(1)} %all-to-all-done.2), channel_id=1, source_target_pairs={{0,16},{8,24},{16,0},{24,8},{1,17},{9,25},{17,1},{25,9},{2,18},{10... | collective-permute-start | bytes 4325384 | tf_op jit(solution)/shard_map/ppermute | solution.py:242
  332.7 48.8 %collective-permute-start.21 = (bf16[8,64,704]{2,1,0:T(8,128)(2,1)}, bf16[8,64,704]{2,1,0:T(8,128)(2,1)}, u32[]{:S(2)}, u32[]{:S(2)}) collective-permute-start(bf16[8,64,704]{2,1,0:T(8,128)(2,1)} %all-to-all-done.3.refs_4_.refs_0_), channel_id=1, source_target_pairs={{0,24},{8,16},{16,8},{24,0},{1,25},{9,17},{17,9},{25,1},{2,26},{10... | collective-permute-start | bytes 2162696 | tf_op jit(solution)/shard_map/ppermute | solution.py:242
  334.2 47.3 %collective-permute-start.20 = (bf16[8,64,704]{2,1,0:T(8,128)(2,1)}, bf16[8,64,704]{2,1,0:T(8,128)(2,1)}, u32[]{:S(2)}, u32[]{:S(2)}) collective-permute-start(bf16[8,64,704]{2,1,0:T(8,128)(2,1)} %all-to-all-done.3.refs_4_.refs_0_), channel_id=1, source_target_pairs={{0,16},{8,24},{16,0},{24,8},{1,17},{9,25},{17,1},{25,9},{2,18},{10... | collective-permute-start | bytes 2162696 | tf_op jit(solution)/shard_map/ppermute | solution.py:242
  335.0 61.0 %collective-permute-start.19 = (bf16[8,64,704]{2,1,0:T(8,128)(2,1)}, bf16[8,64,704]{2,1,0:T(8,128)(2,1)}, u32[]{:S(2)}, u32[]{:S(2)}) collective-permute-start(bf16[8,64,704]{2,1,0:T(8,128)(2,1)} %all-to-all-done.3.refs_4_.refs_0_), channel_id=1, source_target_pairs={{0,8},{8,0},{16,24},{24,16},{1,9},{9,1},{17,25},{25,17},{2,10},{10... | collective-permute-start | bytes 2162696 | tf_op jit(solution)/shard_map/ppermute | solution.py:242
  419.6 181.1 %all-gather.8.cloned.1.call-start = ((), (), s32[]{:S(2)}) async-start(), calls=%async_computation.13 | async-start | bytes 4718592 | tf_op jit(solution)/shard_map/all_gather | solution.py:451
  479.3 54.4 %collective-permute-start.32 = (bf16[8,3,64,704]{3,2,1,0:T(8,128)(2,1)}, bf16[8,3,64,704]{3,2,1,0:T(8,128)(2,1)S(1)}, u32[]{:S(2)}, u32[]{:S(2)}) collective-permute-start(bf16[8,3,64,704]{3,2,1,0:T(8,128)(2,1)} %gw.5), channel_id=1, source_target_pairs={{0,8},{8,0},{16,24},{24,16},{1,9},{9,1},{17,25},{25,17},{2,10},{10... | collective-permute-start | bytes 6488072 | tf_op jit(solution)/shard_map/ppermute | solution.py:242
  487.5 102.1 %collective-permute-start.33 = (bf16[8,3,64,704]{3,2,1,0:T(8,128)(2,1)}, bf16[8,3,64,704]{3,2,1,0:T(8,128)(2,1)}, u32[]{:S(2)}, u32[]{:S(2)}) collective-permute-start(bf16[8,3,64,704]{3,2,1,0:T(8,128)(2,1)} %gw.6), channel_id=1, source_target_pairs={{0,16},{8,24},{16,0},{24,8},{1,17},{9,25},{17,1},{25,9},{2,18},{10... | collective-permute-start | bytes 6488072 | tf_op jit(solution)/shard_map/ppermute | solution.py:242
  495.7 93.9 %collective-permute-start.34 = (bf16[8,3,64,704]{3,2,1,0:T(8,128)(2,1)}, bf16[8,3,64,704]{3,2,1,0:T(8,128)(2,1)}, u32[]{:S(2)}, u32[]{:S(2)}) collective-permute-start(bf16[8,3,64,704]{3,2,1,0:T(8,128)(2,1)} %gw.7), channel_id=1, source_target_pairs={{0,24},{8,16},{16,8},{24,0},{1,25},{9,17},{17,9},{25,1},{2,26},{10... | collective-permute-start | bytes 6488072 | tf_op jit(solution)/shard_map/ppermute | solution.py:242
  594.9 100.5 %all-to-all-start.5 = ((bf16[8,192,704]{2,1,0:T(8,128)(2,1)}), bf16[8,192,704]{2,1,0:T(8,128)(2,1)S(1)}, u32[]{:S(2)}, u32[]{:S(2)}) async-start(bf16[8,192,704]{2,1,0:T(8,128)(2,1)} %bitcast.156), calls=%async_computation.8 | async-start | bytes 4718592 | tf_op jit(solution)/shard_map/all_to_all | solution.py:278
  599.0 135.9 %reduce-scatter.8.cloned.1.call-start = ((), (), s32[]{:S(2)}) async-start(), calls=%async_computation.14 | async-start | bytes 4718592 | tf_op jit(solution)/shard_map/reduce_scatter | solution.py:447
  649.9 43.9 %collective-permute-start.26 = (bf16[8,64,768]{2,1,0:T(8,128)(2,1)S(1)}, bf16[8,64,768]{2,1,0:T(8,128)(2,1)S(1)}, u32[]{:S(2)}, u32[]{:S(2)}) collective-permute-start(bf16[8,64,768]{2,1,0:T(8,128)(2,1)S(1)} %bitcast.198), channel_id=1, source_target_pairs={{0,8},{8,0},{16,24},{24,16},{1,9},{9,1},{17,25},{25,17},{2,10},{10... | collective-permute-start | bytes 2359304 | tf_op jit(solution)/shard_map/ppermute | solution.py:242
  653.9 46.4 %collective-permute-start.22 = (bf16[4,128,2048]{2,1,0:T(8,128)(2,1)}, bf16[4,128,2048]{2,1,0:T(8,128)(2,1)}, u32[]{:S(2)}, u32[]{:S(2)}) collective-permute-start(bf16[4,128,2048]{2,1,0:T(8,128)(2,1)} %dynamic-slice_bitcast_fusion), channel_id=1, source_target_pairs={{0,1},{1,0},{2,3},{3,2},{4,5},{5,4},{6,7},{7,6},{8,9},{9,8},{10,11... | collective-permute-start | bytes 6291464 | tf_op jit(solution)/shard_map/ppermute | solution.py:459
  715.6 59.1 %collective-permute-start.24 = (bf16[128,2048]{1,0:T(8,128)(2,1)}, bf16[128,2048]{1,0:T(8,128)(2,1)}, u32[]{:S(2)}, u32[]{:S(2)}) collective-permute-start(bf16[128,2048]{1,0:T(8,128)(2,1)} %get-tuple-element.74), channel_id=1, source_target_pairs={{0,4},{1,5},{2,6},{3,7},{4,0},{5,1},{6,2},{7,3},{8,12},{9,13},{10,... | collective-permute-start | bytes 1572872 | tf_op jit(solution)/shard_map/ppermute | solution.py:455
  715.6 59.1 %collective-permute-start.23 = (bf16[128,2048]{1,0:T(8,128)(2,1)}, bf16[128,2048]{1,0:T(8,128)(2,1)}, u32[]{:S(2)}, u32[]{:S(2)}) collective-permute-start(bf16[128,2048]{1,0:T(8,128)(2,1)} %get-tuple-element.75), channel_id=1, source_target_pairs={{0,2},{1,3},{2,4},{3,5},{4,6},{5,7},{6,0},{7,1},{8,10},{9,11},{10,... | collective-permute-start | bytes 1572872 | tf_op jit(solution)/shard_map/ppermute | solution.py:455
  (66 other events, 1659.5 us)
Sparse Core Ops, SparseCore 0:
  44.5 49.3 all-gather.3
  134.7 53.3 reduce-scatter.3
  192.1 76.2 all-gather.5
  419.8 47.9 reduce-scatter.5
  472.7 45.3 all-gather.7
  626.7 63.5 reduce-scatter.7

commit v6 on v3

--- a/solution.py
+++ b/solution.py
@@ -459,7 +459,7 @@
     return lax.ppermute(values, SEQ, [(s, s ^ 1) for s in range(groups)])
 
 
-def own_rows_beside(partial, me, groups):
+def own_rows_beside(partial, me, groups, after):
     chips = groups // 2
     tokens = partial.shape[0] // groups
     blocks = partial.reshape(chips, 2, tokens, partial.shape[1])
@@ -468,6 +468,7 @@
     ours = lax.dynamic_index_in_dim(blocks, core, 1, keepdims=False)
     moved = core_swap(theirs, groups)
     pair = (ours.astype(F32) + moved.astype(F32)).astype(BF)
+    pair, _ = lax.optimization_barrier((pair, after))
     chip = me // 2
     moved = [
         chip_shift(lax.dynamic_index_in_dim(pair, (chip + k) % chips, 0, keepdims=False), k, groups)
@@ -505,6 +506,7 @@
 
     own = relate(inputs, mine, copies, 1)
     own_up = relate(upstream, mine, copies, 1)
+    up_all = every(own_up)
 
     def by_group(weight, parts=1):
         cols = weight.shape[1] // (parts * groups)
@@ -529,8 +531,6 @@
     taken, own = lax.optimization_barrier((take(view_qkv), own))
     x_all = every(own)
     pieces_qkv = [piece for pair in spread_halves(taken) for piece in pair]
-    own_up, unused = lax.optimization_barrier((own_up, taken))
-    up_all = every(own_up)
     weight_out = stack_rows(spread(take(by_group(out_weight))), 0, rows)
     spot = taken[:, rows, 4 * rows + nbias : 4 * rows + nbias + 2 * tokens]
     positions = (
@@ -582,8 +582,8 @@
 
     grad_middle = own_up.astype(F32) + norm_back(grad_normed_two, unit_two, factor_two, gain_two)
     grad_mixed = grad_middle.astype(BF)
-    down_sum = own_rows_beside(down_part, me, groups)
     grad_mixed = every(grad_mixed)
+    down_sum = own_rows_beside(down_part, me, groups, grad_mixed)
     grad_context = dot(grad_mixed, weight_out, NN).astype(BF)
     grad_projected, bias_part = attend_bwd(qkv, context, lse, grad_context, tables, low8, first, heads, bq)
     dqkv = back_rows(grad_projected[None], 0, pieces_qkv, rows, width, bq)

time: 767 us -> 767 us (level)
  no operation moved by 1% of the time
where the time goes in v6:
time: 767 us; the launch traced here: 757 us
  waiting for transfers between devices  400 us (52%)
  Pallas kernels  102 us (13%)
  blocking collectives  70.1 us (9%)
  starting transfers between devices  57.9 us (8%)
  other arithmetic  46.9 us (6%)
  local copies, waits for them, and re-layouts  44.2 us (6%)
  matrix products  20.4 us (3%)
  between operations  15.1 us (2%)
    ppermute x24, waiting for transfers between devices, swap_dp(): lax.ppermute(values, DP, [(d, d ^ rel) for d in range(lax.axis_size(DP))])  186 us
    reduce_scatter x3, waiting for transfers between devices, own_rows(): lax.psum_scatter(partial.astype(BF), SEQ, scatter_dimension=0, tiled=True)  96.4 us
    all_to_all x1, blocking collectives, take(): return lax.all_to_all(view, SEQ, split_axis=0, concat_axis=0, tiled=True)  70.1 us
    all_to_all x3, waiting for transfers between devices, take(): return lax.all_to_all(view, SEQ, split_axis=0, concat_axis=0, tiled=True)  65.5 us
    ppermute x3, waiting for transfers between devices, chip_shift(): lax.ppermute(values, SEQ, [(s, (s + 2 * k) % groups) for s in range(group...  38.3 us
    ppermute x24, starting transfers between devices, swap_dp(): lax.ppermute(values, DP, [(d, d ^ rel) for d in range(lax.axis_size(DP))])  29.7 us
    pallas_call x4, Pallas kernels, ffn_grads(): pl.pallas_call(grad_kernel, grid=(3,), in_specs=[side, side, pl.BlockSpec...  26.9 us
    pallas_call x1, Pallas kernels, ffn_both(): pl.pallas_call(functools.partial(ffn_kernel, len(pair), rows), grid=(leng...  23.5 us
  transfers between devices with their start and end apart: 40, of which 22 were waited for; matrix products, arithmetic and copies ran while one was open for 11% of the time, Pallas kernels for 8%

profile of v6, /device:TPU:0, one launch (start us, length us, event | category | flops | bytes accessed | tf_op | source)
XLA Modules:
  0.0 756.7 jit_solution(18367297289272348158)
XLA Ops:
  22.5 21.8 %all-to-all-done = bf16[8,72,768]{2,1,0:T(8,128)(2,1)S(1)} async-done(((bf16[8,72,768]{2,1,0:T(8,128)(2,1)}), bf16[8,72,768]{2,1,0:T(8,128)(2,1)S(1)}, u32[]{:S(2)}, u32[]{:S(2)}) %all-to-all-start) | async-done | bytes 884768 | tf_op jit(solution)/shard_map/all_to_all | solution.py:246
  56.2 8.1 %all-to-all-done.1 = bf16[8,64,256]{2,1,0:T(8,128)(2,1)S(1)} async-done(((bf16[8,64,256]{2,1,0:T(8,128)(2,1)}), bf16[8,64,256]{2,1,0:T(8,128)(2,1)S(1)}, u32[]{:S(2)}, u32[]{:S(2)}) %all-to-all-start.1) | async-done | bytes 262176 | tf_op jit(solution)/shard_map/all_to_all | solution.py:246
  85.0 8.9 %collective-permute-done.3.refs_5_ = bf16[4,72,768]{2,1,0:T(8,128)(2,1)} collective-permute-done((bf16[4,72,768]{2,1,0:T(8,128)(2,1)}, bf16[4,72,768]{2,1,0:T(8,128)(2,1)}, u32[]{:S(2)}, u32[]{:S(2)}) %collective-permute-start.3) | collective-permute-done | bytes 442400 | tf_op jit(solution)/shard_map/ppermute | solution.py:242
  95.4 9.4 %collective-permute-done.refs_2_ = bf16[4,72,768]{2,1,0:T(8,128)(2,1)} collective-permute-done((bf16[4,72,768]{2,1,0:T(8,128)(2,1)}, bf16[4,72,768]{2,1,0:T(8,128)(2,1)}, u32[]{:S(2)}, u32[]{:S(2)}) %collective-permute-start) | collective-permute-done | bytes 442400 | tf_op jit(solution)/shard_map/ppermute | solution.py:242
  119.1 16.4 %af.1 = (bf16[1024,2048]{1,0:T(8,128)(2,1)}, bf16[1024,768]{1,0:T(8,128)(2,1)}, bf16[1024,256]{1,0:T(8,128)(2,1)}, f32[8,1024]{1,0:T(8,128)}) custom-call(s32[4]{0:T(128)} %and_select_fusion.2.first_ref, s32[8,1024]{1,0:T(8,128)} %broadcast_in_dim.30.low_ref, f32[1024,128]{1,0:T(8,128)} %get-tuple-element.134.cos_ref, ...), custom_call_target="tpu_custom_call" | custom-call | flops 4294967296 | bytes 14680064 | tf_op jit(solution)/shard_map/af/pallas_call | solution.py:138
  142.4 48.3 %reduce-scatter.4.cloned.1.call-done = bf16[128,2048]{1,0:T(8,128)(2,1)} async-done(((bf16[1024,2048]{1,0:T(8,128)(2,1)}), bf16[128,2048]{1,0:T(8,128)(2,1)}) %reduce-scatter.4.cloned.1.call-update) | async-done | bytes 524304 | tf_op jit(solution)/shard_map/reduce_scatter | solution.py:447
  196.4 70.1 %all_to_all.30 = bf16[8,128,704]{1,2,0:T(8,128)(2,1)S(1)} all-to-all(bf16[8,128,704]{1,2,0:T(8,128)(2,1)} %copy.124), channel_id=1, replica_groups=mesh['dp'=4,'seq'=8] {'seq'}, dimensions={0} | all-to-all | bytes 2883584 | tf_op jit(solution)/shard_map/all_to_all | solution.py:246
  273.6 35.6 %all-to-all-done.3.refs_4_.refs_0_ = bf16[8,64,704]{2,1,0:T(8,128)(2,1)S(1)} async-done(((bf16[8,64,704]{2,1,0:T(8,128)(2,1)}), bf16[8,64,704]{2,1,0:T(8,128)(2,1)S(1)}, u32[]{:S(2)}, u32[]{:S(2)}) %all-to-all-start.3) | async-done | bytes 720928 | tf_op jit(solution)/shard_map/all_to_all | solution.py:246
  316.9 16.0 %collective-permute-done.10 = bf16[8,128,704]{1,2,0:T(8,128)(2,1)} collective-permute-done((bf16[8,128,704]{1,2,0:T(8,128)(2,1)S(1)}, bf16[8,128,704]{1,2,0:T(8,128)(2,1)}, u32[]{:S(2)}, u32[]{:S(2)}) %collective-permute-start.10) | collective-permute-done | bytes 1441824 | tf_op jit(solution)/shard_map/ppermute | solution.py:242
  338.1 11.7 %collective-permute-done.14.refs_7_.refs_3_ = bf16[8,64,704]{2,1,0:T(8,128)(2,1)} collective-permute-done((bf16[8,64,704]{2,1,0:T(8,128)(2,1)S(1)}, bf16[8,64,704]{2,1,0:T(8,128)(2,1)}, u32[]{:S(2)}, u32[]{:S(2)}) %collective-permute-start.14) | collective-permute-done | bytes 720928 | tf_op jit(solution)/shard_map/ppermute | solution.py:242
  349.8 15.9 %collective-permute-done.13.refs_6_.refs_2_ = bf16[8,64,704]{2,1,0:T(8,128)(2,1)} collective-permute-done((bf16[8,64,704]{2,1,0:T(8,128)(2,1)S(1)}, bf16[8,64,704]{2,1,0:T(8,128)(2,1)}, u32[]{:S(2)}, u32[]{:S(2)}) %collective-permute-start.13) | collective-permute-done | bytes 720928 | tf_op jit(solution)/shard_map/ppermute | solution.py:242
  365.8 23.5 %ffn.1 = (bf16[3,1024,704]{2,1,0:T(8,128)(2,1)}, bf16[1024,2048]{1,0:T(8,128)(2,1)}) custom-call(bf16[1024,2048]{1,0:T(8,128)(2,1)} %all-gather.7.cloned.1.call-done.n_ref, bf16[1024,2048]{1,0:T(8,128)(2,1)} %all-gather.9.cloned.1.call-done.u_ref, bf16[8,128,704]{2,1,0:T(8,128)(2,1)} %copy.125.refs_0_, bf16[8,128,704]{2,1,0:T(8,128)(2,1)} %copy.126.refs_1_, ...), custom_call_target="tpu_custom_call" | custom-call | flops 14763950080 | bytes 21233664 | tf_op jit(solution)/shard_map/ffn/pallas_call | solution.py:319
  389.6 48.1 %reduce-scatter.6.cloned.1.call-done = bf16[128,2048]{1,0:T(8,128)(2,1)} async-done(((bf16[1024,2048]{1,0:T(8,128)(2,1)}), bf16[128,2048]{1,0:T(8,128)(2,1)}) %reduce-scatter.6.cloned.1.call-update) | async-done | bytes 524304 | tf_op jit(solution)/shard_map/reduce_scatter | solution.py:447
  442.5 6.7 gw.5
  450.7 6.8 gw.6
  458.9 6.8 gw.7
  472.9 7.4 back.2
  483.7 19.9 %collective-permute-done.25 = bf16[8,3,64,704]{3,2,1,0:T(8,128)(2,1)S(1)} collective-permute-done((bf16[8,3,64,704]{3,2,1,0:T(8,128)(2,1)}, bf16[8,3,64,704]{3,2,1,0:T(8,128)(2,1)S(1)}, u32[]{:S(2)}, u32[]{:S(2)}) %collective-permute-start.25) | collective-permute-done | bytes 2162720 | tf_op jit(solution)/shard_map/ppermute | solution.py:242
  503.5 56.0 %collective-permute-done.26 = bf16[8,3,64,704]{3,2,1,0:T(8,128)(2,1)} collective-permute-done((bf16[8,3,64,704]{3,2,1,0:T(8,128)(2,1)}, bf16[8,3,64,704]{3,2,1,0:T(8,128)(2,1)}, u32[]{:S(2)}, u32[]{:S(2)}) %collective-permute-start.26) | collective-permute-done | bytes 2162720 | tf_op jit(solution)/shard_map/ppermute | solution.py:242
  575.2 13.8 %ab.1 = (bf16[1024,768]{1,0:T(8,128)(2,1)}, f32[8,768]{1,0:T(8,128)}) custom-call(s32[4]{0:T(128)} %and_select_fusion.2.first_ref, s32[8,1024]{1,0:T(8,128)} %broadcast_in_dim.30.low_ref, f32[1024,128]{1,0:T(8,128)} %get-tuple-element.134.cos_ref, f32[1024,128]{1,0:T(8,128)} %get-tuple-element.133.s1_ref, f32[1024,128]{1,0:T(8,128)} %get-tuple-element.132.s2_ref, ...), custom_call_target="tpu_custom_call" | custom-call | flops 2684354560 | bytes 6291456 | tf_op jit(solution)/shard_map/ab/pallas_call | solution.py:215
  589.0 7.5 back.3
  631.5 32.1 %collective-permute-done.22 = bf16[8,72,256]{2,1,0:T(8,128)(2,1)S(1)} collective-permute-done((bf16[8,72,256]{2,1,0:T(8,128)(2,1)S(1)}, bf16[8,72,256]{2,1,0:T(8,128)(2,1)S(1)}, u32[]{:S(2)}, u32[]{:S(2)}) %collective-permute-start.22) | collective-permute-done | bytes 294944 | tf_op jit(solution)/shard_map/ppermute | solution.py:242
  686.5 13.7 %all-to-all-done.4.back_ref = bf16[8,72,1024]{2,1,0:T(8,128)(2,1)} async-done(((bf16[8,72,1024]{2,1,0:T(8,128)(2,1)}), bf16[8,72,1024]{2,1,0:T(8,128)(2,1)}, u32[]{:S(2)}, u32[]{:S(2)}) %all-to-all-start.4) | async-done | bytes 1179680 | tf_op jit(solution)/shard_map/all_to_all | solution.py:278
  706.2 38.3 %collective-permute-done.17 = bf16[128,2048]{1,0:T(8,128)(2,1)} collective-permute-done((bf16[128,2048]{1,0:T(8,128)(2,1)}, bf16[128,2048]{1,0:T(8,128)(2,1)}, u32[]{:S(2)}, u32[]{:S(2)}) %collective-permute-start.17) | collective-permute-done | bytes 524320 | tf_op jit(solution)/shard_map/ppermute | solution.py:455
  (286 shorter events, 199.0 us)
Async XLA Ops:
  21.3 97.2 %all-gather.5.cloned.1.call-start = ((), (), s32[]{:S(2)}) async-start(), calls=%async_computation.9 | async-start | bytes 4718592 | tf_op jit(solution)/shard_map/all_gather | solution.py:451
  49.6 141.2 %reduce-scatter.4.cloned.1.call-start = ((), (), s32[]{:S(2)}) async-start(), calls=%async_computation.10 | async-start | bytes 4718592 | tf_op jit(solution)/shard_map/reduce_scatter | solution.py:447
  139.9 198.2 %all-gather.9.cloned.1.call-start = ((), (), s32[]{:S(2)}) async-start(), calls=%async_computation.12 | async-start | bytes 4718592 | tf_op jit(solution)/shard_map/all_gather | solution.py:451
  142.1 223.7 %all-gather.7.cloned.1.call-start = ((), (), s32[]{:S(2)}) async-start(), calls=%async_computation.11 | async-start | bytes 4718592 | tf_op jit(solution)/shard_map/all_gather | solution.py:451
  266.5 44.7 %collective-permute-start.11 = (bf16[8,128,704]{1,2,0:T(8,128)(2,1)S(1)}, bf16[8,128,704]{1,2,0:T(8,128)(2,1)}, u32[]{:S(2)}, u32[]{:S(2)}) collective-permute-start(bf16[8,128,704]{1,2,0:T(8,128)(2,1)S(1)} %all_to_all.30), channel_id=1, source_target_pairs={{0,24},{8,16},{16,8},{24,0},{1,25},{9,17},{17,9},{25,1},{2,26},{10... | collective-permute-start | bytes 4325384 | tf_op jit(solution)/shard_map/ppermute | solution.py:242
  268.9 40.4 %all-to-all-start.3 = ((bf16[8,64,704]{2,1,0:T(8,128)(2,1)}), bf16[8,64,704]{2,1,0:T(8,128)(2,1)S(1)}, u32[]{:S(2)}, u32[]{:S(2)}) async-start(bf16[8,64,704]{2,1,0:T(8,128)(2,1)} %bitcast.161), calls=%async_computation.4 | async-start | bytes 1572864 | tf_op jit(solution)/shard_map/all_to_all | solution.py:246
  272.4 165.3 %reduce-scatter.6.cloned.1.call-start = ((), (), s32[]{:S(2)}) async-start(), calls=%async_computation.13 | async-start | bytes 4718592 | tf_op jit(solution)/shard_map/reduce_scatter | solution.py:447
  272.5 60.4 %collective-permute-start.10 = (bf16[8,128,704]{1,2,0:T(8,128)(2,1)S(1)}, bf16[8,128,704]{1,2,0:T(8,128)(2,1)}, u32[]{:S(2)}, u32[]{:S(2)}) collective-permute-start(bf16[8,128,704]{1,2,0:T(8,128)(2,1)S(1)} %all_to_all.30), channel_id=1, source_target_pairs={{0,16},{8,24},{16,0},{24,8},{1,17},{9,25},{17,1},{25,9},{2,18},{10... | collective-permute-start | bytes 4325384 | tf_op jit(solution)/shard_map/ppermute | solution.py:242
  273.1 62.4 %collective-permute-start.9 = (bf16[8,128,704]{1,2,0:T(8,128)(2,1)S(1)}, bf16[8,128,704]{1,2,0:T(8,128)(2,1)}, u32[]{:S(2)}, u32[]{:S(2)}) collective-permute-start(bf16[8,128,704]{1,2,0:T(8,128)(2,1)S(1)} %all_to_all.30), channel_id=1, source_target_pairs={{0,8},{8,0},{16,24},{24,16},{1,9},{9,1},{17,25},{25,17},{2,10},{10... | collective-permute-start | bytes 4325384 | tf_op jit(solution)/shard_map/ppermute | solution.py:242
  309.3 40.5 %collective-permute-start.14 = (bf16[8,64,704]{2,1,0:T(8,128)(2,1)S(1)}, bf16[8,64,704]{2,1,0:T(8,128)(2,1)}, u32[]{:S(2)}, u32[]{:S(2)}) collective-permute-start(bf16[8,64,704]{2,1,0:T(8,128)(2,1)S(1)} %all-to-all-done.3.refs_4_.refs_0_), channel_id=1, source_target_pairs={{0,24},{8,16},{16,8},{24,0},{1,25},{9,17},{17,9},{25,1},{2,26},{10... | collective-permute-start | bytes 2162696 | tf_op jit(solution)/shard_map/ppermute | solution.py:242
  309.5 56.2 %collective-permute-start.13 = (bf16[8,64,704]{2,1,0:T(8,128)(2,1)S(1)}, bf16[8,64,704]{2,1,0:T(8,128)(2,1)}, u32[]{:S(2)}, u32[]{:S(2)}) collective-permute-start(bf16[8,64,704]{2,1,0:T(8,128)(2,1)S(1)} %all-to-all-done.3.refs_4_.refs_0_), channel_id=1, source_target_pairs={{0,16},{8,24},{16,0},{24,8},{1,17},{9,25},{17,1},{25,9},{2,18},{10... | collective-permute-start | bytes 2162696 | tf_op jit(solution)/shard_map/ppermute | solution.py:242
  311.2 54.6 %collective-permute-start.12 = (bf16[8,64,704]{2,1,0:T(8,128)(2,1)S(1)}, bf16[8,64,704]{2,1,0:T(8,128)(2,1)}, u32[]{:S(2)}, u32[]{:S(2)}) collective-permute-start(bf16[8,64,704]{2,1,0:T(8,128)(2,1)S(1)} %all-to-all-done.3.refs_4_.refs_0_), channel_id=1, source_target_pairs={{0,8},{8,0},{16,24},{24,16},{1,9},{9,1},{17,25},{25,17},{2,10},{10... | collective-permute-start | bytes 2162696 | tf_op jit(solution)/shard_map/ppermute | solution.py:242
  389.4 181.3 %all-gather.11.cloned.1.call-start = ((), (), s32[]{:S(2)}) async-start(), calls=%async_computation.14 | async-start | bytes 4718592 | tf_op jit(solution)/shard_map/all_gather | solution.py:451
  449.2 54.3 %collective-permute-start.25 = (bf16[8,3,64,704]{3,2,1,0:T(8,128)(2,1)}, bf16[8,3,64,704]{3,2,1,0:T(8,128)(2,1)S(1)}, u32[]{:S(2)}, u32[]{:S(2)}) collective-permute-start(bf16[8,3,64,704]{3,2,1,0:T(8,128)(2,1)} %gw.5), channel_id=1, source_target_pairs={{0,8},{8,0},{16,24},{24,16},{1,9},{9,1},{17,25},{25,17},{2,10},{10... | collective-permute-start | bytes 6488072 | tf_op jit(solution)/shard_map/ppermute | solution.py:242
  457.4 102.1 %collective-permute-start.26 = (bf16[8,3,64,704]{3,2,1,0:T(8,128)(2,1)}, bf16[8,3,64,704]{3,2,1,0:T(8,128)(2,1)}, u32[]{:S(2)}, u32[]{:S(2)}) collective-permute-start(bf16[8,3,64,704]{3,2,1,0:T(8,128)(2,1)} %gw.6), channel_id=1, source_target_pairs={{0,16},{8,24},{16,0},{24,8},{1,17},{9,25},{17,1},{25,9},{2,18},{10... | collective-permute-start | bytes 6488072 | tf_op jit(solution)/shard_map/ppermute | solution.py:242
  465.7 93.8 %collective-permute-start.27 = (bf16[8,3,64,704]{3,2,1,0:T(8,128)(2,1)}, bf16[8,3,64,704]{3,2,1,0:T(8,128)(2,1)}, u32[]{:S(2)}, u32[]{:S(2)}) collective-permute-start(bf16[8,3,64,704]{3,2,1,0:T(8,128)(2,1)} %gw.7), channel_id=1, source_target_pairs={{0,24},{8,16},{16,8},{24,0},{1,25},{9,17},{17,9},{25,1},{2,26},{10... | collective-permute-start | bytes 6488072 | tf_op jit(solution)/shard_map/ppermute | solution.py:242
  564.9 100.5 %all-to-all-start.5 = ((bf16[8,192,704]{2,1,0:T(8,128)(2,1)}), bf16[8,192,704]{2,1,0:T(8,128)(2,1)S(1)}, u32[]{:S(2)}, u32[]{:S(2)}) async-start(bf16[8,192,704]{2,1,0:T(8,128)(2,1)} %bitcast.156), calls=%async_computation.8 | async-start | bytes 4718592 | tf_op jit(solution)/shard_map/all_to_all | solution.py:278
  568.9 135.9 %reduce-scatter.8.cloned.1.call-start = ((), (), s32[]{:S(2)}) async-start(), calls=%async_computation.15 | async-start | bytes 4718592 | tf_op jit(solution)/shard_map/reduce_scatter | solution.py:447
  619.8 43.9 %collective-permute-start.19 = (bf16[8,64,768]{2,1,0:T(8,128)(2,1)S(1)}, bf16[8,64,768]{2,1,0:T(8,128)(2,1)S(1)}, u32[]{:S(2)}, u32[]{:S(2)}) collective-permute-start(bf16[8,64,768]{2,1,0:T(8,128)(2,1)S(1)} %bitcast.198), channel_id=1, source_target_pairs={{0,8},{8,0},{16,24},{24,16},{1,9},{9,1},{17,25},{25,17},{2,10},{10... | collective-permute-start | bytes 2359304 | tf_op jit(solution)/shard_map/ppermute | solution.py:242
  621.2 42.5 %collective-permute-start.20 = (bf16[8,64,768]{2,1,0:T(8,128)(2,1)S(1)}, bf16[8,64,768]{2,1,0:T(8,128)(2,1)S(1)}, u32[]{:S(2)}, u32[]{:S(2)}) collective-permute-start(bf16[8,64,768]{2,1,0:T(8,128)(2,1)S(1)} %bitcast.197), channel_id=1, source_target_pairs={{0,16},{8,24},{16,0},{24,8},{1,17},{9,25},{17,1},{25,9},{2,18},{10... | collective-permute-start | bytes 2359304 | tf_op jit(solution)/shard_map/ppermute | solution.py:242
  623.2 40.6 %collective-permute-start.21 = (bf16[8,64,768]{2,1,0:T(8,128)(2,1)S(1)}, bf16[8,64,768]{2,1,0:T(8,128)(2,1)S(1)}, u32[]{:S(2)}, u32[]{:S(2)}) collective-permute-start(bf16[8,64,768]{2,1,0:T(8,128)(2,1)S(1)} %bitcast.196), channel_id=1, source_target_pairs={{0,24},{8,16},{16,8},{24,0},{1,25},{9,17},{17,9},{25,1},{2,26},{10... | collective-permute-start | bytes 2359304 | tf_op jit(solution)/shard_map/ppermute | solution.py:242
  623.8 46.3 %collective-permute-start.15 = (bf16[4,128,2048]{2,1,0:T(8,128)(2,1)}, bf16[4,128,2048]{2,1,0:T(8,128)(2,1)}, u32[]{:S(2)}, u32[]{:S(2)}) collective-permute-start(bf16[4,128,2048]{2,1,0:T(8,128)(2,1)} %dynamic-slice_bitcast_fusion), channel_id=1, source_target_pairs={{0,1},{1,0},{2,3},{3,2},{4,5},{5,4},{6,7},{7,6},{8,9},{9,8},{10,11... | collective-permute-start | bytes 6291464 | tf_op jit(solution)/shard_map/ppermute | solution.py:459
  685.4 59.2 %collective-permute-start.17 = (bf16[128,2048]{1,0:T(8,128)(2,1)}, bf16[128,2048]{1,0:T(8,128)(2,1)}, u32[]{:S(2)}, u32[]{:S(2)}) collective-permute-start(bf16[128,2048]{1,0:T(8,128)(2,1)} %get-tuple-element.74), channel_id=1, source_target_pairs={{0,4},{1,5},{2,6},{3,7},{4,0},{5,1},{6,2},{7,3},{8,12},{9,13},{10,... | collective-permute-start | bytes 1572872 | tf_op jit(solution)/shard_map/ppermute | solution.py:455
  685.4 59.2 %collective-permute-start.16 = (bf16[128,2048]{1,0:T(8,128)(2,1)}, bf16[128,2048]{1,0:T(8,128)(2,1)}, u32[]{:S(2)}, u32[]{:S(2)}) collective-permute-start(bf16[128,2048]{1,0:T(8,128)(2,1)} %get-tuple-element.75), channel_id=1, source_target_pairs={{0,2},{1,3},{2,4},{3,5},{4,6},{5,7},{6,0},{7,1},{8,10},{9,11},{10,... | collective-permute-start | bytes 1572872 | tf_op jit(solution)/shard_map/ppermute | solution.py:455
  (41 other events, 865.3 us)
Sparse Core Ops, SparseCore 0:
  44.5 50.3 all-gather.4
  140.0 50.7 reduce-scatter.3
  192.4 76.2 all-gather.8
  270.7 58.0 all-gather.6
  389.5 48.1 reduce-scatter.5
  442.6 45.3 all-gather.10
  596.6 63.5 reduce-scatter.7
